TPU v7x, 32 devices: a whole 2x2x4 slice. The times are simulated.
32 devices in a mesh: wide: 16 (over z, x, core), narrow: 2 (over y).
Axes of the slice: x: 2, y: 2, z: 4, core: 2. Of those that a mesh axis runs over, the one named last changes fastest.
Arguments:
- tokens: bfloat16 [65536, 384], P(('wide', 'narrow')), may hold values from -6 to 6
- counts: int32 [1024], P(('wide', 'narrow')), may hold values from 13 to 64, as said below
- cotangent: bfloat16 [65536, 384], P(('wide', 'narrow')), may hold values from -6 to 6
- master: float32 [1773312], P(('wide', 'narrow'))
- first: float32 [1773312], P(('wide', 'narrow')), as said below
- second: float32 [1773312], P(('wide', 'narrow')), as said below
- rate: float32 [1], replicated, may hold values from 0.5 to 1
- step: int32 [1], replicated, may hold values from 2 to 20
Outputs:
- layer_out: bfloat16 [65536, 384], P(('wide', 'narrow'))
- grad_input: bfloat16 [65536, 384], P(('wide', 'narrow'))
- master_new: float32 [1773312], P(('wide', 'narrow'))
- first_new: float32 [1773312], P(('wide', 'narrow'))
- second_new: float32 [1773312], P(('wide', 'narrow'))
- copy_new: bfloat16 [1773312], P(('wide', 'narrow'))
Inputs may be any that keep to these rules, and one draw needn't show every extreme that they name: The visible patches of a sample are its first counts[s] slots; the others are padding. `first`: first moments of both signs. `second`: second moments, all positive.
All inputs are finite; a program needn't handle non-finite values.
Results may differ from a plain program's by a relative error of at most 0.007.
The roundings to bfloat16 on the way count: a program that leaves them out, or rounds other values in their place, can miss the bound.
Values may be sent and summed in bfloat16 or wider, within the bound.
No kernel may reach another device: no remote copies, remote signals or barrier semaphores. Data moves between devices by JAX's collectives and lax.ppermute only.
A program may use at most 192 MiB of HBM per device.

v0:
```python
import functools
import itertools

import jax
import jax.numpy as jnp
from jax import lax
from jax.experimental import pallas as pl
from jax.experimental.pallas import tpu as pltpu
from jax.sharding import PartitionSpec as P

D = 384
FF = 1536
HEADS = 6
HEAD_DIM = 64
PATCHES = 64
LANES = 128
PAIRS = HEADS // 2
EPS = 1e-06
AXES = ("wide", "narrow")
QKV_ROWS = 3 * D * D // LANES
OUT_ROWS = D * D // LANES
UP_ROWS = D * FF // LANES
VEC_ROWS = (6 * D + FF) // LANES
FLAT_ROWS = QKV_ROWS + OUT_ROWS + 2 * UP_ROWS + VEC_ROWS
BASE_OUT = QKV_ROWS
BASE_UP = BASE_OUT + OUT_ROWS
BASE_DOWN = BASE_UP + UP_ROWS
BASE_VEC = BASE_DOWN + UP_ROWS
VECTORS = ("gain_one", "shift_one", "bias_out", "gain_two", "shift_two", "bias_up", "bias_down")
VMEM_LIMIT = 60 * 1024 * 1024
BLOCK = 512
GROUP = 8
COLUMNS = 512
FLOWS = 1


def round_up(value, step):
    return (value + step - 1) // step * step


def dot(left, right, left_dim, right_dim):
    return lax.dot_general(
        left, right, (((left_dim,), (right_dim,)), ((), ())), preferred_element_type=jnp.float32
    )


def chunk_rows(shard):
    return round_up(shard + 1024, 16 * FLOWS * LANES) // LANES


class Flow:
    def __init__(self, rounds, devices, core):
        self.swaps = [
            [(device, device ^ pair[1 if device & core else 0]) for device in range(devices)]
            for pair in rounds
        ]
        self.core_swap = [(device, device ^ core) for device in range(devices)]
        self.core = core
        half = devices // 2
        self.across = [[0] * devices, [0] * devices]
        for side in (0, 1):
            for slot in range(half):
                for index, pair in enumerate(rounds):
                    if slot >> index & 1:
                        self.across[side][slot] ^= pair[side]
                        self.across[1 - side][half + slot] ^= pair[side]
                self.across[1 - side][half + slot] ^= core

    def owner(self, me, slot):
        side_one = (me & self.core) != 0
        return me ^ jnp.where(side_one, self.across[1][slot], self.across[0][slot])


def exchange_flows(wide, narrow):
    devices = wide * narrow
    core = narrow
    bits = [1 << k for k in reversed(range(devices.bit_length() - 1)) if 1 << k != core]
    half = (len(bits) + 1) // 2
    flows = []
    for order in range(FLOWS):
        rounds = []
        for first, second in itertools.zip_longest(bits[:half], bits[half:]):
            if second is None:
                rounds.append((first, first))
            else:
                rounds += [(first, second), (second, first)]
        flows.append(Flow(rounds, devices, core))
    return flows


def gather_chunks(own, flow):
    held = own[None]
    for swap in flow.swaps[:-1]:
        held = jnp.concatenate([held, lax.ppermute(held, AXES, swap)], axis=0)
    held_core = lax.ppermute(held, AXES, flow.core_swap)
    taken = lax.ppermute(held, AXES, flow.swaps[-1])
    taken_core = lax.ppermute(taken, AXES, flow.core_swap)
    return held, taken, held_core, taken_core


def scatter_chunks(kept, sent, flow):
    parts = [kept, lax.ppermute(sent, AXES, flow.core_swap)]
    for swap in reversed(flow.swaps):
        half = parts[0].shape[0] // 2
        upper = sum(part[half:].astype(jnp.float32) for part in parts)
        parts = [part[:half] for part in parts]
        parts.append(lax.ppermute(upper.astype(jnp.bfloat16), AXES, swap))
    return sum(part[0].astype(jnp.float32) for part in parts)


def vector_width(name):
    return FF if name == "bias_up" else D


def vector_rows():
    row = BASE_VEC
    for index, name in enumerate(VECTORS):
        for block in range(vector_width(name) // LANES):
            yield index, slice(block * LANES, (block + 1) * LANES), row
            row += 1


def matrix_blocks(matrix, base):
    height, width = matrix.shape
    blocks = width // LANES
    for block in range(blocks):
        columns = slice(block * LANES, (block + 1) * LANES)
        yield columns, pl.ds(base + block, height, stride=blocks)


def first_row(owner, shard):
    return owner * shard // 1024 * 8


def dynamic_first_row(owner, shard):
    return pl.multiple_of(lax.shift_right_logical(owner * shard, 10) * 8, 8)


def unpack(me, pieces, flows, shard, flat, w_qkv, w_out, w_up, w_down, vectors):
    rows = pieces[0].shape[1]
    devices = 4 * pieces[0].shape[0]
    sure = shard // 1024 * 8
    for owner in range(devices):
        start = first_row(owner, shard)
        flat[start : start + 8, :] = jnp.zeros((8, LANES), jnp.float32)
        flat[start + sure : start + FLOWS * rows, :] = jnp.zeros(
            (FLOWS * rows - sure, LANES), jnp.float32
        )
    for index, flow in enumerate(flows):
        low, high = index * rows, (index + 1) * rows
        cuts = sorted({low, high} | {cut for cut in (8, sure) if low < cut < high})
        for slot in range(devices):
            source = pieces[4 * index + slot * 4 // devices]
            start = dynamic_first_row(flow.owner(me, slot), shard)
            for begin, end in zip(cuts, cuts[1:]):
                piece = source[slot % source.shape[0], begin - low : end - low, :]
                piece = piece.astype(jnp.float32)
                target = (pl.ds(pl.multiple_of(start + begin, 8), end - begin), slice(None))
                if begin < 8 or begin >= sure:
                    flat[target] += piece
                else:
                    flat[target] = piece
    for matrix, base in ((w_qkv, 0), (w_out, BASE_OUT), (w_up, BASE_UP), (w_down, BASE_DOWN)):
        for columns, rows_of in matrix_blocks(matrix, base):
            matrix[:, columns] = flat[rows_of, :].astype(jnp.bfloat16)
    for index, columns, row in vector_rows():
        vectors[index : index + 1, columns] = flat[row : row + 1, :]


def pack(me, flows, shard, flat, grad_qkv, grad_out, grad_up, grad_down, vectors, outputs):
    for matrix, base in (
        (grad_qkv, 0),
        (grad_out, BASE_OUT),
        (grad_up, BASE_UP),
        (grad_down, BASE_DOWN),
    ):
        for columns, rows_of in matrix_blocks(matrix, base):
            flat[rows_of, :] = matrix[:, columns]
    for index, columns, row in vector_rows():
        flat[row : row + 1, :] = vectors[index : index + 1, columns]
    flat[FLAT_ROWS:, :] = jnp.zeros((flat.shape[0] - FLAT_ROWS, LANES), jnp.float32)
    for index, flow in enumerate(flows):
        kept, sent = outputs[2 * index : 2 * index + 2]
        half, rows, _ = kept.shape
        for slot in range(half):
            start = dynamic_first_row(flow.owner(me, slot), shard) + index * rows
            kept[slot] = flat[pl.ds(pl.multiple_of(start, 8), rows), :]
            start = dynamic_first_row(flow.owner(me, half + slot), shard) + index * rows
            sent[slot] = flat[pl.ds(pl.multiple_of(start, 8), rows), :].astype(jnp.bfloat16)


def vector(vectors, name):
    index = VECTORS.index(name)
    return vectors[index : index + 1, : vector_width(name)]


def normalize(values):
    center = values - jnp.mean(values, axis=-1, keepdims=True)
    spread = jnp.mean(center * center, axis=-1, keepdims=True)
    scale = lax.rsqrt(spread + EPS)
    return center * scale, scale


def norm_back(grad, gain, hat, scale):
    inner = grad * gain
    mean_inner = jnp.mean(inner, axis=-1, keepdims=True)
    mean_cross = jnp.mean(inner * hat, axis=-1, keepdims=True)
    return scale * (inner - mean_inner - hat * mean_cross)


def first_halves():
    return lax.broadcasted_iota(jnp.int32, (PATCHES, LANES), 1) < HEAD_DIM


def block_diagonal(values, first_half):
    zero = jnp.zeros_like(values)
    return jnp.concatenate(
        [jnp.where(first_half, values, zero), jnp.where(first_half, zero, values)], axis=0
    )


def own_halves(values, first_half):
    return jnp.where(first_half, values[:PATCHES], values[PATCHES:])


def head_chains(samples):
    for sample in range(0, samples, GROUP):
        yield [
            (slice(each * PATCHES, (each + 1) * PATCHES), pair * LANES, each)
            for each in range(sample, min(sample + GROUP, samples))
            for pair in range(PAIRS)
        ]


def attention(count, packed, chance, mixed):
    first_half = first_halves()
    slots = lax.broadcasted_iota(jnp.int32, (PATCHES, LANES), 0)
    for chains in head_chains(packed.shape[0] // PATCHES):
        scores = [
            dot(
                packed[rows, D + at : D + at + LANES],
                block_diagonal(packed[rows, at : at + LANES], first_half),
                1,
                1,
            )
            for rows, at, _ in chains
        ]
        scores = [
            jnp.where(slots < count(each), score * HEAD_DIM**-0.5, -1e30)
            for score, (_, _, each) in zip(scores, chains)
        ]
        exponents = [jnp.exp(score - jnp.max(score, axis=0, keepdims=True)) for score in scores]
        attends = [
            exponent * (1.0 / jnp.sum(exponent, axis=0, keepdims=True)) for exponent in exponents
        ]
        for attend, (rows, at, _) in zip(attends, chains):
            chance[rows, at : at + LANES] = attend
        mixes = [
            dot(attend.astype(jnp.bfloat16), packed[rows, 2 * D + at : 2 * D + at + LANES], 0, 0)
            for attend, (rows, at, _) in zip(attends, chains)
        ]
        for mix, (rows, at, _) in zip(mixes, chains):
            mixed[rows, at : at + LANES] = own_halves(mix, first_half).astype(jnp.bfloat16)


def attention_back(packed, chance, grad_mixed, grad_packed):
    first_half = first_halves()
    factor = HEAD_DIM**-0.5
    for chains in head_chains(packed.shape[0] // PATCHES):
        sides = [
            block_diagonal(grad_mixed[rows, at : at + LANES], first_half) for rows, at, _ in chains
        ]
        grad_attends = [
            dot(packed[rows, 2 * D + at : 2 * D + at + LANES], side, 1, 1)
            for side, (rows, at, _) in zip(sides, chains)
        ]
        attends = [chance[rows, at : at + LANES] for rows, at, _ in chains]
        grad_values = [
            dot(attend.astype(jnp.bfloat16), side, 1, 0) for attend, side in zip(attends, sides)
        ]
        for grad, (rows, at, _) in zip(grad_values, chains):
            grad_packed[rows, 2 * D + at : 2 * D + at + LANES] = grad.astype(jnp.bfloat16)
        inners = [
            jnp.sum(attend * grad, axis=0, keepdims=True)
            for attend, grad in zip(attends, grad_attends)
        ]
        grad_scores = [
            (attend * (grad - inner)).astype(jnp.bfloat16)
            for attend, grad, inner in zip(attends, grad_attends, inners)
        ]
        grad_keys = [
            dot(grad, block_diagonal(packed[rows, at : at + LANES], first_half), 1, 0) * factor
            for grad, (rows, at, _) in zip(grad_scores, chains)
        ]
        for grad, (rows, at, _) in zip(grad_keys, chains):
            grad_packed[rows, D + at : D + at + LANES] = grad.astype(jnp.bfloat16)
        grad_queries = [
            dot(grad, packed[rows, D + at : D + at + LANES], 0, 0)
            for grad, (rows, at, _) in zip(grad_scores, chains)
        ]
        for grad, (rows, at, _) in zip(grad_queries, chains):
            grad_packed[rows, at : at + LANES] = (own_halves(grad, first_half) * factor).astype(
                jnp.bfloat16
            )


def layer_kernel(flows, shard, *refs):
    me, counts = refs[:2]
    pieces = refs[2 : 2 + 4 * FLOWS]
    tokens, cotangent, result, grad_input = refs[2 + 4 * FLOWS : 6 + 4 * FLOWS]
    outputs = refs[6 + 4 * FLOWS : 6 + 6 * FLOWS]
    (
        flat,
        w_qkv,
        w_out,
        w_up,
        w_down,
        vectors,
        acc_qkv,
        acc_out,
        acc_up,
        acc_down,
        acc_vectors,
        packed,
        chance,
        mixed,
        grad_mixed,
        grad_packed,
    ) = refs[6 + 6 * FLOWS :]
    step = pl.program_id(0)
    samples = tokens.shape[0] // PATCHES

    @pl.when(step == 0)
    def _():
        unpack(me[0], pieces, flows, shard, flat, w_qkv, w_out, w_up, w_down, vectors)
        for ref in (acc_qkv, acc_out, acc_up, acc_down, acc_vectors):
            ref[...] = jnp.zeros_like(ref)

    def count(sample):
        return counts[step * samples + sample]

    def add_vector(name, values, at=0):
        index = VECTORS.index(name)
        acc_vectors[index : index + 1, at : at + values.shape[1]] += jnp.sum(
            values, axis=0, keepdims=True
        )

    inputs = tokens[...].astype(jnp.float32)
    hat_one, scale_one = normalize(inputs)
    gain_one = vector(vectors, "gain_one")
    normed_one = (hat_one * gain_one + vector(vectors, "shift_one")).astype(jnp.bfloat16)
    packed[...] = dot(normed_one, w_qkv[...], 1, 0).astype(jnp.bfloat16)
    attention(count, packed, chance, mixed)
    hidden = inputs + dot(mixed[...], w_out[...], 1, 0) + vector(vectors, "bias_out")

    hat_two, scale_two = normalize(hidden)
    gain_two = vector(vectors, "gain_two")
    normed_two = (hat_two * gain_two + vector(vectors, "shift_two")).astype(jnp.bfloat16)
    slots = lax.broadcasted_iota(jnp.int32, (PATCHES, 1), 0)
    visible = jnp.concatenate(
        [jnp.where(slots < count(sample), 1.0, 0.0) for sample in range(samples)], axis=0
    )
    grad_out = cotangent[...].astype(jnp.float32) * visible
    grad_out_low = grad_out.astype(jnp.bfloat16)
    add_vector("bias_down", grad_out)
    total = hidden + vector(vectors, "bias_down")
    grad_normed_two = jnp.zeros_like(hidden)
    bias_up = vector(vectors, "bias_up")
    for at in range(0, FF, COLUMNS):
        columns = slice(at, at + COLUMNS)
        upward = dot(normed_two, w_up[:, columns], 1, 0) + bias_up[:, columns]
        below = 0.5 * (1.0 + lax.erf(upward * 0.5**0.5))
        active = (upward * below).astype(jnp.bfloat16)
        slope = below + upward * (jnp.exp(-0.5 * upward * upward) * (0.5 / jnp.pi) ** 0.5)
        total = total + dot(active, w_down[columns, :], 1, 0)
        grad_upward = dot(grad_out_low, w_down[columns, :], 1, 1) * slope
        grad_upward = grad_upward.astype(jnp.bfloat16)
        add_vector("bias_up", grad_upward.astype(jnp.float32), at)
        acc_down[columns, :] += dot(active, grad_out_low, 0, 0)
        acc_up[:, columns] += dot(normed_two, grad_upward, 0, 0)
        grad_normed_two = grad_normed_two + dot(grad_upward, w_up[:, columns], 1, 1)
    result[...] = total.astype(jnp.bfloat16)
    add_vector("gain_two", grad_normed_two * hat_two)
    add_vector("shift_two", grad_normed_two)
    grad_hidden = grad_out + norm_back(grad_normed_two, gain_two, hat_two, scale_two)

    grad_hidden_low = grad_hidden.astype(jnp.bfloat16)
    add_vector("bias_out", grad_hidden_low.astype(jnp.float32))
    acc_out[...] += dot(mixed[...], grad_hidden_low, 0, 0)
    grad_mixed[...] = dot(grad_hidden_low, w_out[...], 1, 1).astype(jnp.bfloat16)
    attention_back(packed, chance, grad_mixed, grad_packed)
    acc_qkv[...] += dot(normed_one, grad_packed[...], 0, 0)
    grad_normed_one = dot(grad_packed[...], w_qkv[...], 1, 1)
    add_vector("gain_one", grad_normed_one * hat_one)
    add_vector("shift_one", grad_normed_one)
    grad_input[...] = (
        grad_hidden + norm_back(grad_normed_one, gain_one, hat_one, scale_one)
    ).astype(jnp.bfloat16)

    @pl.when(step == pl.num_programs(0) - 1)
    def _():
        pack(
            me[0], flows, shard, flat, acc_qkv, acc_out, acc_up, acc_down, acc_vectors, outputs
        )


def layer(me, counts, pieces, tokens, cotangent, flows, shard):
    rows = tokens.shape[0]
    block = min(BLOCK, rows)
    quarter, piece_rows, _ = pieces[0].shape
    devices = 4 * quarter
    flat_rows = first_row(devices - 1, shard) + FLOWS * piece_rows
    low = jnp.bfloat16
    full = jnp.float32

    def by_rows():
        return pl.BlockSpec((block, D), lambda i, me, counts: (i, 0))

    def whole(shape):
        return pl.BlockSpec(
            shape, lambda i, me, counts: (0,) * len(shape), pipeline_mode=pl.Buffered(1)
        )

    chunk_shape = (devices // 2, piece_rows, LANES)
    return pl.pallas_call(
        functools.partial(layer_kernel, flows, shard),
        name="layer",
        grid_spec=pltpu.PrefetchScalarGridSpec(
            num_scalar_prefetch=2,
            grid=(rows // block,),
            in_specs=[whole(piece.shape) for piece in pieces] + [by_rows(), by_rows()],
            out_specs=[by_rows(), by_rows()] + [whole(chunk_shape)] * (2 * FLOWS),
            scratch_shapes=[
                pltpu.VMEM((flat_rows, LANES), full),
                pltpu.VMEM((D, 3 * D), low),
                pltpu.VMEM((D, D), low),
                pltpu.VMEM((D, FF), low),
                pltpu.VMEM((FF, D), low),
                pltpu.VMEM((8, FF), full),
                pltpu.VMEM((D, 3 * D), full),
                pltpu.VMEM((D, D), full),
                pltpu.VMEM((D, FF), full),
                pltpu.VMEM((FF, D), full),
                pltpu.VMEM((8, FF), full),
                pltpu.VMEM((block, 3 * D), low),
                pltpu.VMEM((block, D), full),
                pltpu.VMEM((block, D), low),
                pltpu.VMEM((block, D), low),
                pltpu.VMEM((block, 3 * D), low),
            ],
        ),
        out_shape=[jax.ShapeDtypeStruct((rows, D), low)] * 2
        + [jax.ShapeDtypeStruct(chunk_shape, dtype) for dtype in (full, low)] * FLOWS,
        compiler_params=pltpu.CompilerParams(vmem_limit_bytes=VMEM_LIMIT),
    )(me, counts, *pieces, tokens, cotangent)


def step_scale(position):
    bound_one = QKV_ROWS * LANES
    bound_two = BASE_UP * LANES
    bound_three = BASE_DOWN * LANES
    bound_four = BASE_VEC * LANES
    scale = jnp.where(
        position < bound_one,
        D ** (-0.5),
        jnp.where(
            position < bound_two,
            (D // 8) ** (-0.5),
            jnp.where(
                position < bound_three,
                D ** (-0.5),
                jnp.where(position < bound_four, FF ** (-0.5), 0.1),
            ),
        ),
    )
    decay = jnp.where(position < bound_four, 0.05, 0.0)
    return (scale, decay)


def on_device(tokens, counts, cotangent, master, first, second, rate, step):
    shard = master.shape[0]
    me = lax.axis_index(AXES)
    flows = exchange_flows(lax.axis_size("wide"), lax.axis_size("narrow"))
    rows = chunk_rows(shard)
    offset = me * shard % 1024
    own = lax.dynamic_update_slice(
        jnp.zeros((rows * LANES,), jnp.bfloat16), master.astype(jnp.bfloat16), (offset,)
    ).reshape(FLOWS, rows // FLOWS, LANES)
    pieces = []
    for index, flow in enumerate(flows):
        pieces += gather_chunks(own[index], flow)
    result, grad_input, *chunks = layer(
        me.reshape(1), counts, pieces, tokens, cotangent, flows, shard
    )
    reduced = jnp.concatenate(
        [
            scatter_chunks(chunks[2 * index], chunks[2 * index + 1], flow)
            for index, flow in enumerate(flows)
        ],
        axis=0,
    )
    reduced = lax.dynamic_slice(reduced.reshape(rows * LANES), (offset,), (shard,))
    position = me * shard + jnp.arange(shard, dtype=jnp.int32)
    first_new = 0.5 * first + 0.5 * reduced
    second_new = 0.5 * second + 0.5 * reduced * reduced
    correct = 1.0 - jnp.power(jnp.float32(0.5), step[0].astype(jnp.float32))
    scale, decay = step_scale(position)
    moved = first_new / correct / (jnp.sqrt(second_new / correct) + 1e-08)
    master_new = master - rate[0] * scale * (moved + decay * master)
    return (
        result,
        grad_input,
        master_new,
        first_new,
        second_new,
        master_new.astype(jnp.bfloat16),
    )


def solution(mesh):
    split = P(AXES)
    by_rows = P(AXES, None)
    return jax.shard_map(
        on_device,
        mesh=mesh,
        in_specs=(by_rows, split, by_rows, split, split, split, P(), P()),
        out_specs=(by_rows, by_rows, split, split, split, split),
        check_vma=False,
    )
```

profile of v0, /device:TPU:0, one launch (start us, length us, event | category | flops | bytes accessed | tf_op | source)
XLA Modules:
  0.0 137.5 jit_solution(18261582048733991906)
XLA Ops:
  0.6 1.0 convert_element_type.81
  1.6 1.1 dynamic_update_slice.3
  2.8 4.1 %collective-permute-start = (bf16[1,448,128]{2,1,0:T(8,128)(2,1)S(1)}, bf16[1,448,128]{2,1,0:T(8,128)(2,1)S(1)}, u32[]{:S(2)}, u32[]{:S(2)}) collective-permute-start(bf16[1,448,128]{2,1,0:T(8,128)(2,1)S(1)} %bitcast.7), channel_id=1, source_target_pairs={{0,16},{1,17},{2,6},{3,7},{4,20},{5,21},{6,2},{7,3},{8,24},{9,25},... | collective-permute-start | bytes 344072 | tf_op jit(solution)/shard_map/ppermute | solution.py:94
  6.9 2.8 %collective-permute-done = bf16[1,448,128]{2,1,0:T(8,128)(2,1)S(1)} collective-permute-done((bf16[1,448,128]{2,1,0:T(8,128)(2,1)S(1)}, bf16[1,448,128]{2,1,0:T(8,128)(2,1)S(1)}, u32[]{:S(2)}, u32[]{:S(2)}) %collective-permute-start) | collective-permute-done | bytes 114720 | tf_op jit(solution)/shard_map/ppermute | solution.py:94
  9.7 3.1 %collective-permute-start.1 = (bf16[2,448,128]{2,1,0:T(8,128)(2,1)S(1)}, bf16[2,448,128]{2,1,0:T(8,128)(2,1)S(1)}, u32[]{:S(2)}, u32[]{:S(2)}) collective-permute-start(bf16[2,448,128]{2,1,0:T(8,128)(2,1)S(1)} %pad_maximum_fusion.2), channel_id=1, source_target_pairs={{0,4},{1,5},{2,18},{3,19},{4,0},{5,1},{6,22},{7,23},{8,12},{9,13},... | collective-permute-start | bytes 688136 | tf_op jit(solution)/shard_map/ppermute | solution.py:94
  12.8 4.0 %collective-permute-done.1 = bf16[2,448,128]{2,1,0:T(8,128)(2,1)S(1)} collective-permute-done((bf16[2,448,128]{2,1,0:T(8,128)(2,1)S(1)}, bf16[2,448,128]{2,1,0:T(8,128)(2,1)S(1)}, u32[]{:S(2)}, u32[]{:S(2)}) %collective-permute-start.1) | collective-permute-done | bytes 229408 | tf_op jit(solution)/shard_map/ppermute | solution.py:94
  16.9 1.3 collective-permute-start.2
  18.1 7.3 %collective-permute-done.2 = bf16[4,448,128]{2,1,0:T(8,128)(2,1)S(1)} collective-permute-done((bf16[4,448,128]{2,1,0:T(8,128)(2,1)S(1)}, bf16[4,448,128]{2,1,0:T(8,128)(2,1)S(1)}, u32[]{:S(2)}, u32[]{:S(2)}) %collective-permute-start.2) | collective-permute-done | bytes 458784 | tf_op jit(solution)/shard_map/ppermute | solution.py:94
  25.4 0.1 pad_maximum_fusion.refs_2_
  25.5 0.0 copy-start.1
  25.5 2.1 %collective-permute-start.3 = (bf16[8,448,128]{2,1,0:T(8,128)(2,1)S(1)}, bf16[8,448,128]{2,1,0:T(8,128)(2,1)S(1)}, u32[]{:S(2)}, u32[]{:S(2)}) collective-permute-start(bf16[8,448,128]{2,1,0:T(8,128)(2,1)S(1)} %pad_maximum_fusion.refs_2_), channel_id=1, source_target_pairs={{0,1},{1,0},{2,10},{3,11},{4,5},{5,4},{6,14},{7,15},{8,9},{9,8},{1... | collective-permute-start | bytes 2752520 | tf_op jit(solution)/shard_map/ppermute | solution.py:96
  27.6 0.0 collective-permute-start.4
  27.6 11.4 %collective-permute-done.3.refs_3_ = bf16[8,448,128]{2,1,0:T(8,128)(2,1)S(1)} collective-permute-done((bf16[8,448,128]{2,1,0:T(8,128)(2,1)S(1)}, bf16[8,448,128]{2,1,0:T(8,128)(2,1)S(1)}, u32[]{:S(2)}, u32[]{:S(2)}) %collective-permute-start.3) | collective-permute-done | bytes 917536 | tf_op jit(solution)/shard_map/ppermute | solution.py:96
  39.0 0.0 copy-start.2
  39.0 0.0 collective-permute-start.5
  39.0 0.0 collective-permute-done.4.refs_4_
  39.0 0.0 copy-start.3
  39.0 2.5 %collective-permute-done.5.refs_5_ = bf16[8,448,128]{2,1,0:T(8,128)(2,1)S(1)} collective-permute-done((bf16[8,448,128]{2,1,0:T(8,128)(2,1)S(1)}, bf16[8,448,128]{2,1,0:T(8,128)(2,1)S(1)}, u32[]{:S(2)}, u32[]{:S(2)}) %collective-permute-start.5) | collective-permute-done | bytes 917536 | tf_op jit(solution)/shard_map/ppermute | solution.py:97
  41.5 0.0 copy-start.4
  41.5 0.0 copy-done.1
  41.5 0.0 copy-done.2
  41.5 0.0 copy-done.3
  41.5 1.0 copy-done.4
  42.5 52.3 %layer.1 = (bf16[2048,384]{1,0:T(8,128)(2,1)}, bf16[2048,384]{1,0:T(8,128)(2,1)}, f32[16,448,128]{2,1,0:T(8,128)}, bf16[16,448,128]{2,1,0:T(8,128)(2,1)}) custom-call(s32[1]{0:T(128)} %bitcast.refs_0_, s32[32]{0:T(128)} %refs_1_.1, bf16[8,448,128]{2,1,0:T(8,128)(2,1)} %copy-done.1, bf16[8,448,128]{2,1,0:T(8,128)(2,1)} %copy-done.2, ...), custom_call_target="tpu_custom_call" | custom-call | tf_op jit(solution)/shard_map/layer/pallas_call | solution.py:425
  94.8 0.2 collective-permute-start.6
  95.0 3.9 %collective-permute-done.6 = bf16[16,448,128]{2,1,0:T(8,128)(2,1)S(1)} collective-permute-done((bf16[16,448,128]{2,1,0:T(8,128)(2,1)}, bf16[16,448,128]{2,1,0:T(8,128)(2,1)S(1)}, u32[]{:S(2)}, u32[]{:S(2)}) %collective-permute-start.6) | collective-permute-done | bytes 1835040 | tf_op jit(solution)/shard_map/ppermute | solution.py:102
  98.9 0.0 copy-start
  98.9 1.9 %add_convert_fusion = bf16[8,448,128]{2,1,0:T(8,128)(2,1)S(1)} fusion(f32[16,448,128]{2,1,0:T(8,128)} %get-tuple-element.12, bf16[16,448,128]{2,1,0:T(8,128)(2,1)S(1)} %collective-permute-done.6), kind=kLoop, calls=%fused_computation | loop fusion | flops 1376256 | bytes 3670016 | tf_op jit(solution)/shard_map/convert_element_type | solution.py:107
  100.8 2.1 %collective-permute-start.7 = (bf16[8,448,128]{2,1,0:T(8,128)(2,1)S(1)}, bf16[8,448,128]{2,1,0:T(8,128)(2,1)S(1)}, u32[]{:S(2)}, u32[]{:S(2)}) collective-permute-start(bf16[8,448,128]{2,1,0:T(8,128)(2,1)S(1)} %add_convert_fusion), channel_id=1, source_target_pairs={{0,1},{1,0},{2,10},{3,11},{4,5},{5,4},{6,14},{7,15},{8,9},{9,8},{1... | collective-permute-start | bytes 2752520 | tf_op jit(solution)/shard_map/ppermute | solution.py:107
  102.8 11.4 %collective-permute-done.7 = bf16[8,448,128]{2,1,0:T(8,128)(2,1)S(1)} collective-permute-done((bf16[8,448,128]{2,1,0:T(8,128)(2,1)S(1)}, bf16[8,448,128]{2,1,0:T(8,128)(2,1)S(1)}, u32[]{:S(2)}, u32[]{:S(2)}) %collective-permute-start.7) | collective-permute-done | bytes 917536 | tf_op jit(solution)/shard_map/ppermute | solution.py:107
  114.2 0.0 copy-done
  114.2 0.2 add_convert_fusion.1
  114.4 0.0 copy-start.5
  114.4 0.0 copy-start.6
  114.4 0.0 copy-start.7
  114.4 1.2 collective-permute-start.8
  115.7 7.3 %collective-permute-done.8 = bf16[4,448,128]{2,1,0:T(8,128)(2,1)S(1)} collective-permute-done((bf16[4,448,128]{2,1,0:T(8,128)(2,1)S(1)}, bf16[4,448,128]{2,1,0:T(8,128)(2,1)S(1)}, u32[]{:S(2)}, u32[]{:S(2)}) %collective-permute-start.8) | collective-permute-done | bytes 458784 | tf_op jit(solution)/shard_map/ppermute | solution.py:107
  123.0 0.1 add_convert_fusion.2
  123.1 2.0 %collective-permute-start.9 = (bf16[2,448,128]{2,1,0:T(8,128)(2,1)S(1)}, bf16[2,448,128]{2,1,0:T(8,128)(2,1)S(1)}, u32[]{:S(2)}, u32[]{:S(2)}) collective-permute-start(bf16[2,448,128]{2,1,0:T(8,128)(2,1)S(1)} %add_convert_fusion.2), channel_id=1, source_target_pairs={{0,4},{1,5},{2,18},{3,19},{4,0},{5,1},{6,22},{7,23},{8,12},{9,13},... | collective-permute-start | bytes 688136 | tf_op jit(solution)/shard_map/ppermute | solution.py:107
  125.1 4.0 %collective-permute-done.9 = bf16[2,448,128]{2,1,0:T(8,128)(2,1)S(1)} collective-permute-done((bf16[2,448,128]{2,1,0:T(8,128)(2,1)S(1)}, bf16[2,448,128]{2,1,0:T(8,128)(2,1)S(1)}, u32[]{:S(2)}, u32[]{:S(2)}) %collective-permute-start.9) | collective-permute-done | bytes 229408 | tf_op jit(solution)/shard_map/ppermute | solution.py:107
  129.2 0.1 add_convert_fusion.3
  129.3 2.6 %collective-permute-start.10 = (bf16[1,448,128]{2,1,0:T(8,128)(2,1)S(1)}, bf16[1,448,128]{2,1,0:T(8,128)(2,1)S(1)}, u32[]{:S(2)}, u32[]{:S(2)}) collective-permute-start(bf16[1,448,128]{2,1,0:T(8,128)(2,1)S(1)} %add_convert_fusion.3), channel_id=1, source_target_pairs={{0,16},{1,17},{2,6},{3,7},{4,20},{5,21},{6,2},{7,3},{8,24},{9,25},... | collective-permute-start | bytes 344072 | tf_op jit(solution)/shard_map/ppermute | solution.py:107
  133.2 3.0 %collective-permute-done.10 = bf16[1,448,128]{2,1,0:T(8,128)(2,1)S(1)} collective-permute-done((bf16[1,448,128]{2,1,0:T(8,128)(2,1)S(1)}, bf16[1,448,128]{2,1,0:T(8,128)(2,1)S(1)}, u32[]{:S(2)}, u32[]{:S(2)}) %collective-permute-start.10) | collective-permute-done | bytes 114720 | tf_op jit(solution)/shard_map/ppermute | solution.py:107
  136.2 0.1 add_bitcast_fusion
  136.3 0.0 copy-done.5
  136.3 0.0 copy-done.6
  136.3 0.0 copy-done.7
  136.4 1.2 fusion.5
  (3 shorter events, 0.1 us)
Async XLA Ops:
  2.8 6.9 %collective-permute-start = (bf16[1,448,128]{2,1,0:T(8,128)(2,1)S(1)}, bf16[1,448,128]{2,1,0:T(8,128)(2,1)S(1)}, u32[]{:S(2)}, u32[]{:S(2)}) collective-permute-start(bf16[1,448,128]{2,1,0:T(8,128)(2,1)S(1)} %bitcast.7), channel_id=1, source_target_pairs={{0,16},{1,17},{2,6},{3,7},{4,20},{5,21},{6,2},{7,3},{8,24},{9,25},... | collective-permute-start | bytes 344072 | tf_op jit(solution)/shard_map/ppermute | solution.py:94
  9.7 7.1 %collective-permute-start.1 = (bf16[2,448,128]{2,1,0:T(8,128)(2,1)S(1)}, bf16[2,448,128]{2,1,0:T(8,128)(2,1)S(1)}, u32[]{:S(2)}, u32[]{:S(2)}) collective-permute-start(bf16[2,448,128]{2,1,0:T(8,128)(2,1)S(1)} %pad_maximum_fusion.2), channel_id=1, source_target_pairs={{0,4},{1,5},{2,18},{3,19},{4,0},{5,1},{6,22},{7,23},{8,12},{9,13},... | collective-permute-start | bytes 688136 | tf_op jit(solution)/shard_map/ppermute | solution.py:94
  16.9 8.5 %collective-permute-start.2 = (bf16[4,448,128]{2,1,0:T(8,128)(2,1)S(1)}, bf16[4,448,128]{2,1,0:T(8,128)(2,1)S(1)}, u32[]{:S(2)}, u32[]{:S(2)}) collective-permute-start(bf16[4,448,128]{2,1,0:T(8,128)(2,1)S(1)} %pad_maximum_fusion.1), channel_id=1, source_target_pairs={{0,8},{1,9},{2,3},{3,2},{4,12},{5,13},{6,7},{7,6},{8,0},{9,1},{10,... | collective-permute-start | bytes 1376264 | tf_op jit(solution)/shard_map/ppermute | solution.py:94
  25.5 16.0 %copy-start.1 = (bf16[8,448,128]{2,1,0:T(8,128)(2,1)}, bf16[8,448,128]{2,1,0:T(8,128)(2,1)S(1)}, u32[]{:S(2)}) copy-start(bf16[8,448,128]{2,1,0:T(8,128)(2,1)S(1)} %pad_maximum_fusion.refs_2_) | copy-start | bytes 2752516
  25.5 13.5 %collective-permute-start.3 = (bf16[8,448,128]{2,1,0:T(8,128)(2,1)S(1)}, bf16[8,448,128]{2,1,0:T(8,128)(2,1)S(1)}, u32[]{:S(2)}, u32[]{:S(2)}) collective-permute-start(bf16[8,448,128]{2,1,0:T(8,128)(2,1)S(1)} %pad_maximum_fusion.refs_2_), channel_id=1, source_target_pairs={{0,1},{1,0},{2,10},{3,11},{4,5},{5,4},{6,14},{7,15},{8,9},{9,8},{1... | collective-permute-start | bytes 2752520 | tf_op jit(solution)/shard_map/ppermute | solution.py:96
  27.6 11.4 %collective-permute-start.4 = (bf16[8,448,128]{2,1,0:T(8,128)(2,1)S(1)}, bf16[8,448,128]{2,1,0:T(8,128)(2,1)S(1)}, u32[]{:S(2)}, u32[]{:S(2)}) collective-permute-start(bf16[8,448,128]{2,1,0:T(8,128)(2,1)S(1)} %pad_maximum_fusion.refs_2_), channel_id=1, source_target_pairs={{0,2},{1,3},{2,0},{3,1},{4,6},{5,7},{6,4},{7,5},{8,10},{9,11},{10,... | collective-permute-start | bytes 2752520 | tf_op jit(solution)/shard_map/ppermute | solution.py:95
  39.0 2.5 %copy-start.2 = (bf16[8,448,128]{2,1,0:T(8,128)(2,1)}, bf16[8,448,128]{2,1,0:T(8,128)(2,1)S(1)}, u32[]{:S(2)}) copy-start(bf16[8,448,128]{2,1,0:T(8,128)(2,1)S(1)} %collective-permute-done.3.refs_3_) | copy-start | bytes 2752516
  39.0 2.5 %collective-permute-start.5 = (bf16[8,448,128]{2,1,0:T(8,128)(2,1)S(1)}, bf16[8,448,128]{2,1,0:T(8,128)(2,1)S(1)}, u32[]{:S(2)}, u32[]{:S(2)}) collective-permute-start(bf16[8,448,128]{2,1,0:T(8,128)(2,1)S(1)} %collective-permute-done.3.refs_3_), channel_id=1, source_target_pairs={{0,2},{1,3},{2,0},{3,1},{4,6},{5,7},{6,4},{7,5},{8,10},{9,11},{10,... | collective-permute-start | bytes 2752520 | tf_op jit(solution)/shard_map/ppermute | solution.py:97
  39.0 2.5 %copy-start.3 = (bf16[8,448,128]{2,1,0:T(8,128)(2,1)}, bf16[8,448,128]{2,1,0:T(8,128)(2,1)S(1)}, u32[]{:S(2)}) copy-start(bf16[8,448,128]{2,1,0:T(8,128)(2,1)S(1)} %collective-permute-done.4.refs_4_) | copy-start | bytes 2752516
  41.5 1.0 copy-start.4
  94.8 4.1 %collective-permute-start.6 = (bf16[16,448,128]{2,1,0:T(8,128)(2,1)}, bf16[16,448,128]{2,1,0:T(8,128)(2,1)S(1)}, u32[]{:S(2)}, u32[]{:S(2)}) collective-permute-start(bf16[16,448,128]{2,1,0:T(8,128)(2,1)} %get-tuple-element.13), channel_id=1, source_target_pairs={{0,2},{1,3},{2,0},{3,1},{4,6},{5,7},{6,4},{7,5},{8,10},{9,11},{10,... | collective-permute-start | bytes 5505032 | tf_op jit(solution)/shard_map/ppermute | solution.py:102
  98.9 15.3 %copy-start = (f32[16,448,128]{2,1,0:T(8,128)S(1)}, f32[16,448,128]{2,1,0:T(8,128)}, u32[]{:S(2)}) copy-start(f32[16,448,128]{2,1,0:T(8,128)} %get-tuple-element.12) | copy-start | bytes 11010052
  100.8 13.5 %collective-permute-start.7 = (bf16[8,448,128]{2,1,0:T(8,128)(2,1)S(1)}, bf16[8,448,128]{2,1,0:T(8,128)(2,1)S(1)}, u32[]{:S(2)}, u32[]{:S(2)}) collective-permute-start(bf16[8,448,128]{2,1,0:T(8,128)(2,1)S(1)} %add_convert_fusion), channel_id=1, source_target_pairs={{0,1},{1,0},{2,10},{3,11},{4,5},{5,4},{6,14},{7,15},{8,9},{9,8},{1... | collective-permute-start | bytes 2752520 | tf_op jit(solution)/shard_map/ppermute | solution.py:107
  114.4 21.9 %copy-start.5 = (f32[55416]{0:T(1024)S(1)}, f32[55416]{0:T(1024)}, u32[]{:S(2)}) copy-start(f32[55416]{0:T(1024)} %param.11) | copy-start | bytes 664996
  114.4 21.9 %copy-start.6 = (f32[55416]{0:T(1024)S(1)}, f32[55416]{0:T(1024)}, u32[]{:S(2)}) copy-start(f32[55416]{0:T(1024)} %param.13) | copy-start | bytes 664996
  114.4 21.9 %copy-start.7 = (f32[55416]{0:T(1024)S(1)}, f32[55416]{0:T(1024)}, u32[]{:S(2)}) copy-start(f32[55416]{0:T(1024)} %param.12) | copy-start | bytes 664996
  114.4 8.5 %collective-permute-start.8 = (bf16[4,448,128]{2,1,0:T(8,128)(2,1)S(1)}, bf16[4,448,128]{2,1,0:T(8,128)(2,1)S(1)}, u32[]{:S(2)}, u32[]{:S(2)}) collective-permute-start(bf16[4,448,128]{2,1,0:T(8,128)(2,1)S(1)} %add_convert_fusion.1), channel_id=1, source_target_pairs={{0,8},{1,9},{2,3},{3,2},{4,12},{5,13},{6,7},{7,6},{8,0},{9,1},{10,... | collective-permute-start | bytes 1376264 | tf_op jit(solution)/shard_map/ppermute | solution.py:107
  123.1 6.1 %collective-permute-start.9 = (bf16[2,448,128]{2,1,0:T(8,128)(2,1)S(1)}, bf16[2,448,128]{2,1,0:T(8,128)(2,1)S(1)}, u32[]{:S(2)}, u32[]{:S(2)}) collective-permute-start(bf16[2,448,128]{2,1,0:T(8,128)(2,1)S(1)} %add_convert_fusion.2), channel_id=1, source_target_pairs={{0,4},{1,5},{2,18},{3,19},{4,0},{5,1},{6,22},{7,23},{8,12},{9,13},... | collective-permute-start | bytes 688136 | tf_op jit(solution)/shard_map/ppermute | solution.py:107
  129.3 7.0 %collective-permute-start.10 = (bf16[1,448,128]{2,1,0:T(8,128)(2,1)S(1)}, bf16[1,448,128]{2,1,0:T(8,128)(2,1)S(1)}, u32[]{:S(2)}, u32[]{:S(2)}) collective-permute-start(bf16[1,448,128]{2,1,0:T(8,128)(2,1)S(1)} %add_convert_fusion.3), channel_id=1, source_target_pairs={{0,16},{1,17},{2,6},{3,7},{4,20},{5,21},{6,2},{7,3},{8,24},{9,25},... | collective-permute-start | bytes 344072 | tf_op jit(solution)/shard_map/ppermute | solution.py:107
where the time goes:
time: 138 us
  waiting for transfers between devices  57.5 us (42%)
  Pallas kernels  52.3 us (38%)
  starting transfers between devices  18.8 us (14%)
  other arithmetic  4.6 us (3%)
  local copies, waits for them, and re-layouts  2.18 us (2%)
  between operations  2.13 us (2%)
    pallas_call x1, Pallas kernels, layer(): pl.pallas_call(functools.partial(layer_kernel, flows, shard), name='layer...  52.3 us
    ppermute x4, waiting for transfers between devices, scatter_chunks(): parts.append(lax.ppermute(upper.astype(jnp.bfloat16), AXES, swap))  25.8 us
    ppermute x3, waiting for transfers between devices, gather_chunks(): held = jnp.concatenate([held, lax.ppermute(held, AXES, swap)], axis=0)  14.1 us
    ppermute x1, waiting for transfers between devices, gather_chunks(): taken = lax.ppermute(held, AXES, flow.swaps[-1])  11.4 us
    ppermute x3, starting transfers between devices, gather_chunks(): held = jnp.concatenate([held, lax.ppermute(held, AXES, swap)], axis=0)  8.48 us
    ppermute x4, starting transfers between devices, scatter_chunks(): parts.append(lax.ppermute(upper.astype(jnp.bfloat16), AXES, swap))  7.96 us
    ppermute x1, waiting for transfers between devices, scatter_chunks(): parts = [kept, lax.ppermute(sent, AXES, flow.core_swap)]  3.87 us
  transfers between devices with their start and end apart: 11, of which 10 were waited for; matrix products, arithmetic and copies ran while one was open for 0% of the time, Pallas kernels for 0%

commit v1 on v0

--- a/solution.py
+++ b/solution.py
@@ -1,5 +1,4 @@
 import functools
-import itertools
 
 import jax
 import jax.numpy as jnp
@@ -31,7 +30,7 @@
 BLOCK = 512
 GROUP = 8
 COLUMNS = 512
-FLOWS = 1
+FLOWS = 2
 
 
 def round_up(value, step):
@@ -71,21 +70,31 @@
         return me ^ jnp.where(side_one, self.across[1][slot], self.across[0][slot])
 
 
-def exchange_flows(wide, narrow):
-    devices = wide * narrow
-    core = narrow
-    bits = [1 << k for k in reversed(range(devices.bit_length() - 1)) if 1 << k != core]
-    half = (len(bits) + 1) // 2
-    flows = []
-    for order in range(FLOWS):
-        rounds = []
-        for first, second in itertools.zip_longest(bits[:half], bits[half:]):
-            if second is None:
-                rounds.append((first, first))
-            else:
-                rounds += [(first, second), (second, first)]
-        flows.append(Flow(rounds, devices, core))
-    return flows
+def gather_flows(wide, narrow):
+    bits = chip_bits(wide * narrow, narrow)
+    upper, (first, second) = bits[:-2], bits[-2:]
+    orders = [
+        (upper + [first, second], upper + [second, first]),
+        (
+            [first] + upper[:-1] + [second] + upper[-1:],
+            [second] + upper[:-1] + [first] + upper[-1:],
+        ),
+    ]
+    return [Flow(list(zip(*order)), wide * narrow, narrow) for order in orders]
+
+
+def scatter_flows(wide, narrow):
+    bits = chip_bits(wide * narrow, narrow)
+    upper, (first, second) = bits[:-2], bits[-2:]
+    orders = [
+        (upper + [first, second], upper + [second, first]),
+        ([first] + upper + [second], [second] + upper + [first]),
+    ]
+    return [Flow(list(zip(*order)), wide * narrow, narrow) for order in orders]
+
+
+def chip_bits(devices, core):
+    return [1 << k for k in reversed(range(devices.bit_length() - 1)) if 1 << k != core]
 
 
 def gather_chunks(own, flow):
@@ -304,7 +313,7 @@
             )
 
 
-def layer_kernel(flows, shard, *refs):
+def layer_kernel(gathers, scatters, shard, *refs):
     me, counts = refs[:2]
     pieces = refs[2 : 2 + 4 * FLOWS]
     tokens, cotangent, result, grad_input = refs[2 + 4 * FLOWS : 6 + 4 * FLOWS]
@@ -332,7 +341,7 @@
 
     @pl.when(step == 0)
     def _():
-        unpack(me[0], pieces, flows, shard, flat, w_qkv, w_out, w_up, w_down, vectors)
+        unpack(me[0], pieces, gathers, shard, flat, w_qkv, w_out, w_up, w_down, vectors)
         for ref in (acc_qkv, acc_out, acc_up, acc_down, acc_vectors):
             ref[...] = jnp.zeros_like(ref)
 
@@ -400,11 +409,11 @@
     @pl.when(step == pl.num_programs(0) - 1)
     def _():
         pack(
-            me[0], flows, shard, flat, acc_qkv, acc_out, acc_up, acc_down, acc_vectors, outputs
+            me[0], scatters, shard, flat, acc_qkv, acc_out, acc_up, acc_down, acc_vectors, outputs
         )
 
 
-def layer(me, counts, pieces, tokens, cotangent, flows, shard):
+def layer(me, counts, pieces, tokens, cotangent, gathers, scatters, shard):
     rows = tokens.shape[0]
     block = min(BLOCK, rows)
     quarter, piece_rows, _ = pieces[0].shape
@@ -423,7 +432,7 @@
 
     chunk_shape = (devices // 2, piece_rows, LANES)
     return pl.pallas_call(
-        functools.partial(layer_kernel, flows, shard),
+        functools.partial(layer_kernel, gathers, scatters, shard),
         name="layer",
         grid_spec=pltpu.PrefetchScalarGridSpec(
             num_scalar_prefetch=2,
@@ -480,22 +489,23 @@
 def on_device(tokens, counts, cotangent, master, first, second, rate, step):
     shard = master.shape[0]
     me = lax.axis_index(AXES)
-    flows = exchange_flows(lax.axis_size("wide"), lax.axis_size("narrow"))
+    sizes = (lax.axis_size("wide"), lax.axis_size("narrow"))
+    gathers, scatters = gather_flows(*sizes), scatter_flows(*sizes)
     rows = chunk_rows(shard)
     offset = me * shard % 1024
     own = lax.dynamic_update_slice(
         jnp.zeros((rows * LANES,), jnp.bfloat16), master.astype(jnp.bfloat16), (offset,)
     ).reshape(FLOWS, rows // FLOWS, LANES)
     pieces = []
-    for index, flow in enumerate(flows):
+    for index, flow in enumerate(gathers):
         pieces += gather_chunks(own[index], flow)
     result, grad_input, *chunks = layer(
-        me.reshape(1), counts, pieces, tokens, cotangent, flows, shard
+        me.reshape(1), counts, pieces, tokens, cotangent, gathers, scatters, shard
     )
     reduced = jnp.concatenate(
         [
             scatter_chunks(chunks[2 * index], chunks[2 * index + 1], flow)
-            for index, flow in enumerate(flows)
+            for index, flow in enumerate(scatters)
         ],
         axis=0,
     )

time: 138 us -> 130 us (0.942)
  waiting for transfers between devices: 57.5 us -> 41.1 us
  starting transfers between devices: 18.8 us -> 27.7 us
    ppermute x3 -> x6, waiting for transfers between devices: 14.1 us -> 7.87 us  [gather_chunks(): held = jnp.concatenate([held, lax.ppermute(held, AXES, swap)], axis=0)]
    ppermute x3 -> x6, starting transfers between devices: 8.48 us -> 13.4 us  [gather_chunks(): held = jnp.concatenate([held, lax.ppermute(held, AXES, swap)], axis=0)]
    ppermute x4 -> x8, waiting for transfers between devices: 25.8 us -> 21.5 us  [scatter_chunks(): parts.append(lax.ppermute(upper.astype(jnp.bfloat16), AXES, swap))]
    ppermute x1 -> x2, waiting for transfers between devices: 11.4 us -> 7.63 us  [gather_chunks(): taken = lax.ppermute(held, AXES, flow.swaps[-1])]
    ppermute x4 -> x8, starting transfers between devices: 7.96 us -> 10.9 us  [scatter_chunks(): parts.append(lax.ppermute(upper.astype(jnp.bfloat16), AXES, swap))]
    ppermute x1 -> x2, waiting for transfers between devices: 3.87 us -> 2.18 us  [scatter_chunks(): parts = [kept, lax.ppermute(sent, AXES, flow.core_swap)]]
  transfers between devices with their start and end apart: 11 -> 22, of which waited for: 10 -> 12; matrix products, arithmetic and copies ran while one was open for 0% -> 2% of each run, Pallas kernels for 0% -> 0%
where the time goes in v1:
time: 130 us
  Pallas kernels  52.5 us (40%)
  waiting for transfers between devices  41.1 us (32%)
  starting transfers between devices  27.7 us (21%)
  other arithmetic  4.28 us (3%)
  between operations  2.24 us (2%)
  local copies, waits for them, and re-layouts  1.93 us (1%)
    pallas_call x1, Pallas kernels, layer(): pl.pallas_call(functools.partial(layer_kernel, gathers, scatters, shard),...  52.5 us
    ppermute x8, waiting for transfers between devices, scatter_chunks(): parts.append(lax.ppermute(upper.astype(jnp.bfloat16), AXES, swap))  21.5 us
    ppermute x6, starting transfers between devices, gather_chunks(): held = jnp.concatenate([held, lax.ppermute(held, AXES, swap)], axis=0)  13.4 us
    ppermute x8, starting transfers between devices, scatter_chunks(): parts.append(lax.ppermute(upper.astype(jnp.bfloat16), AXES, swap))  10.9 us
    ppermute x6, waiting for transfers between devices, gather_chunks(): held = jnp.concatenate([held, lax.ppermute(held, AXES, swap)], axis=0)  7.87 us
    ppermute x2, waiting for transfers between devices, gather_chunks(): taken = lax.ppermute(held, AXES, flow.swaps[-1])  7.63 us
  transfers between devices with their start and end apart: 22, of which 12 were waited for; matrix products, arithmetic and copies ran while one was open for 2% of the time, Pallas kernels for 0%

profile of v1, /device:TPU:0, one launch (start us, length us, event | category | flops | bytes accessed | tf_op | source)
XLA Modules:
  0.0 129.8 jit_solution(15625431705265504654)
XLA Ops:
  0.6 1.0 convert_element_type.142
  1.6 1.1 dynamic_update_slice.3
  2.8 3.0 %collective-permute-start.6 = (bf16[1,224,128]{2,1,0:T(8,128)(2,1)S(1)}, bf16[1,224,128]{2,1,0:T(8,128)(2,1)S(1)}, u32[]{:S(2)}, u32[]{:S(2)}) collective-permute-start(bf16[1,224,128]{2,1,0:T(8,128)(2,1)S(1)} %get-tuple-element.22), channel_id=1, source_target_pairs={{0,4},{1,5},{2,3},{3,2},{4,0},{5,1},{6,7},{7,6},{8,12},{9,13},{10,... | collective-permute-start | bytes 172040 | tf_op jit(solution)/shard_map/ppermute | solution.py:103
  5.8 2.6 %collective-permute-start = (bf16[1,224,128]{2,1,0:T(8,128)(2,1)S(1)}, bf16[1,224,128]{2,1,0:T(8,128)(2,1)S(1)}, u32[]{:S(2)}, u32[]{:S(2)}) collective-permute-start(bf16[1,224,128]{2,1,0:T(8,128)(2,1)S(1)} %get-tuple-element.23), channel_id=1, source_target_pairs={{0,16},{1,17},{2,18},{3,19},{4,20},{5,21},{6,22},{7,23},{8,24},{9,... | collective-permute-start | bytes 172040 | tf_op jit(solution)/shard_map/ppermute | solution.py:103
  8.4 0.0 collective-permute-done.6
  8.4 2.7 %collective-permute-start.7 = (bf16[2,224,128]{2,1,0:T(8,128)(2,1)S(1)}, bf16[2,224,128]{2,1,0:T(8,128)(2,1)S(1)}, u32[]{:S(2)}, u32[]{:S(2)}) collective-permute-start(bf16[2,224,128]{2,1,0:T(8,128)(2,1)S(1)} %pad_maximum_fusion.5), channel_id=1, source_target_pairs={{0,16},{1,17},{2,18},{3,19},{4,20},{5,21},{6,22},{7,23},{8,24},{9,... | collective-permute-start | bytes 344072 | tf_op jit(solution)/shard_map/ppermute | solution.py:103
  11.2 0.0 collective-permute-done
  11.2 2.9 %collective-permute-start.1 = (bf16[2,224,128]{2,1,0:T(8,128)(2,1)S(1)}, bf16[2,224,128]{2,1,0:T(8,128)(2,1)S(1)}, u32[]{:S(2)}, u32[]{:S(2)}) collective-permute-start(bf16[2,224,128]{2,1,0:T(8,128)(2,1)S(1)} %pad_maximum_fusion.4), channel_id=1, source_target_pairs={{0,8},{1,9},{2,10},{3,11},{4,12},{5,13},{6,14},{7,15},{8,0},{9,1},... | collective-permute-start | bytes 344072 | tf_op jit(solution)/shard_map/ppermute | solution.py:103
  14.1 2.8 %collective-permute-done.7 = bf16[2,224,128]{2,1,0:T(8,128)(2,1)S(1)} collective-permute-done((bf16[2,224,128]{2,1,0:T(8,128)(2,1)S(1)}, bf16[2,224,128]{2,1,0:T(8,128)(2,1)S(1)}, u32[]{:S(2)}, u32[]{:S(2)}) %collective-permute-start.7) | collective-permute-done | bytes 114720 | tf_op jit(solution)/shard_map/ppermute | solution.py:103
  16.9 1.2 collective-permute-start.8
  18.1 0.0 collective-permute-done.1
  18.2 1.0 collective-permute-start.2
  19.2 5.0 %collective-permute-done.8 = bf16[4,224,128]{2,1,0:T(8,128)(2,1)S(1)} collective-permute-done((bf16[4,224,128]{2,1,0:T(8,128)(2,1)S(1)}, bf16[4,224,128]{2,1,0:T(8,128)(2,1)S(1)}, u32[]{:S(2)}, u32[]{:S(2)}) %collective-permute-start.8) | collective-permute-done | bytes 229408 | tf_op jit(solution)/shard_map/ppermute | solution.py:103
  24.2 0.0 copy-start
  24.2 1.2 collective-permute-start.9
  25.4 0.0 collective-permute-done.2
  25.5 0.0 copy-start.1
  25.5 0.6 collective-permute-start.3
  26.1 0.0 collective-permute-start.10
  26.1 0.5 collective-permute-start.4
  26.6 7.6 %collective-permute-done.9.refs_7_ = bf16[8,224,128]{2,1,0:T(8,128)(2,1)S(1)} collective-permute-done((bf16[8,224,128]{2,1,0:T(8,128)(2,1)S(1)}, bf16[8,224,128]{2,1,0:T(8,128)(2,1)S(1)}, u32[]{:S(2)}, u32[]{:S(2)}) %collective-permute-start.9) | collective-permute-done | bytes 458784 | tf_op jit(solution)/shard_map/ppermute | solution.py:105
  34.3 0.0 collective-permute-start.11
  34.3 0.0 collective-permute-done.3.refs_3_
  34.3 0.0 copy-start.6
  34.3 0.5 collective-permute-start.5
  34.8 0.0 collective-permute-done.10.refs_8_
  34.8 0.0 collective-permute-done.4.refs_4_
  34.8 1.3 collective-permute-done.11.refs_9_
  36.1 0.7 collective-permute-done.5.refs_5_
  36.8 0.1 copy-done.9
  36.9 0.6 copy-done.10
  37.5 52.5 %layer.1 = (bf16[2048,384]{1,0:T(8,128)(2,1)}, bf16[2048,384]{1,0:T(8,128)(2,1)}, f32[16,224,128]{2,1,0:T(8,128)}, bf16[16,224,128]{2,1,0:T(8,128)(2,1)}, f32[16...) custom-call(s32[1]{0:T(128)} %bitcast.refs_0_, s32[32]{0:T(128)} %refs_1_.1, bf16[8,224,128]{2,1,0:T(8,128)(2,1)} %copy-done.1, ...), custom_call_target="tpu_custom_call" | custom-call | tf_op jit(solution)/shard_map/layer/pallas_call | solution.py:434
  90.0 0.2 collective-permute-start.12
  90.2 0.3 collective-permute-start.17
  90.6 2.2 %collective-permute-done.12 = bf16[16,224,128]{2,1,0:T(8,128)(2,1)S(1)} collective-permute-done((bf16[16,224,128]{2,1,0:T(8,128)(2,1)}, bf16[16,224,128]{2,1,0:T(8,128)(2,1)S(1)}, u32[]{:S(2)}, u32[]{:S(2)}) %collective-permute-start.12) | collective-permute-done | bytes 917536 | tf_op jit(solution)/shard_map/ppermute | solution.py:111
  92.7 1.4 %add_convert_fusion.1 = bf16[8,224,128]{2,1,0:T(8,128)(2,1)S(1)} fusion(f32[16,224,128]{2,1,0:T(8,128)} %get-tuple-element.14, bf16[16,224,128]{2,1,0:T(8,128)(2,1)S(1)} %collective-permute-done.12), kind=kLoop, calls=%fused_computation.1 | loop fusion | flops 688128 | bytes 1835008 | tf_op jit(solution)/shard_map/convert_element_type | solution.py:116
  94.1 1.1 collective-permute-start.13
  95.2 0.0 collective-permute-done.17
  95.2 0.1 add_convert_fusion
  95.3 1.1 collective-permute-start.18
  97.7 4.9 %collective-permute-done.13 = bf16[8,224,128]{2,1,0:T(8,128)(2,1)S(1)} collective-permute-done((bf16[8,224,128]{2,1,0:T(8,128)(2,1)S(1)}, bf16[8,224,128]{2,1,0:T(8,128)(2,1)S(1)}, u32[]{:S(2)}, u32[]{:S(2)}) %collective-permute-start.13) | collective-permute-done | bytes 458784 | tf_op jit(solution)/shard_map/ppermute | solution.py:116
  102.7 0.0 copy-done.3
  102.7 0.1 add_convert_fusion.3
  102.8 0.7 collective-permute-start.14
  103.4 6.6 %collective-permute-done.18 = bf16[8,224,128]{2,1,0:T(8,128)(2,1)S(1)} collective-permute-done((bf16[8,224,128]{2,1,0:T(8,128)(2,1)S(1)}, bf16[8,224,128]{2,1,0:T(8,128)(2,1)S(1)}, u32[]{:S(2)}, u32[]{:S(2)}) %collective-permute-start.18) | collective-permute-done | bytes 458784 | tf_op jit(solution)/shard_map/ppermute | solution.py:116
  110.1 0.1 add_convert_fusion.2
  110.1 0.0 copy-start.4
  110.2 0.0 copy-start.11
  110.2 0.0 copy-start.12
  110.2 0.4 collective-permute-start.19
  110.5 0.0 collective-permute-done.14
  110.5 0.1 add_convert_fusion.5
  110.6 1.8 %collective-permute-start.15 = (bf16[2,224,128]{2,1,0:T(8,128)(2,1)S(1)}, bf16[2,224,128]{2,1,0:T(8,128)(2,1)S(1)}, u32[]{:S(2)}, u32[]{:S(2)}) collective-permute-start(bf16[2,224,128]{2,1,0:T(8,128)(2,1)S(1)} %add_convert_fusion.5), channel_id=1, source_target_pairs={{0,8},{1,9},{2,10},{3,11},{4,12},{5,13},{6,14},{7,15},{8,0},{9,1},... | collective-permute-start | bytes 344072 | tf_op jit(solution)/shard_map/ppermute | solution.py:116
  112.4 4.4 %collective-permute-done.19 = bf16[4,224,128]{2,1,0:T(8,128)(2,1)S(1)} collective-permute-done((bf16[4,224,128]{2,1,0:T(8,128)(2,1)S(1)}, bf16[4,224,128]{2,1,0:T(8,128)(2,1)S(1)}, u32[]{:S(2)}, u32[]{:S(2)}) %collective-permute-start.19) | collective-permute-done | bytes 229408 | tf_op jit(solution)/shard_map/ppermute | solution.py:116
  116.8 0.1 add_convert_fusion.4
  116.9 3.9 %collective-permute-start.20 = (bf16[2,224,128]{2,1,0:T(8,128)(2,1)S(1)}, bf16[2,224,128]{2,1,0:T(8,128)(2,1)S(1)}, u32[]{:S(2)}, u32[]{:S(2)}) collective-permute-start(bf16[2,224,128]{2,1,0:T(8,128)(2,1)S(1)} %add_convert_fusion.4), channel_id=1, source_target_pairs={{0,16},{1,17},{2,18},{3,19},{4,20},{5,21},{6,22},{7,23},{8,24},{9,... | collective-permute-start | bytes 344072 | tf_op jit(solution)/shard_map/ppermute | solution.py:116
  120.8 0.0 collective-permute-done.15
  120.8 1.2 collective-permute-start.16
  122.0 2.2 %collective-permute-done.20 = bf16[2,224,128]{2,1,0:T(8,128)(2,1)S(1)} collective-permute-done((bf16[2,224,128]{2,1,0:T(8,128)(2,1)S(1)}, bf16[2,224,128]{2,1,0:T(8,128)(2,1)S(1)}, u32[]{:S(2)}, u32[]{:S(2)}) %collective-permute-start.20) | collective-permute-done | bytes 114720 | tf_op jit(solution)/shard_map/ppermute | solution.py:116
  124.2 0.9 collective-permute-start.21
  125.1 0.9 collective-permute-done.16
  126.1 2.4 %collective-permute-done.21 = bf16[1,224,128]{2,1,0:T(8,128)(2,1)S(1)} collective-permute-done((bf16[1,224,128]{2,1,0:T(8,128)(2,1)S(1)}, bf16[1,224,128]{2,1,0:T(8,128)(2,1)S(1)}, u32[]{:S(2)}, u32[]{:S(2)}) %collective-permute-start.21) | collective-permute-done | bytes 57376 | tf_op jit(solution)/shard_map/ppermute | solution.py:116
  128.5 0.1 add_bitcast_fusion
  128.6 1.2 fusion.5
  (29 shorter events, 0.4 us)
Async XLA Ops:
  2.8 5.6 %collective-permute-start.6 = (bf16[1,224,128]{2,1,0:T(8,128)(2,1)S(1)}, bf16[1,224,128]{2,1,0:T(8,128)(2,1)S(1)}, u32[]{:S(2)}, u32[]{:S(2)}) collective-permute-start(bf16[1,224,128]{2,1,0:T(8,128)(2,1)S(1)} %get-tuple-element.22), channel_id=1, source_target_pairs={{0,4},{1,5},{2,3},{3,2},{4,0},{5,1},{6,7},{7,6},{8,12},{9,13},{10,... | collective-permute-start | bytes 172040 | tf_op jit(solution)/shard_map/ppermute | solution.py:103
  5.8 5.4 %collective-permute-start = (bf16[1,224,128]{2,1,0:T(8,128)(2,1)S(1)}, bf16[1,224,128]{2,1,0:T(8,128)(2,1)S(1)}, u32[]{:S(2)}, u32[]{:S(2)}) collective-permute-start(bf16[1,224,128]{2,1,0:T(8,128)(2,1)S(1)} %get-tuple-element.23), channel_id=1, source_target_pairs={{0,16},{1,17},{2,18},{3,19},{4,20},{5,21},{6,22},{7,23},{8,24},{9,... | collective-permute-start | bytes 172040 | tf_op jit(solution)/shard_map/ppermute | solution.py:103
  8.4 8.5 %collective-permute-start.7 = (bf16[2,224,128]{2,1,0:T(8,128)(2,1)S(1)}, bf16[2,224,128]{2,1,0:T(8,128)(2,1)S(1)}, u32[]{:S(2)}, u32[]{:S(2)}) collective-permute-start(bf16[2,224,128]{2,1,0:T(8,128)(2,1)S(1)} %pad_maximum_fusion.5), channel_id=1, source_target_pairs={{0,16},{1,17},{2,18},{3,19},{4,20},{5,21},{6,22},{7,23},{8,24},{9,... | collective-permute-start | bytes 344072 | tf_op jit(solution)/shard_map/ppermute | solution.py:103
  11.2 7.0 %collective-permute-start.1 = (bf16[2,224,128]{2,1,0:T(8,128)(2,1)S(1)}, bf16[2,224,128]{2,1,0:T(8,128)(2,1)S(1)}, u32[]{:S(2)}, u32[]{:S(2)}) collective-permute-start(bf16[2,224,128]{2,1,0:T(8,128)(2,1)S(1)} %pad_maximum_fusion.4), channel_id=1, source_target_pairs={{0,8},{1,9},{2,10},{3,11},{4,12},{5,13},{6,14},{7,15},{8,0},{9,1},... | collective-permute-start | bytes 344072 | tf_op jit(solution)/shard_map/ppermute | solution.py:103
  16.9 7.2 %collective-permute-start.8 = (bf16[4,224,128]{2,1,0:T(8,128)(2,1)S(1)}, bf16[4,224,128]{2,1,0:T(8,128)(2,1)S(1)}, u32[]{:S(2)}, u32[]{:S(2)}) collective-permute-start(bf16[4,224,128]{2,1,0:T(8,128)(2,1)S(1)} %pad_maximum_fusion.3), channel_id=1, source_target_pairs={{0,1},{1,0},{2,6},{3,7},{4,5},{5,4},{6,2},{7,3},{8,9},{9,8},{10,14... | collective-permute-start | bytes 688136 | tf_op jit(solution)/shard_map/ppermute | solution.py:103
  18.2 7.3 %collective-permute-start.2 = (bf16[4,224,128]{2,1,0:T(8,128)(2,1)S(1)}, bf16[4,224,128]{2,1,0:T(8,128)(2,1)S(1)}, u32[]{:S(2)}, u32[]{:S(2)}) collective-permute-start(bf16[4,224,128]{2,1,0:T(8,128)(2,1)S(1)} %pad_maximum_fusion.2), channel_id=1, source_target_pairs={{0,4},{1,5},{2,3},{3,2},{4,0},{5,1},{6,7},{7,6},{8,12},{9,13},{10,... | collective-permute-start | bytes 688136 | tf_op jit(solution)/shard_map/ppermute | solution.py:103
  24.2 12.5 %copy-start = (bf16[8,224,128]{2,1,0:T(8,128)(2,1)}, bf16[8,224,128]{2,1,0:T(8,128)(2,1)S(1)}, u32[]{:S(2)}) copy-start(bf16[8,224,128]{2,1,0:T(8,128)(2,1)S(1)} %pad_maximum_fusion.1.refs_6_) | copy-start | bytes 1376260
  24.2 10.0 %collective-permute-start.9 = (bf16[8,224,128]{2,1,0:T(8,128)(2,1)S(1)}, bf16[8,224,128]{2,1,0:T(8,128)(2,1)S(1)}, u32[]{:S(2)}, u32[]{:S(2)}) collective-permute-start(bf16[8,224,128]{2,1,0:T(8,128)(2,1)S(1)} %pad_maximum_fusion.1.refs_6_), channel_id=1, source_target_pairs={{0,8},{1,9},{2,10},{3,11},{4,12},{5,13},{6,14},{7,15},{8,0},{9,1},... | collective-permute-start | bytes 1376264 | tf_op jit(solution)/shard_map/ppermute | solution.py:105
  25.5 11.2 %copy-start.1 = (bf16[8,224,128]{2,1,0:T(8,128)(2,1)}, bf16[8,224,128]{2,1,0:T(8,128)(2,1)S(1)}, u32[]{:S(2)}) copy-start(bf16[8,224,128]{2,1,0:T(8,128)(2,1)S(1)} %pad_maximum_fusion.refs_2_) | copy-start | bytes 1376260
  25.5 8.8 %collective-permute-start.3 = (bf16[8,224,128]{2,1,0:T(8,128)(2,1)S(1)}, bf16[8,224,128]{2,1,0:T(8,128)(2,1)S(1)}, u32[]{:S(2)}, u32[]{:S(2)}) collective-permute-start(bf16[8,224,128]{2,1,0:T(8,128)(2,1)S(1)} %pad_maximum_fusion.refs_2_), channel_id=1, source_target_pairs={{0,1},{1,0},{2,6},{3,7},{4,5},{5,4},{6,2},{7,3},{8,9},{9,8},{10,14... | collective-permute-start | bytes 1376264 | tf_op jit(solution)/shard_map/ppermute | solution.py:105
  26.1 8.7 %collective-permute-start.10 = (bf16[8,224,128]{2,1,0:T(8,128)(2,1)S(1)}, bf16[8,224,128]{2,1,0:T(8,128)(2,1)S(1)}, u32[]{:S(2)}, u32[]{:S(2)}) collective-permute-start(bf16[8,224,128]{2,1,0:T(8,128)(2,1)S(1)} %pad_maximum_fusion.1.refs_6_), channel_id=1, source_target_pairs={{0,2},{1,3},{2,0},{3,1},{4,6},{5,7},{6,4},{7,5},{8,10},{9,11},{10,... | collective-permute-start | bytes 1376264 | tf_op jit(solution)/shard_map/ppermute | solution.py:104
  26.1 8.7 %collective-permute-start.4 = (bf16[8,224,128]{2,1,0:T(8,128)(2,1)S(1)}, bf16[8,224,128]{2,1,0:T(8,128)(2,1)S(1)}, u32[]{:S(2)}, u32[]{:S(2)}) collective-permute-start(bf16[8,224,128]{2,1,0:T(8,128)(2,1)S(1)} %pad_maximum_fusion.refs_2_), channel_id=1, source_target_pairs={{0,2},{1,3},{2,0},{3,1},{4,6},{5,7},{6,4},{7,5},{8,10},{9,11},{10,... | collective-permute-start | bytes 1376264 | tf_op jit(solution)/shard_map/ppermute | solution.py:104
  34.3 2.5 %copy-start.5 = (bf16[8,224,128]{2,1,0:T(8,128)(2,1)}, bf16[8,224,128]{2,1,0:T(8,128)(2,1)S(1)}, u32[]{:S(2)}) copy-start(bf16[8,224,128]{2,1,0:T(8,128)(2,1)S(1)} %collective-permute-done.9.refs_7_) | copy-start | bytes 1376260
  34.3 1.8 %collective-permute-start.11 = (bf16[8,224,128]{2,1,0:T(8,128)(2,1)S(1)}, bf16[8,224,128]{2,1,0:T(8,128)(2,1)S(1)}, u32[]{:S(2)}, u32[]{:S(2)}) collective-permute-start(bf16[8,224,128]{2,1,0:T(8,128)(2,1)S(1)} %collective-permute-done.9.refs_7_), channel_id=1, source_target_pairs={{0,2},{1,3},{2,0},{3,1},{4,6},{5,7},{6,4},{7,5},{8,10},{9,11},{10,... | collective-permute-start | bytes 1376264 | tf_op jit(solution)/shard_map/ppermute | solution.py:106
  34.3 2.5 %copy-start.6 = (bf16[8,224,128]{2,1,0:T(8,128)(2,1)}, bf16[8,224,128]{2,1,0:T(8,128)(2,1)S(1)}, u32[]{:S(2)}) copy-start(bf16[8,224,128]{2,1,0:T(8,128)(2,1)S(1)} %collective-permute-done.3.refs_3_) | copy-start | bytes 1376260
  34.3 2.5 %collective-permute-start.5 = (bf16[8,224,128]{2,1,0:T(8,128)(2,1)S(1)}, bf16[8,224,128]{2,1,0:T(8,128)(2,1)S(1)}, u32[]{:S(2)}, u32[]{:S(2)}) collective-permute-start(bf16[8,224,128]{2,1,0:T(8,128)(2,1)S(1)} %collective-permute-done.3.refs_3_), channel_id=1, source_target_pairs={{0,2},{1,3},{2,0},{3,1},{4,6},{5,7},{6,4},{7,5},{8,10},{9,11},{10,... | collective-permute-start | bytes 1376264 | tf_op jit(solution)/shard_map/ppermute | solution.py:106
  34.8 2.0 %copy-start.7 = (bf16[8,224,128]{2,1,0:T(8,128)(2,1)}, bf16[8,224,128]{2,1,0:T(8,128)(2,1)S(1)}, u32[]{:S(2)}) copy-start(bf16[8,224,128]{2,1,0:T(8,128)(2,1)S(1)} %collective-permute-done.10.refs_8_) | copy-start | bytes 1376260
  34.8 2.0 %copy-start.8 = (bf16[8,224,128]{2,1,0:T(8,128)(2,1)}, bf16[8,224,128]{2,1,0:T(8,128)(2,1)S(1)}, u32[]{:S(2)}) copy-start(bf16[8,224,128]{2,1,0:T(8,128)(2,1)S(1)} %collective-permute-done.4.refs_4_) | copy-start | bytes 1376260
  36.1 0.8 copy-start.9
  36.7 0.8 copy-start.10
  90.0 5.2 %copy-start.2 = (f32[16,224,128]{2,1,0:T(8,128)S(1)}, f32[16,224,128]{2,1,0:T(8,128)}, u32[]{:S(2)}) copy-start(f32[16,224,128]{2,1,0:T(8,128)} %get-tuple-element.16) | copy-start | bytes 5505028
  90.0 2.7 %collective-permute-start.12 = (bf16[16,224,128]{2,1,0:T(8,128)(2,1)}, bf16[16,224,128]{2,1,0:T(8,128)(2,1)S(1)}, u32[]{:S(2)}, u32[]{:S(2)}) collective-permute-start(bf16[16,224,128]{2,1,0:T(8,128)(2,1)} %get-tuple-element.15), channel_id=1, source_target_pairs={{0,2},{1,3},{2,0},{3,1},{4,6},{5,7},{6,4},{7,5},{8,10},{9,11},{10,... | collective-permute-start | bytes 2752520 | tf_op jit(solution)/shard_map/ppermute | solution.py:111
  90.2 5.0 %collective-permute-start.17 = (bf16[16,224,128]{2,1,0:T(8,128)(2,1)}, bf16[16,224,128]{2,1,0:T(8,128)(2,1)S(1)}, u32[]{:S(2)}, u32[]{:S(2)}) collective-permute-start(bf16[16,224,128]{2,1,0:T(8,128)(2,1)} %get-tuple-element.17), channel_id=1, source_target_pairs={{0,2},{1,3},{2,0},{3,1},{4,6},{5,7},{6,4},{7,5},{8,10},{9,11},{10,... | collective-permute-start | bytes 2752520 | tf_op jit(solution)/shard_map/ppermute | solution.py:111
  92.7 10.0 %copy-start.3 = (f32[16,224,128]{2,1,0:T(8,128)S(1)}, f32[16,224,128]{2,1,0:T(8,128)}, u32[]{:S(2)}) copy-start(f32[16,224,128]{2,1,0:T(8,128)} %get-tuple-element.14) | copy-start | bytes 5505028
  94.1 8.5 %collective-permute-start.13 = (bf16[8,224,128]{2,1,0:T(8,128)(2,1)S(1)}, bf16[8,224,128]{2,1,0:T(8,128)(2,1)S(1)}, u32[]{:S(2)}, u32[]{:S(2)}) collective-permute-start(bf16[8,224,128]{2,1,0:T(8,128)(2,1)S(1)} %add_convert_fusion.1), channel_id=1, source_target_pairs={{0,1},{1,0},{2,6},{3,7},{4,5},{5,4},{6,2},{7,3},{8,9},{9,8},{10,14... | collective-permute-start | bytes 1376264 | tf_op jit(solution)/shard_map/ppermute | solution.py:116
  95.3 14.7 %collective-permute-start.18 = (bf16[8,224,128]{2,1,0:T(8,128)(2,1)S(1)}, bf16[8,224,128]{2,1,0:T(8,128)(2,1)S(1)}, u32[]{:S(2)}, u32[]{:S(2)}) collective-permute-start(bf16[8,224,128]{2,1,0:T(8,128)(2,1)S(1)} %add_convert_fusion), channel_id=1, source_target_pairs={{0,1},{1,0},{2,6},{3,7},{4,5},{5,4},{6,2},{7,3},{8,9},{9,8},{10,14... | collective-permute-start | bytes 1376264 | tf_op jit(solution)/shard_map/ppermute | solution.py:116
  102.8 7.8 %collective-permute-start.14 = (bf16[4,224,128]{2,1,0:T(8,128)(2,1)S(1)}, bf16[4,224,128]{2,1,0:T(8,128)(2,1)S(1)}, u32[]{:S(2)}, u32[]{:S(2)}) collective-permute-start(bf16[4,224,128]{2,1,0:T(8,128)(2,1)S(1)} %add_convert_fusion.3), channel_id=1, source_target_pairs={{0,4},{1,5},{2,3},{3,2},{4,0},{5,1},{6,7},{7,6},{8,12},{9,13},{10,... | collective-permute-start | bytes 688136 | tf_op jit(solution)/shard_map/ppermute | solution.py:116
  110.1 18.4 %copy-start.4 = (f32[55416]{0:T(1024)S(1)}, f32[55416]{0:T(1024)}, u32[]{:S(2)}) copy-start(f32[55416]{0:T(1024)} %param.11) | copy-start | bytes 664996
  110.2 18.4 %copy-start.11 = (f32[55416]{0:T(1024)S(1)}, f32[55416]{0:T(1024)}, u32[]{:S(2)}) copy-start(f32[55416]{0:T(1024)} %param.13) | copy-start | bytes 664996
  110.2 18.4 %copy-start.12 = (f32[55416]{0:T(1024)S(1)}, f32[55416]{0:T(1024)}, u32[]{:S(2)}) copy-start(f32[55416]{0:T(1024)} %param.12) | copy-start | bytes 664996
  110.2 6.7 %collective-permute-start.19 = (bf16[4,224,128]{2,1,0:T(8,128)(2,1)S(1)}, bf16[4,224,128]{2,1,0:T(8,128)(2,1)S(1)}, u32[]{:S(2)}, u32[]{:S(2)}) collective-permute-start(bf16[4,224,128]{2,1,0:T(8,128)(2,1)S(1)} %add_convert_fusion.2), channel_id=1, source_target_pairs={{0,8},{1,9},{2,10},{3,11},{4,12},{5,13},{6,14},{7,15},{8,0},{9,1},... | collective-permute-start | bytes 688136 | tf_op jit(solution)/shard_map/ppermute | solution.py:116
  110.6 10.2 %collective-permute-start.15 = (bf16[2,224,128]{2,1,0:T(8,128)(2,1)S(1)}, bf16[2,224,128]{2,1,0:T(8,128)(2,1)S(1)}, u32[]{:S(2)}, u32[]{:S(2)}) collective-permute-start(bf16[2,224,128]{2,1,0:T(8,128)(2,1)S(1)} %add_convert_fusion.5), channel_id=1, source_target_pairs={{0,8},{1,9},{2,10},{3,11},{4,12},{5,13},{6,14},{7,15},{8,0},{9,1},... | collective-permute-start | bytes 344072 | tf_op jit(solution)/shard_map/ppermute | solution.py:116
  116.9 7.3 %collective-permute-start.20 = (bf16[2,224,128]{2,1,0:T(8,128)(2,1)S(1)}, bf16[2,224,128]{2,1,0:T(8,128)(2,1)S(1)}, u32[]{:S(2)}, u32[]{:S(2)}) collective-permute-start(bf16[2,224,128]{2,1,0:T(8,128)(2,1)S(1)} %add_convert_fusion.4), channel_id=1, source_target_pairs={{0,16},{1,17},{2,18},{3,19},{4,20},{5,21},{6,22},{7,23},{8,24},{9,... | collective-permute-start | bytes 344072 | tf_op jit(solution)/shard_map/ppermute | solution.py:116
  120.8 5.2 %collective-permute-start.16 = (bf16[1,224,128]{2,1,0:T(8,128)(2,1)S(1)}, bf16[1,224,128]{2,1,0:T(8,128)(2,1)S(1)}, u32[]{:S(2)}, u32[]{:S(2)}) collective-permute-start(bf16[1,224,128]{2,1,0:T(8,128)(2,1)S(1)} %add_convert_fusion.7), channel_id=1, source_target_pairs={{0,16},{1,17},{2,18},{3,19},{4,20},{5,21},{6,22},{7,23},{8,24},{9,... | collective-permute-start | bytes 172040 | tf_op jit(solution)/shard_map/ppermute | solution.py:116
  124.2 4.2 %collective-permute-start.21 = (bf16[1,224,128]{2,1,0:T(8,128)(2,1)S(1)}, bf16[1,224,128]{2,1,0:T(8,128)(2,1)S(1)}, u32[]{:S(2)}, u32[]{:S(2)}) collective-permute-start(bf16[1,224,128]{2,1,0:T(8,128)(2,1)S(1)} %add_convert_fusion.6), channel_id=1, source_target_pairs={{0,4},{1,5},{2,3},{3,2},{4,0},{5,1},{6,7},{7,6},{8,12},{9,13},{10,... | collective-permute-start | bytes 172040 | tf_op jit(solution)/shard_map/ppermute | solution.py:116

commit v2 on v1

--- a/solution.py
+++ b/solution.py
@@ -26,7 +26,7 @@
 BASE_DOWN = BASE_UP + UP_ROWS
 BASE_VEC = BASE_DOWN + UP_ROWS
 VECTORS = ("gain_one", "shift_one", "bias_out", "gain_two", "shift_two", "bias_up", "bias_down")
-VMEM_LIMIT = 60 * 1024 * 1024
+VMEM_LIMIT = 44 * 1024 * 1024
 BLOCK = 512
 GROUP = 8
 COLUMNS = 512
@@ -70,51 +70,62 @@
         return me ^ jnp.where(side_one, self.across[1][slot], self.across[0][slot])
 
 
-def gather_flows(wide, narrow):
+def exchange_flows(wide, narrow):
     bits = chip_bits(wide * narrow, narrow)
     upper, (first, second) = bits[:-2], bits[-2:]
     orders = [
         (upper + [first, second], upper + [second, first]),
         (
-            [first] + upper[:-1] + [second] + upper[-1:],
-            [second] + upper[:-1] + [first] + upper[-1:],
+            upper[:1] + [second, first] + upper[1:],
+            upper[:1] + [first, second] + upper[1:],
         ),
     ]
     return [Flow(list(zip(*order)), wide * narrow, narrow) for order in orders]
 
 
-def scatter_flows(wide, narrow):
-    bits = chip_bits(wide * narrow, narrow)
-    upper, (first, second) = bits[:-2], bits[-2:]
-    orders = [
-        (upper + [first, second], upper + [second, first]),
-        ([first] + upper + [second], [second] + upper + [first]),
-    ]
-    return [Flow(list(zip(*order)), wide * narrow, narrow) for order in orders]
-
-
 def chip_bits(devices, core):
     return [1 << k for k in reversed(range(devices.bit_length() - 1)) if 1 << k != core]
 
 
-def gather_chunks(own, flow):
-    held = own[None]
-    for swap in flow.swaps[:-1]:
-        held = jnp.concatenate([held, lax.ppermute(held, AXES, swap)], axis=0)
-    held_core = lax.ppermute(held, AXES, flow.core_swap)
-    taken = lax.ppermute(held, AXES, flow.swaps[-1])
-    taken_core = lax.ppermute(taken, AXES, flow.core_swap)
-    return held, taken, held_core, taken_core
-
-
-def scatter_chunks(kept, sent, flow):
-    parts = [kept, lax.ppermute(sent, AXES, flow.core_swap)]
-    for swap in reversed(flow.swaps):
-        half = parts[0].shape[0] // 2
-        upper = sum(part[half:].astype(jnp.float32) for part in parts)
-        parts = [part[:half] for part in parts]
-        parts.append(lax.ppermute(upper.astype(jnp.bfloat16), AXES, swap))
-    return sum(part[0].astype(jnp.float32) for part in parts)
+def after(value, other):
+    if other is None:
+        return value
+    return lax.optimization_barrier((value, other))[0]
+
+
+def gather_chunks(owns, flows):
+    held = [own[None] for own in owns]
+    taken = [None] * len(flows)
+    turns = list(reversed(range(len(flows))))
+    last = None
+    for index in range(len(flows[0].swaps)):
+        for turn in turns:
+            if index:
+                held[turn] = jnp.concatenate([after(held[turn], last), taken[turn]], axis=0)
+            last = held[turn]
+            taken[turn] = lax.ppermute(last, AXES, flows[turn].swaps[index])
+    pieces = []
+    for flow, kept, new in zip(flows, held, taken):
+        pieces += [kept, new]
+        pieces += [lax.ppermute(piece, AXES, flow.core_swap) for piece in (kept, new)]
+    return pieces
+
+
+def scatter_chunks(chunks, flows):
+    parts = [
+        [kept, lax.ppermute(sent, AXES, flow.core_swap)]
+        for kept, sent, flow in zip(chunks[::2], chunks[1::2], flows)
+    ]
+    last = None
+    for index in reversed(range(len(flows[0].swaps))):
+        for turn, flow in enumerate(flows):
+            half = parts[turn][0].shape[0] // 2
+            parts[turn][0] = after(parts[turn][0], last)
+            upper = sum(part[half:].astype(jnp.float32) for part in parts[turn])
+            last = upper.astype(jnp.bfloat16)
+            parts[turn] = [part[:half] for part in parts[turn]]
+            parts[turn].append(lax.ppermute(last, AXES, flow.swaps[index]))
+    return [sum(part[0].astype(jnp.float32) for part in flow) for flow in parts]
 
 
 def vector_width(name):
@@ -313,7 +324,7 @@
             )
 
 
-def layer_kernel(gathers, scatters, shard, *refs):
+def layer_kernel(flows, shard, *refs):
     me, counts = refs[:2]
     pieces = refs[2 : 2 + 4 * FLOWS]
     tokens, cotangent, result, grad_input = refs[2 + 4 * FLOWS : 6 + 4 * FLOWS]
@@ -341,7 +352,7 @@
 
     @pl.when(step == 0)
     def _():
-        unpack(me[0], pieces, gathers, shard, flat, w_qkv, w_out, w_up, w_down, vectors)
+        unpack(me[0], pieces, flows, shard, flat, w_qkv, w_out, w_up, w_down, vectors)
         for ref in (acc_qkv, acc_out, acc_up, acc_down, acc_vectors):
             ref[...] = jnp.zeros_like(ref)
 
@@ -409,11 +420,11 @@
     @pl.when(step == pl.num_programs(0) - 1)
     def _():
         pack(
-            me[0], scatters, shard, flat, acc_qkv, acc_out, acc_up, acc_down, acc_vectors, outputs
+            me[0], flows, shard, flat, acc_qkv, acc_out, acc_up, acc_down, acc_vectors, outputs
         )
 
 
-def layer(me, counts, pieces, tokens, cotangent, gathers, scatters, shard):
+def layer(me, counts, pieces, tokens, cotangent, flows, shard):
     rows = tokens.shape[0]
     block = min(BLOCK, rows)
     quarter, piece_rows, _ = pieces[0].shape
@@ -425,20 +436,17 @@
     def by_rows():
         return pl.BlockSpec((block, D), lambda i, me, counts: (i, 0))
 
-    def whole(shape):
-        return pl.BlockSpec(
-            shape, lambda i, me, counts: (0,) * len(shape), pipeline_mode=pl.Buffered(1)
-        )
-
     chunk_shape = (devices // 2, piece_rows, LANES)
     return pl.pallas_call(
-        functools.partial(layer_kernel, gathers, scatters, shard),
+        functools.partial(layer_kernel, flows, shard),
         name="layer",
         grid_spec=pltpu.PrefetchScalarGridSpec(
             num_scalar_prefetch=2,
             grid=(rows // block,),
-            in_specs=[whole(piece.shape) for piece in pieces] + [by_rows(), by_rows()],
-            out_specs=[by_rows(), by_rows()] + [whole(chunk_shape)] * (2 * FLOWS),
+            in_specs=[pl.BlockSpec(memory_space=pltpu.VMEM)] * len(pieces)
+            + [by_rows(), by_rows()],
+            out_specs=[by_rows(), by_rows()]
+            + [pl.BlockSpec(memory_space=pltpu.VMEM)] * (2 * FLOWS),
             scratch_shapes=[
                 pltpu.VMEM((flat_rows, LANES), full),
                 pltpu.VMEM((D, 3 * D), low),
@@ -459,7 +467,7 @@
             ],
         ),
         out_shape=[jax.ShapeDtypeStruct((rows, D), low)] * 2
-        + [jax.ShapeDtypeStruct(chunk_shape, dtype) for dtype in (full, low)] * FLOWS,
+        + [pltpu.VMEM(chunk_shape, dtype) for dtype in (full, low)] * FLOWS,
         compiler_params=pltpu.CompilerParams(vmem_limit_bytes=VMEM_LIMIT),
     )(me, counts, *pieces, tokens, cotangent)
 
@@ -490,25 +498,17 @@
     shard = master.shape[0]
     me = lax.axis_index(AXES)
     sizes = (lax.axis_size("wide"), lax.axis_size("narrow"))
-    gathers, scatters = gather_flows(*sizes), scatter_flows(*sizes)
+    flows = exchange_flows(*sizes)
     rows = chunk_rows(shard)
     offset = me * shard % 1024
     own = lax.dynamic_update_slice(
         jnp.zeros((rows * LANES,), jnp.bfloat16), master.astype(jnp.bfloat16), (offset,)
     ).reshape(FLOWS, rows // FLOWS, LANES)
-    pieces = []
-    for index, flow in enumerate(gathers):
-        pieces += gather_chunks(own[index], flow)
+    pieces = gather_chunks(own, flows)
     result, grad_input, *chunks = layer(
-        me.reshape(1), counts, pieces, tokens, cotangent, gathers, scatters, shard
-    )
-    reduced = jnp.concatenate(
-        [
-            scatter_chunks(chunks[2 * index], chunks[2 * index + 1], flow)
-            for index, flow in enumerate(scatters)
-        ],
-        axis=0,
-    )
+        me.reshape(1), counts, pieces, tokens, cotangent, flows, shard
+    )
+    reduced = jnp.concatenate(scatter_chunks(chunks, flows), axis=0)
     reduced = lax.dynamic_slice(reduced.reshape(rows * LANES), (offset,), (shard,))
     position = me * shard + jnp.arange(shard, dtype=jnp.int32)
     first_new = 0.5 * first + 0.5 * reduced

time: 130 us -> 122 us (0.938)
  waiting for transfers between devices: 41.1 us -> 35 us
  Pallas kernels: 52.5 us -> 49.3 us
  starting transfers between devices: 27.7 us -> 30.7 us
    ppermute x22, waiting for transfers between devices: 41.1 us -> 35 us  [the longest x8 17.4 us: gather_chunks(): taken[turn] = lax.ppermute(last, AXES, flows[turn].swaps[index])]
    pallas_call x1, Pallas kernels: 52.5 us -> 49.3 us  [layer(): pl.pallas_call(functools.partial(layer_kernel, flows, shard), name='layer...]
    ppermute x22, starting transfers between devices: 27.7 us -> 30.7 us  [the longest x8 14.8 us: scatter_chunks(): parts[turn].append(lax.ppermute(last, AXES, flow.swaps[index]))]
    convert_element_type x8 -> x5, other arithmetic: 1.87 us -> 0.42 us  [scatter_chunks(): last = upper.astype(jnp.bfloat16)]
  transfers between devices with their start and end apart: 22 -> 22, of which waited for: 12 -> 14; matrix products, arithmetic and copies ran while one was open for 2% -> 1% of each run, Pallas kernels for 0% -> 0%
where the time goes in v2:
time: 122 us; the launch traced here: 121 us
  Pallas kernels  49.3 us (40%)
  waiting for transfers between devices  35 us (29%)
  starting transfers between devices  30.7 us (25%)
  other arithmetic  3 us (2%)
  between operations  2.18 us (2%)
  local copies, waits for them, and re-layouts  1.37 us (1%)
    pallas_call x1, Pallas kernels, layer(): pl.pallas_call(functools.partial(layer_kernel, flows, shard), name='layer...  49.3 us
    ppermute x8, waiting for transfers between devices, gather_chunks(): taken[turn] = lax.ppermute(last, AXES, flows[turn].swaps[index])  17.4 us
    ppermute x8, starting transfers between devices, scatter_chunks(): parts[turn].append(lax.ppermute(last, AXES, flow.swaps[index]))  14.8 us
    ppermute x8, starting transfers between devices, gather_chunks(): taken[turn] = lax.ppermute(last, AXES, flows[turn].swaps[index])  14.8 us
    ppermute x8, waiting for transfers between devices, scatter_chunks(): parts[turn].append(lax.ppermute(last, AXES, flow.swaps[index]))  13.8 us
  transfers between devices with their start and end apart: 22, of which 14 were waited for; matrix products, arithmetic and copies ran while one was open for 1% of the time, Pallas kernels for 0%

profile of v2, /device:TPU:0, one launch (start us, length us, event | category | flops | bytes accessed | tf_op | source)
XLA Modules:
  0.0 121.5 jit_solution(352292227838280931)
XLA Ops:
  0.6 1.0 convert_element_type.142
  1.6 0.0 copy-start
  1.6 1.1 dynamic_update_slice.3
  2.8 4.1 %collective-permute-start = (bf16[1,224,128]{2,1,0:T(8,128)(2,1)S(1)}, bf16[1,224,128]{2,1,0:T(8,128)(2,1)S(1)}, u32[]{:S(2)}, u32[]{:S(2)}) collective-permute-start(bf16[1,224,128]{2,1,0:T(8,128)(2,1)S(1)} %get-tuple-element.60), channel_id=1, source_target_pairs={{0,16},{1,17},{2,18},{3,19},{4,20},{5,21},{6,22},{7,23},{8,24},{9,... | collective-permute-start | bytes 172040 | tf_op jit(solution)/shard_map/ppermute | solution.py:106
  6.9 0.1 collective-permute-start.1
  7.0 2.7 %collective-permute-done = bf16[1,224,128]{2,1,0:T(8,128)(2,1)S(1)} collective-permute-done((bf16[1,224,128]{2,1,0:T(8,128)(2,1)S(1)}, bf16[1,224,128]{2,1,0:T(8,128)(2,1)S(1)}, u32[]{:S(2)}, u32[]{:S(2)}) %collective-permute-start) | collective-permute-done | bytes 57376 | tf_op jit(solution)/shard_map/ppermute | solution.py:106
  9.7 1.8 %collective-permute-start.2 = (bf16[2,224,128]{2,1,0:T(8,128)(2,1)S(1)}, bf16[2,224,128]{2,1,0:T(8,128)(2,1)S(1)}, u32[]{:S(2)}, u32[]{:S(2)}) collective-permute-start(bf16[2,224,128]{2,1,0:T(8,128)(2,1)S(1)} %constant_dynamic-update-slice_fusion), channel_id=1, source_target_pairs={{0,1},{1,0},{2,6},{3,7},{4,5},{5,4},{6,2},{7,3},{8,9},{9,8},{10,14... | collective-permute-start | bytes 344072 | tf_op jit(solution)/shard_map/ppermute | solution.py:106
  11.5 0.7 collective-permute-done.1
  12.3 1.5 %collective-permute-start.3 = (bf16[2,224,128]{2,1,0:T(8,128)(2,1)S(1)}, bf16[2,224,128]{2,1,0:T(8,128)(2,1)S(1)}, u32[]{:S(2)}, u32[]{:S(2)}) collective-permute-start(bf16[2,224,128]{2,1,0:T(8,128)(2,1)S(1)} %constant_dynamic-update-slice_fusion.2), channel_id=1, source_target_pairs={{0,8},{1,9},{2,10},{3,11},{4,12},{5,13},{6,14},{7,15},{8,0},{9,1},... | collective-permute-start | bytes 344072 | tf_op jit(solution)/shard_map/ppermute | solution.py:106
  13.8 0.7 collective-permute-done.2
  14.6 1.8 %collective-permute-start.4 = (bf16[4,224,128]{2,1,0:T(8,128)(2,1)S(1)}, bf16[4,224,128]{2,1,0:T(8,128)(2,1)S(1)}, u32[]{:S(2)}, u32[]{:S(2)}) collective-permute-start(bf16[4,224,128]{2,1,0:T(8,128)(2,1)S(1)} %constant_dynamic-update-slice_fusion.4), channel_id=1, source_target_pairs={{0,4},{1,5},{2,3},{3,2},{4,0},{5,1},{6,7},{7,6},{8,12},{9,13},{10,... | collective-permute-start | bytes 688136 | tf_op jit(solution)/shard_map/ppermute | solution.py:106
  16.4 0.8 collective-permute-done.3
  17.1 1.6 %collective-permute-start.5 = (bf16[4,224,128]{2,1,0:T(8,128)(2,1)S(1)}, bf16[4,224,128]{2,1,0:T(8,128)(2,1)S(1)}, u32[]{:S(2)}, u32[]{:S(2)}) collective-permute-start(bf16[4,224,128]{2,1,0:T(8,128)(2,1)S(1)} %constant_dynamic-update-slice_fusion.6), channel_id=1, source_target_pairs={{0,4},{1,5},{2,3},{3,2},{4,0},{5,1},{6,7},{7,6},{8,12},{9,13},{10,... | collective-permute-start | bytes 688136 | tf_op jit(solution)/shard_map/ppermute | solution.py:106
  18.8 1.8 %collective-permute-done.4 = bf16[4,224,128]{2,1,0:T(8,128)(2,1)S(1)} collective-permute-done((bf16[4,224,128]{2,1,0:T(8,128)(2,1)S(1)}, bf16[4,224,128]{2,1,0:T(8,128)(2,1)S(1)}, u32[]{:S(2)}, u32[]{:S(2)}) %collective-permute-start.4) | collective-permute-done | bytes 229408 | tf_op jit(solution)/shard_map/ppermute | solution.py:106
  20.7 2.5 %collective-permute-done.5 = bf16[4,224,128]{2,1,0:T(8,128)(2,1)S(1)} collective-permute-done((bf16[4,224,128]{2,1,0:T(8,128)(2,1)S(1)}, bf16[4,224,128]{2,1,0:T(8,128)(2,1)S(1)}, u32[]{:S(2)}, u32[]{:S(2)}) %collective-permute-start.5) | collective-permute-done | bytes 229408 | tf_op jit(solution)/shard_map/ppermute | solution.py:106
  23.3 1.7 %collective-permute-start.6 = (bf16[8,224,128]{2,1,0:T(8,128)(2,1)S(1)}, bf16[8,224,128]{2,1,0:T(8,128)(2,1)S(1)}, u32[]{:S(2)}, u32[]{:S(2)}) collective-permute-start(bf16[8,224,128]{2,1,0:T(8,128)(2,1)S(1)} %constant_dynamic-update-slice_fusion.10.refs_2_), channel_id=1, source_target_pairs={{0,1},{1,0},{2,6},{3,7},{4,5},{5,4},{6,2},{7,3},{8,9},{9,8},{10,14... | collective-permute-start | bytes 1376264 | tf_op jit(solution)/shard_map/ppermute | solution.py:106
  25.0 2.2 %collective-permute-start.9 = (bf16[8,224,128]{2,1,0:T(8,128)(2,1)S(1)}, bf16[8,224,128]{2,1,0:T(8,128)(2,1)S(1)}, u32[]{:S(2)}, u32[]{:S(2)}) collective-permute-start(bf16[8,224,128]{2,1,0:T(8,128)(2,1)S(1)} %constant_dynamic-update-slice_fusion.8.refs_6_), channel_id=1, source_target_pairs={{0,8},{1,9},{2,10},{3,11},{4,12},{5,13},{6,14},{7,15},{8,0},{9,1},... | collective-permute-start | bytes 1376264 | tf_op jit(solution)/shard_map/ppermute | solution.py:106
  27.2 0.0 collective-permute-start.7
  27.2 0.5 collective-permute-start.10
  27.7 4.1 %collective-permute-done.6.refs_3_ = bf16[8,224,128]{2,1,0:T(8,128)(2,1)S(1)} collective-permute-done((bf16[8,224,128]{2,1,0:T(8,128)(2,1)S(1)}, bf16[8,224,128]{2,1,0:T(8,128)(2,1)S(1)}, u32[]{:S(2)}, u32[]{:S(2)}) %collective-permute-start.6) | collective-permute-done | bytes 458784 | tf_op jit(solution)/shard_map/ppermute | solution.py:106
  31.8 0.0 collective-permute-start.8
  31.8 3.9 %collective-permute-done.9.refs_7_ = bf16[8,224,128]{2,1,0:T(8,128)(2,1)S(1)} collective-permute-done((bf16[8,224,128]{2,1,0:T(8,128)(2,1)S(1)}, bf16[8,224,128]{2,1,0:T(8,128)(2,1)S(1)}, u32[]{:S(2)}, u32[]{:S(2)}) %collective-permute-start.9) | collective-permute-done | bytes 458784 | tf_op jit(solution)/shard_map/ppermute | solution.py:106
  35.7 0.0 collective-permute-start.11
  35.8 0.0 collective-permute-done.7.refs_4_
  35.8 0.0 collective-permute-done.10.refs_8_
  35.8 0.0 collective-permute-done.8.refs_5_
  35.8 1.8 %collective-permute-done.11.refs_9_ = bf16[8,224,128]{2,1,0:T(8,128)(2,1)S(1)} collective-permute-done((bf16[8,224,128]{2,1,0:T(8,128)(2,1)S(1)}, bf16[8,224,128]{2,1,0:T(8,128)(2,1)S(1)}, u32[]{:S(2)}, u32[]{:S(2)}) %collective-permute-start.11) | collective-permute-done | bytes 458784 | tf_op jit(solution)/shard_map/ppermute | solution.py:110
  37.6 0.0 copy-done
  37.6 49.3 %layer.1 = (bf16[2048,384]{1,0:T(8,128)(2,1)}, bf16[2048,384]{1,0:T(8,128)(2,1)}, f32[16,224,128]{2,1,0:T(8,128)S(1)}, bf16[16,224,128]{2,1,0:T(8,128)(2,1)S(1)}...) custom-call(s32[1]{0:T(128)} %bitcast.refs_0_, s32[32]{0:T(128)S(1)} %copy-done, ...), custom_call_target="tpu_custom_call" | custom-call | tf_op jit(solution)/shard_map/layer/pallas_call | solution.py:440
  86.8 0.1 collective-permute-start.12
  87.0 0.4 collective-permute-start.13
  87.4 2.0 %collective-permute-done.12 = bf16[16,224,128]{2,1,0:T(8,128)(2,1)S(1)} collective-permute-done((bf16[16,224,128]{2,1,0:T(8,128)(2,1)S(1)}, bf16[16,224,128]{2,1,0:T(8,128)(2,1)S(1)}, u32[]{:S(2)}, u32[]{:S(2)}) %collective-permute-start.12) | collective-permute-done | bytes 917536 | tf_op jit(solution)/shard_map/ppermute | solution.py:116
  89.3 0.2 fusion.7
  89.5 1.6 %collective-permute-start.14 = (bf16[8,224,128]{2,1,0:T(8,128)(2,1)S(1)}, bf16[8,224,128]{2,1,0:T(8,128)(2,1)S(1)}, u32[]{:S(2)}, u32[]{:S(2)}) collective-permute-start(bf16[8,224,128]{2,1,0:T(8,128)(2,1)S(1)} %get-tuple-element.51), channel_id=1, source_target_pairs={{0,1},{1,0},{2,6},{3,7},{4,5},{5,4},{6,2},{7,3},{8,9},{9,8},{10,14... | collective-permute-start | bytes 1376264 | tf_op jit(solution)/shard_map/ppermute | solution.py:127
  91.1 0.0 collective-permute-done.13
  91.1 0.2 add_convert_fusion
  91.3 1.8 %collective-permute-start.15 = (bf16[8,224,128]{2,1,0:T(8,128)(2,1)S(1)}, bf16[8,224,128]{2,1,0:T(8,128)(2,1)S(1)}, u32[]{:S(2)}, u32[]{:S(2)}) collective-permute-start(bf16[8,224,128]{2,1,0:T(8,128)(2,1)S(1)} %get-tuple-element.48), channel_id=1, source_target_pairs={{0,8},{1,9},{2,10},{3,11},{4,12},{5,13},{6,14},{7,15},{8,0},{9,1},... | collective-permute-start | bytes 1376264 | tf_op jit(solution)/shard_map/ppermute | solution.py:127
  94.4 3.6 %collective-permute-done.14 = bf16[8,224,128]{2,1,0:T(8,128)(2,1)S(1)} collective-permute-done((bf16[8,224,128]{2,1,0:T(8,128)(2,1)S(1)}, bf16[8,224,128]{2,1,0:T(8,128)(2,1)S(1)}, u32[]{:S(2)}, u32[]{:S(2)}) %collective-permute-start.14) | collective-permute-done | bytes 458784 | tf_op jit(solution)/shard_map/ppermute | solution.py:127
  98.0 0.1 fusion.8
  98.1 0.6 collective-permute-start.16
  98.8 4.7 %collective-permute-done.15 = bf16[8,224,128]{2,1,0:T(8,128)(2,1)S(1)} collective-permute-done((bf16[8,224,128]{2,1,0:T(8,128)(2,1)S(1)}, bf16[8,224,128]{2,1,0:T(8,128)(2,1)S(1)}, u32[]{:S(2)}, u32[]{:S(2)}) %collective-permute-start.15) | collective-permute-done | bytes 458784 | tf_op jit(solution)/shard_map/ppermute | solution.py:127
  103.4 0.1 add_convert_fusion.2
  103.5 0.7 collective-permute-start.17
  104.3 0.0 collective-permute-done.16
  104.3 0.1 fusion.9
  104.4 0.0 copy-start.1
  104.4 0.0 copy-start.2
  104.4 0.0 copy-start.3
  104.4 1.8 %collective-permute-start.18 = (bf16[2,224,128]{2,1,0:T(8,128)(2,1)S(1)}, bf16[2,224,128]{2,1,0:T(8,128)(2,1)S(1)}, u32[]{:S(2)}, u32[]{:S(2)}) collective-permute-start(bf16[2,224,128]{2,1,0:T(8,128)(2,1)S(1)} %get-tuple-element.59), channel_id=1, source_target_pairs={{0,8},{1,9},{2,10},{3,11},{4,12},{5,13},{6,14},{7,15},{8,0},{9,1},... | collective-permute-start | bytes 344072 | tf_op jit(solution)/shard_map/ppermute | solution.py:127
  106.2 3.4 %collective-permute-done.17 = bf16[4,224,128]{2,1,0:T(8,128)(2,1)S(1)} collective-permute-done((bf16[4,224,128]{2,1,0:T(8,128)(2,1)S(1)}, bf16[4,224,128]{2,1,0:T(8,128)(2,1)S(1)}, u32[]{:S(2)}, u32[]{:S(2)}) %collective-permute-start.17) | collective-permute-done | bytes 229408 | tf_op jit(solution)/shard_map/ppermute | solution.py:127
  109.6 0.1 add_convert_fusion.4
  109.7 1.6 %collective-permute-start.20 = (bf16[2,224,128]{2,1,0:T(8,128)(2,1)S(1)}, bf16[2,224,128]{2,1,0:T(8,128)(2,1)S(1)}, u32[]{:S(2)}, u32[]{:S(2)}) collective-permute-start(bf16[2,224,128]{2,1,0:T(8,128)(2,1)S(1)} %get-tuple-element.56), channel_id=1, source_target_pairs={{0,1},{1,0},{2,6},{3,7},{4,5},{5,4},{6,2},{7,3},{8,9},{9,8},{10,14... | collective-permute-start | bytes 344072 | tf_op jit(solution)/shard_map/ppermute | solution.py:127
  111.3 0.0 collective-permute-done.18
  111.3 3.5 %collective-permute-start.19 = (bf16[1,224,128]{2,1,0:T(8,128)(2,1)S(1)}, bf16[1,224,128]{2,1,0:T(8,128)(2,1)S(1)}, u32[]{:S(2)}, u32[]{:S(2)}) collective-permute-start(bf16[1,224,128]{2,1,0:T(8,128)(2,1)S(1)} %add_convert_fusion.7), channel_id=1, source_target_pairs={{0,16},{1,17},{2,18},{3,19},{4,20},{5,21},{6,22},{7,23},{8,24},{9,... | collective-permute-start | bytes 172040 | tf_op jit(solution)/shard_map/ppermute | solution.py:127
  114.8 0.0 collective-permute-done.20
  114.8 3.2 %collective-permute-start.21 = (bf16[1,224,128]{2,1,0:T(8,128)(2,1)S(1)}, bf16[1,224,128]{2,1,0:T(8,128)(2,1)S(1)}, u32[]{:S(2)}, u32[]{:S(2)}) collective-permute-start(bf16[1,224,128]{2,1,0:T(8,128)(2,1)S(1)} %add_convert_fusion.6), channel_id=1, source_target_pairs={{0,16},{1,17},{2,18},{3,19},{4,20},{5,21},{6,22},{7,23},{8,24},{9,... | collective-permute-start | bytes 172040 | tf_op jit(solution)/shard_map/ppermute | solution.py:127
  118.1 0.0 collective-permute-done.19
  118.1 2.1 %collective-permute-done.21 = bf16[1,224,128]{2,1,0:T(8,128)(2,1)S(1)} collective-permute-done((bf16[1,224,128]{2,1,0:T(8,128)(2,1)S(1)}, bf16[1,224,128]{2,1,0:T(8,128)(2,1)S(1)}, u32[]{:S(2)}, u32[]{:S(2)}) %collective-permute-start.21) | collective-permute-done | bytes 57376 | tf_op jit(solution)/shard_map/ppermute | solution.py:127
  120.3 0.0 copy-done.1
  120.3 0.0 copy-done.2
  120.3 0.0 copy-done.3
  120.3 1.2 fusion.5
  (19 shorter events, 0.4 us)
Async XLA Ops:
  1.6 35.9 %copy-start = (s32[32]{0:T(128)S(1)}, s32[32]{0:T(128)}, u32[]{:S(2)}) copy-start(s32[32]{0:T(128)} %refs_1_.1) | copy-start | bytes 388
  2.8 6.9 %collective-permute-start = (bf16[1,224,128]{2,1,0:T(8,128)(2,1)S(1)}, bf16[1,224,128]{2,1,0:T(8,128)(2,1)S(1)}, u32[]{:S(2)}, u32[]{:S(2)}) collective-permute-start(bf16[1,224,128]{2,1,0:T(8,128)(2,1)S(1)} %get-tuple-element.60), channel_id=1, source_target_pairs={{0,16},{1,17},{2,18},{3,19},{4,20},{5,21},{6,22},{7,23},{8,24},{9,... | collective-permute-start | bytes 172040 | tf_op jit(solution)/shard_map/ppermute | solution.py:106
  6.9 5.3 %collective-permute-start.1 = (bf16[1,224,128]{2,1,0:T(8,128)(2,1)S(1)}, bf16[1,224,128]{2,1,0:T(8,128)(2,1)S(1)}, u32[]{:S(2)}, u32[]{:S(2)}) collective-permute-start(bf16[1,224,128]{2,1,0:T(8,128)(2,1)S(1)} %get-tuple-element.26), channel_id=1, source_target_pairs={{0,16},{1,17},{2,18},{3,19},{4,20},{5,21},{6,22},{7,23},{8,24},{9,... | collective-permute-start | bytes 172040 | tf_op jit(solution)/shard_map/ppermute | solution.py:106
  9.7 4.9 %collective-permute-start.2 = (bf16[2,224,128]{2,1,0:T(8,128)(2,1)S(1)}, bf16[2,224,128]{2,1,0:T(8,128)(2,1)S(1)}, u32[]{:S(2)}, u32[]{:S(2)}) collective-permute-start(bf16[2,224,128]{2,1,0:T(8,128)(2,1)S(1)} %constant_dynamic-update-slice_fusion), channel_id=1, source_target_pairs={{0,1},{1,0},{2,6},{3,7},{4,5},{5,4},{6,2},{7,3},{8,9},{9,8},{10,14... | collective-permute-start | bytes 344072 | tf_op jit(solution)/shard_map/ppermute | solution.py:106
  12.3 4.9 %collective-permute-start.3 = (bf16[2,224,128]{2,1,0:T(8,128)(2,1)S(1)}, bf16[2,224,128]{2,1,0:T(8,128)(2,1)S(1)}, u32[]{:S(2)}, u32[]{:S(2)}) collective-permute-start(bf16[2,224,128]{2,1,0:T(8,128)(2,1)S(1)} %constant_dynamic-update-slice_fusion.2), channel_id=1, source_target_pairs={{0,8},{1,9},{2,10},{3,11},{4,12},{5,13},{6,14},{7,15},{8,0},{9,1},... | collective-permute-start | bytes 344072 | tf_op jit(solution)/shard_map/ppermute | solution.py:106
  14.6 6.1 %collective-permute-start.4 = (bf16[4,224,128]{2,1,0:T(8,128)(2,1)S(1)}, bf16[4,224,128]{2,1,0:T(8,128)(2,1)S(1)}, u32[]{:S(2)}, u32[]{:S(2)}) collective-permute-start(bf16[4,224,128]{2,1,0:T(8,128)(2,1)S(1)} %constant_dynamic-update-slice_fusion.4), channel_id=1, source_target_pairs={{0,4},{1,5},{2,3},{3,2},{4,0},{5,1},{6,7},{7,6},{8,12},{9,13},{10,... | collective-permute-start | bytes 688136 | tf_op jit(solution)/shard_map/ppermute | solution.py:106
  17.1 6.1 %collective-permute-start.5 = (bf16[4,224,128]{2,1,0:T(8,128)(2,1)S(1)}, bf16[4,224,128]{2,1,0:T(8,128)(2,1)S(1)}, u32[]{:S(2)}, u32[]{:S(2)}) collective-permute-start(bf16[4,224,128]{2,1,0:T(8,128)(2,1)S(1)} %constant_dynamic-update-slice_fusion.6), channel_id=1, source_target_pairs={{0,4},{1,5},{2,3},{3,2},{4,0},{5,1},{6,7},{7,6},{8,12},{9,13},{10,... | collective-permute-start | bytes 688136 | tf_op jit(solution)/shard_map/ppermute | solution.py:106
  23.3 8.5 %collective-permute-start.6 = (bf16[8,224,128]{2,1,0:T(8,128)(2,1)S(1)}, bf16[8,224,128]{2,1,0:T(8,128)(2,1)S(1)}, u32[]{:S(2)}, u32[]{:S(2)}) collective-permute-start(bf16[8,224,128]{2,1,0:T(8,128)(2,1)S(1)} %constant_dynamic-update-slice_fusion.10.refs_2_), channel_id=1, source_target_pairs={{0,1},{1,0},{2,6},{3,7},{4,5},{5,4},{6,2},{7,3},{8,9},{9,8},{10,14... | collective-permute-start | bytes 1376264 | tf_op jit(solution)/shard_map/ppermute | solution.py:106
  25.0 10.8 %collective-permute-start.9 = (bf16[8,224,128]{2,1,0:T(8,128)(2,1)S(1)}, bf16[8,224,128]{2,1,0:T(8,128)(2,1)S(1)}, u32[]{:S(2)}, u32[]{:S(2)}) collective-permute-start(bf16[8,224,128]{2,1,0:T(8,128)(2,1)S(1)} %constant_dynamic-update-slice_fusion.8.refs_6_), channel_id=1, source_target_pairs={{0,8},{1,9},{2,10},{3,11},{4,12},{5,13},{6,14},{7,15},{8,0},{9,1},... | collective-permute-start | bytes 1376264 | tf_op jit(solution)/shard_map/ppermute | solution.py:106
  27.2 8.6 %collective-permute-start.7 = (bf16[8,224,128]{2,1,0:T(8,128)(2,1)S(1)}, bf16[8,224,128]{2,1,0:T(8,128)(2,1)S(1)}, u32[]{:S(2)}, u32[]{:S(2)}) collective-permute-start(bf16[8,224,128]{2,1,0:T(8,128)(2,1)S(1)} %constant_dynamic-update-slice_fusion.10.refs_2_), channel_id=1, source_target_pairs={{0,2},{1,3},{2,0},{3,1},{4,6},{5,7},{6,4},{7,5},{8,10},{9,11},{10,... | collective-permute-start | bytes 1376264 | tf_op jit(solution)/shard_map/ppermute | solution.py:110
  27.2 8.6 %collective-permute-start.10 = (bf16[8,224,128]{2,1,0:T(8,128)(2,1)S(1)}, bf16[8,224,128]{2,1,0:T(8,128)(2,1)S(1)}, u32[]{:S(2)}, u32[]{:S(2)}) collective-permute-start(bf16[8,224,128]{2,1,0:T(8,128)(2,1)S(1)} %constant_dynamic-update-slice_fusion.8.refs_6_), channel_id=1, source_target_pairs={{0,2},{1,3},{2,0},{3,1},{4,6},{5,7},{6,4},{7,5},{8,10},{9,11},{10,... | collective-permute-start | bytes 1376264 | tf_op jit(solution)/shard_map/ppermute | solution.py:110
  31.8 3.9 %collective-permute-start.8 = (bf16[8,224,128]{2,1,0:T(8,128)(2,1)S(1)}, bf16[8,224,128]{2,1,0:T(8,128)(2,1)S(1)}, u32[]{:S(2)}, u32[]{:S(2)}) collective-permute-start(bf16[8,224,128]{2,1,0:T(8,128)(2,1)S(1)} %collective-permute-done.6.refs_3_), channel_id=1, source_target_pairs={{0,2},{1,3},{2,0},{3,1},{4,6},{5,7},{6,4},{7,5},{8,10},{9,11},{10,... | collective-permute-start | bytes 1376264 | tf_op jit(solution)/shard_map/ppermute | solution.py:110
  35.7 1.8 %collective-permute-start.11 = (bf16[8,224,128]{2,1,0:T(8,128)(2,1)S(1)}, bf16[8,224,128]{2,1,0:T(8,128)(2,1)S(1)}, u32[]{:S(2)}, u32[]{:S(2)}) collective-permute-start(bf16[8,224,128]{2,1,0:T(8,128)(2,1)S(1)} %collective-permute-done.9.refs_7_), channel_id=1, source_target_pairs={{0,2},{1,3},{2,0},{3,1},{4,6},{5,7},{6,4},{7,5},{8,10},{9,11},{10,... | collective-permute-start | bytes 1376264 | tf_op jit(solution)/shard_map/ppermute | solution.py:110
  86.8 2.5 %collective-permute-start.12 = (bf16[16,224,128]{2,1,0:T(8,128)(2,1)S(1)}, bf16[16,224,128]{2,1,0:T(8,128)(2,1)S(1)}, u32[]{:S(2)}, u32[]{:S(2)}) collective-permute-start(bf16[16,224,128]{2,1,0:T(8,128)(2,1)S(1)} %get-tuple-element.35), channel_id=1, source_target_pairs={{0,2},{1,3},{2,0},{3,1},{4,6},{5,7},{6,4},{7,5},{8,10},{9,11},{10,... | collective-permute-start | bytes 2752520 | tf_op jit(solution)/shard_map/ppermute | solution.py:116
  87.0 4.1 %collective-permute-start.13 = (bf16[16,224,128]{2,1,0:T(8,128)(2,1)S(1)}, bf16[16,224,128]{2,1,0:T(8,128)(2,1)S(1)}, u32[]{:S(2)}, u32[]{:S(2)}) collective-permute-start(bf16[16,224,128]{2,1,0:T(8,128)(2,1)S(1)} %get-tuple-element.37), channel_id=1, source_target_pairs={{0,2},{1,3},{2,0},{3,1},{4,6},{5,7},{6,4},{7,5},{8,10},{9,11},{10,... | collective-permute-start | bytes 2752520 | tf_op jit(solution)/shard_map/ppermute | solution.py:116
  89.5 8.5 %collective-permute-start.14 = (bf16[8,224,128]{2,1,0:T(8,128)(2,1)S(1)}, bf16[8,224,128]{2,1,0:T(8,128)(2,1)S(1)}, u32[]{:S(2)}, u32[]{:S(2)}) collective-permute-start(bf16[8,224,128]{2,1,0:T(8,128)(2,1)S(1)} %get-tuple-element.51), channel_id=1, source_target_pairs={{0,1},{1,0},{2,6},{3,7},{4,5},{5,4},{6,2},{7,3},{8,9},{9,8},{10,14... | collective-permute-start | bytes 1376264 | tf_op jit(solution)/shard_map/ppermute | solution.py:127
  91.3 12.2 %collective-permute-start.15 = (bf16[8,224,128]{2,1,0:T(8,128)(2,1)S(1)}, bf16[8,224,128]{2,1,0:T(8,128)(2,1)S(1)}, u32[]{:S(2)}, u32[]{:S(2)}) collective-permute-start(bf16[8,224,128]{2,1,0:T(8,128)(2,1)S(1)} %get-tuple-element.48), channel_id=1, source_target_pairs={{0,8},{1,9},{2,10},{3,11},{4,12},{5,13},{6,14},{7,15},{8,0},{9,1},... | collective-permute-start | bytes 1376264 | tf_op jit(solution)/shard_map/ppermute | solution.py:127
  98.1 6.1 %collective-permute-start.16 = (bf16[4,224,128]{2,1,0:T(8,128)(2,1)S(1)}, bf16[4,224,128]{2,1,0:T(8,128)(2,1)S(1)}, u32[]{:S(2)}, u32[]{:S(2)}) collective-permute-start(bf16[4,224,128]{2,1,0:T(8,128)(2,1)S(1)} %get-tuple-element.55), channel_id=1, source_target_pairs={{0,4},{1,5},{2,3},{3,2},{4,0},{5,1},{6,7},{7,6},{8,12},{9,13},{10,... | collective-permute-start | bytes 688136 | tf_op jit(solution)/shard_map/ppermute | solution.py:127
  103.5 6.1 %collective-permute-start.17 = (bf16[4,224,128]{2,1,0:T(8,128)(2,1)S(1)}, bf16[4,224,128]{2,1,0:T(8,128)(2,1)S(1)}, u32[]{:S(2)}, u32[]{:S(2)}) collective-permute-start(bf16[4,224,128]{2,1,0:T(8,128)(2,1)S(1)} %get-tuple-element.52), channel_id=1, source_target_pairs={{0,4},{1,5},{2,3},{3,2},{4,0},{5,1},{6,7},{7,6},{8,12},{9,13},{10,... | collective-permute-start | bytes 688136 | tf_op jit(solution)/shard_map/ppermute | solution.py:127
  104.4 15.9 %copy-start.1 = (f32[55416]{0:T(1024)S(1)}, f32[55416]{0:T(1024)}, u32[]{:S(2)}) copy-start(f32[55416]{0:T(1024)} %param.11) | copy-start | bytes 664996
  104.4 15.9 %copy-start.2 = (f32[55416]{0:T(1024)S(1)}, f32[55416]{0:T(1024)}, u32[]{:S(2)}) copy-start(f32[55416]{0:T(1024)} %param.13) | copy-start | bytes 664996
  104.4 15.9 %copy-start.3 = (f32[55416]{0:T(1024)S(1)}, f32[55416]{0:T(1024)}, u32[]{:S(2)}) copy-start(f32[55416]{0:T(1024)} %param.12) | copy-start | bytes 664996
  104.4 6.9 %collective-permute-start.18 = (bf16[2,224,128]{2,1,0:T(8,128)(2,1)S(1)}, bf16[2,224,128]{2,1,0:T(8,128)(2,1)S(1)}, u32[]{:S(2)}, u32[]{:S(2)}) collective-permute-start(bf16[2,224,128]{2,1,0:T(8,128)(2,1)S(1)} %get-tuple-element.59), channel_id=1, source_target_pairs={{0,8},{1,9},{2,10},{3,11},{4,12},{5,13},{6,14},{7,15},{8,0},{9,1},... | collective-permute-start | bytes 344072 | tf_op jit(solution)/shard_map/ppermute | solution.py:127
  109.7 5.1 %collective-permute-start.20 = (bf16[2,224,128]{2,1,0:T(8,128)(2,1)S(1)}, bf16[2,224,128]{2,1,0:T(8,128)(2,1)S(1)}, u32[]{:S(2)}, u32[]{:S(2)}) collective-permute-start(bf16[2,224,128]{2,1,0:T(8,128)(2,1)S(1)} %get-tuple-element.56), channel_id=1, source_target_pairs={{0,1},{1,0},{2,6},{3,7},{4,5},{5,4},{6,2},{7,3},{8,9},{9,8},{10,14... | collective-permute-start | bytes 344072 | tf_op jit(solution)/shard_map/ppermute | solution.py:127
  111.3 6.7 %collective-permute-start.19 = (bf16[1,224,128]{2,1,0:T(8,128)(2,1)S(1)}, bf16[1,224,128]{2,1,0:T(8,128)(2,1)S(1)}, u32[]{:S(2)}, u32[]{:S(2)}) collective-permute-start(bf16[1,224,128]{2,1,0:T(8,128)(2,1)S(1)} %add_convert_fusion.7), channel_id=1, source_target_pairs={{0,16},{1,17},{2,18},{3,19},{4,20},{5,21},{6,22},{7,23},{8,24},{9,... | collective-permute-start | bytes 172040 | tf_op jit(solution)/shard_map/ppermute | solution.py:127
  114.8 5.4 %collective-permute-start.21 = (bf16[1,224,128]{2,1,0:T(8,128)(2,1)S(1)}, bf16[1,224,128]{2,1,0:T(8,128)(2,1)S(1)}, u32[]{:S(2)}, u32[]{:S(2)}) collective-permute-start(bf16[1,224,128]{2,1,0:T(8,128)(2,1)S(1)} %add_convert_fusion.6), channel_id=1, source_target_pairs={{0,16},{1,17},{2,18},{3,19},{4,20},{5,21},{6,22},{7,23},{8,24},{9,... | collective-permute-start | bytes 172040 | tf_op jit(solution)/shard_map/ppermute | solution.py:127

commit v3 on v2

--- a/solution.py
+++ b/solution.py
@@ -72,13 +72,10 @@
 
 def exchange_flows(wide, narrow):
     bits = chip_bits(wide * narrow, narrow)
-    upper, (first, second) = bits[:-2], bits[-2:]
+    top, middle, (first, second) = bits[:1], bits[1:-2], bits[-2:]
     orders = [
-        (upper + [first, second], upper + [second, first]),
-        (
-            upper[:1] + [second, first] + upper[1:],
-            upper[:1] + [first, second] + upper[1:],
-        ),
+        (top + [second, first] + middle, [first] + top + middle + [second]),
+        (top + middle + [first, second], [second] + middle + top + [first]),
     ]
     return [Flow(list(zip(*order)), wide * narrow, narrow) for order in orders]
 

time: 122 us -> 119 us (0.975)
  waiting for transfers between devices: 35 us -> 30.7 us
  starting transfers between devices: 30.7 us -> 32.2 us
    ppermute x8, waiting for transfers between devices: 13.8 us -> 11.5 us  [scatter_chunks(): parts[turn].append(lax.ppermute(last, AXES, flow.swaps[index]))]
    ppermute x8, waiting for transfers between devices: 17.4 us -> 15.5 us  [gather_chunks(): taken[turn] = lax.ppermute(last, AXES, flows[turn].swaps[index])]
    ppermute x8, starting transfers between devices: 14.8 us -> 16.5 us  [scatter_chunks(): parts[turn].append(lax.ppermute(last, AXES, flow.swaps[index]))]
  transfers between devices with their start and end apart: 22 -> 22, of which waited for: 14 -> 15; matrix products, arithmetic and copies ran while one was open for 1% -> 1% of each run, Pallas kernels for 0% -> 0%
where the time goes in v3:
time: 119 us
  Pallas kernels  49.2 us (41%)
  starting transfers between devices  32.2 us (27%)
  waiting for transfers between devices  30.7 us (26%)
  other arithmetic  3 us (3%)
  between operations  2.18 us (2%)
  local copies, waits for them, and re-layouts  1.37 us (1%)
    pallas_call x1, Pallas kernels, layer(): pl.pallas_call(functools.partial(layer_kernel, flows, shard), name='layer...  49.2 us
    ppermute x8, starting transfers between devices, scatter_chunks(): parts[turn].append(lax.ppermute(last, AXES, flow.swaps[index]))  16.5 us
    ppermute x8, waiting for transfers between devices, gather_chunks(): taken[turn] = lax.ppermute(last, AXES, flows[turn].swaps[index])  15.5 us
    ppermute x8, starting transfers between devices, gather_chunks(): taken[turn] = lax.ppermute(last, AXES, flows[turn].swaps[index])  14.7 us
    ppermute x8, waiting for transfers between devices, scatter_chunks(): parts[turn].append(lax.ppermute(last, AXES, flow.swaps[index]))  11.5 us
  transfers between devices with their start and end apart: 22, of which 15 were waited for; matrix products, arithmetic and copies ran while one was open for 1% of the time, Pallas kernels for 0%

profile of v3, /device:TPU:0, one launch (start us, length us, event | category | flops | bytes accessed | tf_op | source)
XLA Modules:
  0.0 118.6 jit_solution(13154670939243288064)
XLA Ops:
  0.6 1.0 convert_element_type.142
  1.6 0.0 copy-start
  1.6 1.1 dynamic_update_slice.3
  2.8 4.1 %collective-permute-start = (bf16[1,224,128]{2,1,0:T(8,128)(2,1)S(1)}, bf16[1,224,128]{2,1,0:T(8,128)(2,1)S(1)}, u32[]{:S(2)}, u32[]{:S(2)}) collective-permute-start(bf16[1,224,128]{2,1,0:T(8,128)(2,1)S(1)} %get-tuple-element.60), channel_id=1, source_target_pairs={{0,16},{1,17},{2,3},{3,2},{4,20},{5,21},{6,7},{7,6},{8,24},{9,25},... | collective-permute-start | bytes 172040 | tf_op jit(solution)/shard_map/ppermute | solution.py:103
  6.9 0.1 collective-permute-start.1
  7.0 2.1 %collective-permute-done = bf16[1,224,128]{2,1,0:T(8,128)(2,1)S(1)} collective-permute-done((bf16[1,224,128]{2,1,0:T(8,128)(2,1)S(1)}, bf16[1,224,128]{2,1,0:T(8,128)(2,1)S(1)}, u32[]{:S(2)}, u32[]{:S(2)}) %collective-permute-start) | collective-permute-done | bytes 57376 | tf_op jit(solution)/shard_map/ppermute | solution.py:103
  9.1 2.3 %collective-permute-start.2 = (bf16[2,224,128]{2,1,0:T(8,128)(2,1)S(1)}, bf16[2,224,128]{2,1,0:T(8,128)(2,1)S(1)}, u32[]{:S(2)}, u32[]{:S(2)}) collective-permute-start(bf16[2,224,128]{2,1,0:T(8,128)(2,1)S(1)} %constant_dynamic-update-slice_fusion), channel_id=1, source_target_pairs={{0,8},{1,9},{2,10},{3,11},{4,12},{5,13},{6,14},{7,15},{8,0},{9,1},... | collective-permute-start | bytes 344072 | tf_op jit(solution)/shard_map/ppermute | solution.py:103
  11.4 0.6 collective-permute-done.1
  12.0 1.6 %collective-permute-start.3 = (bf16[2,224,128]{2,1,0:T(8,128)(2,1)S(1)}, bf16[2,224,128]{2,1,0:T(8,128)(2,1)S(1)}, u32[]{:S(2)}, u32[]{:S(2)}) collective-permute-start(bf16[2,224,128]{2,1,0:T(8,128)(2,1)S(1)} %constant_dynamic-update-slice_fusion.2), channel_id=1, source_target_pairs={{0,1},{1,0},{2,18},{3,19},{4,5},{5,4},{6,22},{7,23},{8,9},{9,8},{1... | collective-permute-start | bytes 344072 | tf_op jit(solution)/shard_map/ppermute | solution.py:103
  13.6 1.1 collective-permute-done.2
  14.7 1.6 %collective-permute-start.4 = (bf16[4,224,128]{2,1,0:T(8,128)(2,1)S(1)}, bf16[4,224,128]{2,1,0:T(8,128)(2,1)S(1)}, u32[]{:S(2)}, u32[]{:S(2)}) collective-permute-start(bf16[4,224,128]{2,1,0:T(8,128)(2,1)S(1)} %constant_dynamic-update-slice_fusion.4), channel_id=1, source_target_pairs={{0,4},{1,5},{2,18},{3,19},{4,0},{5,1},{6,22},{7,23},{8,12},{9,13},... | collective-permute-start | bytes 688136 | tf_op jit(solution)/shard_map/ppermute | solution.py:103
  16.3 0.6 collective-permute-done.3
  16.9 1.6 %collective-permute-start.5 = (bf16[4,224,128]{2,1,0:T(8,128)(2,1)S(1)}, bf16[4,224,128]{2,1,0:T(8,128)(2,1)S(1)}, u32[]{:S(2)}, u32[]{:S(2)}) collective-permute-start(bf16[4,224,128]{2,1,0:T(8,128)(2,1)S(1)} %constant_dynamic-update-slice_fusion.6), channel_id=1, source_target_pairs={{0,4},{1,5},{2,10},{3,11},{4,0},{5,1},{6,14},{7,15},{8,12},{9,13},... | collective-permute-start | bytes 688136 | tf_op jit(solution)/shard_map/ppermute | solution.py:103
  18.5 2.3 %collective-permute-done.4 = bf16[4,224,128]{2,1,0:T(8,128)(2,1)S(1)} collective-permute-done((bf16[4,224,128]{2,1,0:T(8,128)(2,1)S(1)}, bf16[4,224,128]{2,1,0:T(8,128)(2,1)S(1)}, u32[]{:S(2)}, u32[]{:S(2)}) %collective-permute-start.4) | collective-permute-done | bytes 229408 | tf_op jit(solution)/shard_map/ppermute | solution.py:103
  20.8 2.4 %collective-permute-done.5 = bf16[4,224,128]{2,1,0:T(8,128)(2,1)S(1)} collective-permute-done((bf16[4,224,128]{2,1,0:T(8,128)(2,1)S(1)}, bf16[4,224,128]{2,1,0:T(8,128)(2,1)S(1)}, u32[]{:S(2)}, u32[]{:S(2)}) %collective-permute-start.5) | collective-permute-done | bytes 229408 | tf_op jit(solution)/shard_map/ppermute | solution.py:103
  23.3 1.9 %collective-permute-start.6 = (bf16[8,224,128]{2,1,0:T(8,128)(2,1)S(1)}, bf16[8,224,128]{2,1,0:T(8,128)(2,1)S(1)}, u32[]{:S(2)}, u32[]{:S(2)}) collective-permute-start(bf16[8,224,128]{2,1,0:T(8,128)(2,1)S(1)} %constant_dynamic-update-slice_fusion.10.refs_2_), channel_id=1, source_target_pairs={{0,8},{1,9},{2,3},{3,2},{4,12},{5,13},{6,7},{7,6},{8,0},{9,1},{10,... | collective-permute-start | bytes 1376264 | tf_op jit(solution)/shard_map/ppermute | solution.py:103
  25.2 1.5 %collective-permute-start.9 = (bf16[8,224,128]{2,1,0:T(8,128)(2,1)S(1)}, bf16[8,224,128]{2,1,0:T(8,128)(2,1)S(1)}, u32[]{:S(2)}, u32[]{:S(2)}) collective-permute-start(bf16[8,224,128]{2,1,0:T(8,128)(2,1)S(1)} %constant_dynamic-update-slice_fusion.8.refs_6_), channel_id=1, source_target_pairs={{0,1},{1,0},{2,6},{3,7},{4,5},{5,4},{6,2},{7,3},{8,9},{9,8},{10,14... | collective-permute-start | bytes 1376264 | tf_op jit(solution)/shard_map/ppermute | solution.py:103
  26.7 0.0 collective-permute-start.7
  26.7 0.5 collective-permute-start.10
  27.2 4.6 %collective-permute-done.6.refs_3_ = bf16[8,224,128]{2,1,0:T(8,128)(2,1)S(1)} collective-permute-done((bf16[8,224,128]{2,1,0:T(8,128)(2,1)S(1)}, bf16[8,224,128]{2,1,0:T(8,128)(2,1)S(1)}, u32[]{:S(2)}, u32[]{:S(2)}) %collective-permute-start.6) | collective-permute-done | bytes 458784 | tf_op jit(solution)/shard_map/ppermute | solution.py:103
  31.8 0.0 collective-permute-start.8
  31.8 1.9 %collective-permute-done.9.refs_7_ = bf16[8,224,128]{2,1,0:T(8,128)(2,1)S(1)} collective-permute-done((bf16[8,224,128]{2,1,0:T(8,128)(2,1)S(1)}, bf16[8,224,128]{2,1,0:T(8,128)(2,1)S(1)}, u32[]{:S(2)}, u32[]{:S(2)}) %collective-permute-start.9) | collective-permute-done | bytes 458784 | tf_op jit(solution)/shard_map/ppermute | solution.py:103
  33.7 0.0 collective-permute-start.11
  33.7 0.0 collective-permute-done.7.refs_4_
  33.7 0.0 collective-permute-done.10.refs_8_
  33.7 0.0 collective-permute-done.8.refs_5_
  33.7 1.8 %collective-permute-done.11.refs_9_ = bf16[8,224,128]{2,1,0:T(8,128)(2,1)S(1)} collective-permute-done((bf16[8,224,128]{2,1,0:T(8,128)(2,1)S(1)}, bf16[8,224,128]{2,1,0:T(8,128)(2,1)S(1)}, u32[]{:S(2)}, u32[]{:S(2)}) %collective-permute-start.11) | collective-permute-done | bytes 458784 | tf_op jit(solution)/shard_map/ppermute | solution.py:107
  35.5 0.0 copy-done
  35.5 49.2 %layer.1 = (bf16[2048,384]{1,0:T(8,128)(2,1)}, bf16[2048,384]{1,0:T(8,128)(2,1)}, f32[16,224,128]{2,1,0:T(8,128)S(1)}, bf16[16,224,128]{2,1,0:T(8,128)(2,1)S(1)}...) custom-call(s32[1]{0:T(128)} %bitcast.refs_0_, s32[32]{0:T(128)S(1)} %copy-done, ...), custom_call_target="tpu_custom_call" | custom-call | tf_op jit(solution)/shard_map/layer/pallas_call | solution.py:437
  84.7 0.1 collective-permute-start.12
  84.9 0.4 collective-permute-start.13
  85.2 2.0 %collective-permute-done.12 = bf16[16,224,128]{2,1,0:T(8,128)(2,1)S(1)} collective-permute-done((bf16[16,224,128]{2,1,0:T(8,128)(2,1)S(1)}, bf16[16,224,128]{2,1,0:T(8,128)(2,1)S(1)}, u32[]{:S(2)}, u32[]{:S(2)}) %collective-permute-start.12) | collective-permute-done | bytes 917536 | tf_op jit(solution)/shard_map/ppermute | solution.py:113
  87.2 0.2 fusion.7
  87.4 1.2 %collective-permute-start.14 = (bf16[8,224,128]{2,1,0:T(8,128)(2,1)S(1)}, bf16[8,224,128]{2,1,0:T(8,128)(2,1)S(1)}, u32[]{:S(2)}, u32[]{:S(2)}) collective-permute-start(bf16[8,224,128]{2,1,0:T(8,128)(2,1)S(1)} %get-tuple-element.51), channel_id=1, source_target_pairs={{0,8},{1,9},{2,3},{3,2},{4,12},{5,13},{6,7},{7,6},{8,0},{9,1},{10,... | collective-permute-start | bytes 1376264 | tf_op jit(solution)/shard_map/ppermute | solution.py:124
  88.6 0.0 collective-permute-done.13
  88.6 0.2 add_convert_fusion
  88.8 1.8 %collective-permute-start.15 = (bf16[8,224,128]{2,1,0:T(8,128)(2,1)S(1)}, bf16[8,224,128]{2,1,0:T(8,128)(2,1)S(1)}, u32[]{:S(2)}, u32[]{:S(2)}) collective-permute-start(bf16[8,224,128]{2,1,0:T(8,128)(2,1)S(1)} %get-tuple-element.48), channel_id=1, source_target_pairs={{0,1},{1,0},{2,6},{3,7},{4,5},{5,4},{6,2},{7,3},{8,9},{9,8},{10,14... | collective-permute-start | bytes 1376264 | tf_op jit(solution)/shard_map/ppermute | solution.py:124
  91.9 4.0 %collective-permute-done.14 = bf16[8,224,128]{2,1,0:T(8,128)(2,1)S(1)} collective-permute-done((bf16[8,224,128]{2,1,0:T(8,128)(2,1)S(1)}, bf16[8,224,128]{2,1,0:T(8,128)(2,1)S(1)}, u32[]{:S(2)}, u32[]{:S(2)}) %collective-permute-start.14) | collective-permute-done | bytes 458784 | tf_op jit(solution)/shard_map/ppermute | solution.py:124
  95.9 0.1 fusion.8
  96.0 1.5 %collective-permute-start.16 = (bf16[4,224,128]{2,1,0:T(8,128)(2,1)S(1)}, bf16[4,224,128]{2,1,0:T(8,128)(2,1)S(1)}, u32[]{:S(2)}, u32[]{:S(2)}) collective-permute-start(bf16[4,224,128]{2,1,0:T(8,128)(2,1)S(1)} %get-tuple-element.55), channel_id=1, source_target_pairs={{0,4},{1,5},{2,10},{3,11},{4,0},{5,1},{6,14},{7,15},{8,12},{9,13},... | collective-permute-start | bytes 688136 | tf_op jit(solution)/shard_map/ppermute | solution.py:124
  97.5 2.5 %collective-permute-done.15 = bf16[8,224,128]{2,1,0:T(8,128)(2,1)S(1)} collective-permute-done((bf16[8,224,128]{2,1,0:T(8,128)(2,1)S(1)}, bf16[8,224,128]{2,1,0:T(8,128)(2,1)S(1)}, u32[]{:S(2)}, u32[]{:S(2)}) %collective-permute-start.15) | collective-permute-done | bytes 458784 | tf_op jit(solution)/shard_map/ppermute | solution.py:124
  100.0 0.1 add_convert_fusion.2
  100.1 1.5 %collective-permute-start.17 = (bf16[4,224,128]{2,1,0:T(8,128)(2,1)S(1)}, bf16[4,224,128]{2,1,0:T(8,128)(2,1)S(1)}, u32[]{:S(2)}, u32[]{:S(2)}) collective-permute-start(bf16[4,224,128]{2,1,0:T(8,128)(2,1)S(1)} %get-tuple-element.52), channel_id=1, source_target_pairs={{0,4},{1,5},{2,18},{3,19},{4,0},{5,1},{6,22},{7,23},{8,12},{9,13},... | collective-permute-start | bytes 688136 | tf_op jit(solution)/shard_map/ppermute | solution.py:124
  101.6 0.5 collective-permute-done.16
  102.1 0.1 fusion.9
  102.2 0.0 copy-start.1
  102.2 0.0 copy-start.2
  102.2 0.0 copy-start.3
  102.2 1.6 %collective-permute-start.18 = (bf16[2,224,128]{2,1,0:T(8,128)(2,1)S(1)}, bf16[2,224,128]{2,1,0:T(8,128)(2,1)S(1)}, u32[]{:S(2)}, u32[]{:S(2)}) collective-permute-start(bf16[2,224,128]{2,1,0:T(8,128)(2,1)S(1)} %get-tuple-element.59), channel_id=1, source_target_pairs={{0,1},{1,0},{2,18},{3,19},{4,5},{5,4},{6,22},{7,23},{8,9},{9,8},{1... | collective-permute-start | bytes 344072 | tf_op jit(solution)/shard_map/ppermute | solution.py:124
  103.8 2.4 %collective-permute-done.17 = bf16[4,224,128]{2,1,0:T(8,128)(2,1)S(1)} collective-permute-done((bf16[4,224,128]{2,1,0:T(8,128)(2,1)S(1)}, bf16[4,224,128]{2,1,0:T(8,128)(2,1)S(1)}, u32[]{:S(2)}, u32[]{:S(2)}) %collective-permute-start.17) | collective-permute-done | bytes 229408 | tf_op jit(solution)/shard_map/ppermute | solution.py:124
  106.2 0.1 add_convert_fusion.4
  106.3 1.2 %collective-permute-start.20 = (bf16[2,224,128]{2,1,0:T(8,128)(2,1)S(1)}, bf16[2,224,128]{2,1,0:T(8,128)(2,1)S(1)}, u32[]{:S(2)}, u32[]{:S(2)}) collective-permute-start(bf16[2,224,128]{2,1,0:T(8,128)(2,1)S(1)} %get-tuple-element.56), channel_id=1, source_target_pairs={{0,8},{1,9},{2,10},{3,11},{4,12},{5,13},{6,14},{7,15},{8,0},{9,1},... | collective-permute-start | bytes 344072 | tf_op jit(solution)/shard_map/ppermute | solution.py:124
  107.5 0.0 collective-permute-done.18
  107.5 3.8 %collective-permute-start.19 = (bf16[1,224,128]{2,1,0:T(8,128)(2,1)S(1)}, bf16[1,224,128]{2,1,0:T(8,128)(2,1)S(1)}, u32[]{:S(2)}, u32[]{:S(2)}) collective-permute-start(bf16[1,224,128]{2,1,0:T(8,128)(2,1)S(1)} %add_convert_fusion.7), channel_id=1, source_target_pairs={{0,16},{1,17},{2,6},{3,7},{4,20},{5,21},{6,2},{7,3},{8,24},{9,25},... | collective-permute-start | bytes 172040 | tf_op jit(solution)/shard_map/ppermute | solution.py:124
  111.3 0.0 collective-permute-done.20
  111.4 3.8 %collective-permute-start.21 = (bf16[1,224,128]{2,1,0:T(8,128)(2,1)S(1)}, bf16[1,224,128]{2,1,0:T(8,128)(2,1)S(1)}, u32[]{:S(2)}, u32[]{:S(2)}) collective-permute-start(bf16[1,224,128]{2,1,0:T(8,128)(2,1)S(1)} %add_convert_fusion.6), channel_id=1, source_target_pairs={{0,16},{1,17},{2,3},{3,2},{4,20},{5,21},{6,7},{7,6},{8,24},{9,25},... | collective-permute-start | bytes 172040 | tf_op jit(solution)/shard_map/ppermute | solution.py:124
  115.2 0.0 collective-permute-done.19
  115.3 2.1 %collective-permute-done.21 = bf16[1,224,128]{2,1,0:T(8,128)(2,1)S(1)} collective-permute-done((bf16[1,224,128]{2,1,0:T(8,128)(2,1)S(1)}, bf16[1,224,128]{2,1,0:T(8,128)(2,1)S(1)}, u32[]{:S(2)}, u32[]{:S(2)}) %collective-permute-start.21) | collective-permute-done | bytes 57376 | tf_op jit(solution)/shard_map/ppermute | solution.py:124
  117.4 0.0 copy-done.1
  117.4 0.0 copy-done.2
  117.5 0.0 copy-done.3
  117.5 1.2 fusion.5
  (19 shorter events, 0.4 us)
Async XLA Ops:
  1.6 33.9 %copy-start = (s32[32]{0:T(128)S(1)}, s32[32]{0:T(128)}, u32[]{:S(2)}) copy-start(s32[32]{0:T(128)} %refs_1_.1) | copy-start | bytes 388
  2.8 6.3 %collective-permute-start = (bf16[1,224,128]{2,1,0:T(8,128)(2,1)S(1)}, bf16[1,224,128]{2,1,0:T(8,128)(2,1)S(1)}, u32[]{:S(2)}, u32[]{:S(2)}) collective-permute-start(bf16[1,224,128]{2,1,0:T(8,128)(2,1)S(1)} %get-tuple-element.60), channel_id=1, source_target_pairs={{0,16},{1,17},{2,3},{3,2},{4,20},{5,21},{6,7},{7,6},{8,24},{9,25},... | collective-permute-start | bytes 172040 | tf_op jit(solution)/shard_map/ppermute | solution.py:103
  6.9 5.1 %collective-permute-start.1 = (bf16[1,224,128]{2,1,0:T(8,128)(2,1)S(1)}, bf16[1,224,128]{2,1,0:T(8,128)(2,1)S(1)}, u32[]{:S(2)}, u32[]{:S(2)}) collective-permute-start(bf16[1,224,128]{2,1,0:T(8,128)(2,1)S(1)} %get-tuple-element.26), channel_id=1, source_target_pairs={{0,16},{1,17},{2,6},{3,7},{4,20},{5,21},{6,2},{7,3},{8,24},{9,25},... | collective-permute-start | bytes 172040 | tf_op jit(solution)/shard_map/ppermute | solution.py:103
  9.1 5.6 %collective-permute-start.2 = (bf16[2,224,128]{2,1,0:T(8,128)(2,1)S(1)}, bf16[2,224,128]{2,1,0:T(8,128)(2,1)S(1)}, u32[]{:S(2)}, u32[]{:S(2)}) collective-permute-start(bf16[2,224,128]{2,1,0:T(8,128)(2,1)S(1)} %constant_dynamic-update-slice_fusion), channel_id=1, source_target_pairs={{0,8},{1,9},{2,10},{3,11},{4,12},{5,13},{6,14},{7,15},{8,0},{9,1},... | collective-permute-start | bytes 344072 | tf_op jit(solution)/shard_map/ppermute | solution.py:103
  12.0 4.9 %collective-permute-start.3 = (bf16[2,224,128]{2,1,0:T(8,128)(2,1)S(1)}, bf16[2,224,128]{2,1,0:T(8,128)(2,1)S(1)}, u32[]{:S(2)}, u32[]{:S(2)}) collective-permute-start(bf16[2,224,128]{2,1,0:T(8,128)(2,1)S(1)} %constant_dynamic-update-slice_fusion.2), channel_id=1, source_target_pairs={{0,1},{1,0},{2,18},{3,19},{4,5},{5,4},{6,22},{7,23},{8,9},{9,8},{1... | collective-permute-start | bytes 344072 | tf_op jit(solution)/shard_map/ppermute | solution.py:103
  14.7 6.1 %collective-permute-start.4 = (bf16[4,224,128]{2,1,0:T(8,128)(2,1)S(1)}, bf16[4,224,128]{2,1,0:T(8,128)(2,1)S(1)}, u32[]{:S(2)}, u32[]{:S(2)}) collective-permute-start(bf16[4,224,128]{2,1,0:T(8,128)(2,1)S(1)} %constant_dynamic-update-slice_fusion.4), channel_id=1, source_target_pairs={{0,4},{1,5},{2,18},{3,19},{4,0},{5,1},{6,22},{7,23},{8,12},{9,13},... | collective-permute-start | bytes 688136 | tf_op jit(solution)/shard_map/ppermute | solution.py:103
  16.9 6.3 %collective-permute-start.5 = (bf16[4,224,128]{2,1,0:T(8,128)(2,1)S(1)}, bf16[4,224,128]{2,1,0:T(8,128)(2,1)S(1)}, u32[]{:S(2)}, u32[]{:S(2)}) collective-permute-start(bf16[4,224,128]{2,1,0:T(8,128)(2,1)S(1)} %constant_dynamic-update-slice_fusion.6), channel_id=1, source_target_pairs={{0,4},{1,5},{2,10},{3,11},{4,0},{5,1},{6,14},{7,15},{8,12},{9,13},... | collective-permute-start | bytes 688136 | tf_op jit(solution)/shard_map/ppermute | solution.py:103
  23.3 8.5 %collective-permute-start.6 = (bf16[8,224,128]{2,1,0:T(8,128)(2,1)S(1)}, bf16[8,224,128]{2,1,0:T(8,128)(2,1)S(1)}, u32[]{:S(2)}, u32[]{:S(2)}) collective-permute-start(bf16[8,224,128]{2,1,0:T(8,128)(2,1)S(1)} %constant_dynamic-update-slice_fusion.10.refs_2_), channel_id=1, source_target_pairs={{0,8},{1,9},{2,3},{3,2},{4,12},{5,13},{6,7},{7,6},{8,0},{9,1},{10,... | collective-permute-start | bytes 1376264 | tf_op jit(solution)/shard_map/ppermute | solution.py:103
  25.2 8.5 %collective-permute-start.9 = (bf16[8,224,128]{2,1,0:T(8,128)(2,1)S(1)}, bf16[8,224,128]{2,1,0:T(8,128)(2,1)S(1)}, u32[]{:S(2)}, u32[]{:S(2)}) collective-permute-start(bf16[8,224,128]{2,1,0:T(8,128)(2,1)S(1)} %constant_dynamic-update-slice_fusion.8.refs_6_), channel_id=1, source_target_pairs={{0,1},{1,0},{2,6},{3,7},{4,5},{5,4},{6,2},{7,3},{8,9},{9,8},{10,14... | collective-permute-start | bytes 1376264 | tf_op jit(solution)/shard_map/ppermute | solution.py:103
  26.7 7.0 %collective-permute-start.7 = (bf16[8,224,128]{2,1,0:T(8,128)(2,1)S(1)}, bf16[8,224,128]{2,1,0:T(8,128)(2,1)S(1)}, u32[]{:S(2)}, u32[]{:S(2)}) collective-permute-start(bf16[8,224,128]{2,1,0:T(8,128)(2,1)S(1)} %constant_dynamic-update-slice_fusion.10.refs_2_), channel_id=1, source_target_pairs={{0,2},{1,3},{2,0},{3,1},{4,6},{5,7},{6,4},{7,5},{8,10},{9,11},{10,... | collective-permute-start | bytes 1376264 | tf_op jit(solution)/shard_map/ppermute | solution.py:107
  26.7 7.0 %collective-permute-start.10 = (bf16[8,224,128]{2,1,0:T(8,128)(2,1)S(1)}, bf16[8,224,128]{2,1,0:T(8,128)(2,1)S(1)}, u32[]{:S(2)}, u32[]{:S(2)}) collective-permute-start(bf16[8,224,128]{2,1,0:T(8,128)(2,1)S(1)} %constant_dynamic-update-slice_fusion.8.refs_6_), channel_id=1, source_target_pairs={{0,2},{1,3},{2,0},{3,1},{4,6},{5,7},{6,4},{7,5},{8,10},{9,11},{10,... | collective-permute-start | bytes 1376264 | tf_op jit(solution)/shard_map/ppermute | solution.py:107
  31.8 1.9 %collective-permute-start.8 = (bf16[8,224,128]{2,1,0:T(8,128)(2,1)S(1)}, bf16[8,224,128]{2,1,0:T(8,128)(2,1)S(1)}, u32[]{:S(2)}, u32[]{:S(2)}) collective-permute-start(bf16[8,224,128]{2,1,0:T(8,128)(2,1)S(1)} %collective-permute-done.6.refs_3_), channel_id=1, source_target_pairs={{0,2},{1,3},{2,0},{3,1},{4,6},{5,7},{6,4},{7,5},{8,10},{9,11},{10,... | collective-permute-start | bytes 1376264 | tf_op jit(solution)/shard_map/ppermute | solution.py:107
  33.7 1.8 %collective-permute-start.11 = (bf16[8,224,128]{2,1,0:T(8,128)(2,1)S(1)}, bf16[8,224,128]{2,1,0:T(8,128)(2,1)S(1)}, u32[]{:S(2)}, u32[]{:S(2)}) collective-permute-start(bf16[8,224,128]{2,1,0:T(8,128)(2,1)S(1)} %collective-permute-done.9.refs_7_), channel_id=1, source_target_pairs={{0,2},{1,3},{2,0},{3,1},{4,6},{5,7},{6,4},{7,5},{8,10},{9,11},{10,... | collective-permute-start | bytes 1376264 | tf_op jit(solution)/shard_map/ppermute | solution.py:107
  84.7 2.5 %collective-permute-start.12 = (bf16[16,224,128]{2,1,0:T(8,128)(2,1)S(1)}, bf16[16,224,128]{2,1,0:T(8,128)(2,1)S(1)}, u32[]{:S(2)}, u32[]{:S(2)}) collective-permute-start(bf16[16,224,128]{2,1,0:T(8,128)(2,1)S(1)} %get-tuple-element.35), channel_id=1, source_target_pairs={{0,2},{1,3},{2,0},{3,1},{4,6},{5,7},{6,4},{7,5},{8,10},{9,11},{10,... | collective-permute-start | bytes 2752520 | tf_op jit(solution)/shard_map/ppermute | solution.py:113
  84.9 3.7 %collective-permute-start.13 = (bf16[16,224,128]{2,1,0:T(8,128)(2,1)S(1)}, bf16[16,224,128]{2,1,0:T(8,128)(2,1)S(1)}, u32[]{:S(2)}, u32[]{:S(2)}) collective-permute-start(bf16[16,224,128]{2,1,0:T(8,128)(2,1)S(1)} %get-tuple-element.37), channel_id=1, source_target_pairs={{0,2},{1,3},{2,0},{3,1},{4,6},{5,7},{6,4},{7,5},{8,10},{9,11},{10,... | collective-permute-start | bytes 2752520 | tf_op jit(solution)/shard_map/ppermute | solution.py:113
  87.4 8.5 %collective-permute-start.14 = (bf16[8,224,128]{2,1,0:T(8,128)(2,1)S(1)}, bf16[8,224,128]{2,1,0:T(8,128)(2,1)S(1)}, u32[]{:S(2)}, u32[]{:S(2)}) collective-permute-start(bf16[8,224,128]{2,1,0:T(8,128)(2,1)S(1)} %get-tuple-element.51), channel_id=1, source_target_pairs={{0,8},{1,9},{2,3},{3,2},{4,12},{5,13},{6,7},{7,6},{8,0},{9,1},{10,... | collective-permute-start | bytes 1376264 | tf_op jit(solution)/shard_map/ppermute | solution.py:124
  88.8 11.2 %collective-permute-start.15 = (bf16[8,224,128]{2,1,0:T(8,128)(2,1)S(1)}, bf16[8,224,128]{2,1,0:T(8,128)(2,1)S(1)}, u32[]{:S(2)}, u32[]{:S(2)}) collective-permute-start(bf16[8,224,128]{2,1,0:T(8,128)(2,1)S(1)} %get-tuple-element.48), channel_id=1, source_target_pairs={{0,1},{1,0},{2,6},{3,7},{4,5},{5,4},{6,2},{7,3},{8,9},{9,8},{10,14... | collective-permute-start | bytes 1376264 | tf_op jit(solution)/shard_map/ppermute | solution.py:124
  96.0 6.1 %collective-permute-start.16 = (bf16[4,224,128]{2,1,0:T(8,128)(2,1)S(1)}, bf16[4,224,128]{2,1,0:T(8,128)(2,1)S(1)}, u32[]{:S(2)}, u32[]{:S(2)}) collective-permute-start(bf16[4,224,128]{2,1,0:T(8,128)(2,1)S(1)} %get-tuple-element.55), channel_id=1, source_target_pairs={{0,4},{1,5},{2,10},{3,11},{4,0},{5,1},{6,14},{7,15},{8,12},{9,13},... | collective-permute-start | bytes 688136 | tf_op jit(solution)/shard_map/ppermute | solution.py:124
  100.1 6.1 %collective-permute-start.17 = (bf16[4,224,128]{2,1,0:T(8,128)(2,1)S(1)}, bf16[4,224,128]{2,1,0:T(8,128)(2,1)S(1)}, u32[]{:S(2)}, u32[]{:S(2)}) collective-permute-start(bf16[4,224,128]{2,1,0:T(8,128)(2,1)S(1)} %get-tuple-element.52), channel_id=1, source_target_pairs={{0,4},{1,5},{2,18},{3,19},{4,0},{5,1},{6,22},{7,23},{8,12},{9,13},... | collective-permute-start | bytes 688136 | tf_op jit(solution)/shard_map/ppermute | solution.py:124
  102.2 15.2 %copy-start.1 = (f32[55416]{0:T(1024)S(1)}, f32[55416]{0:T(1024)}, u32[]{:S(2)}) copy-start(f32[55416]{0:T(1024)} %param.11) | copy-start | bytes 664996
  102.2 15.2 %copy-start.2 = (f32[55416]{0:T(1024)S(1)}, f32[55416]{0:T(1024)}, u32[]{:S(2)}) copy-start(f32[55416]{0:T(1024)} %param.13) | copy-start | bytes 664996
  102.2 15.2 %copy-start.3 = (f32[55416]{0:T(1024)S(1)}, f32[55416]{0:T(1024)}, u32[]{:S(2)}) copy-start(f32[55416]{0:T(1024)} %param.12) | copy-start | bytes 664996
  102.2 5.3 %collective-permute-start.18 = (bf16[2,224,128]{2,1,0:T(8,128)(2,1)S(1)}, bf16[2,224,128]{2,1,0:T(8,128)(2,1)S(1)}, u32[]{:S(2)}, u32[]{:S(2)}) collective-permute-start(bf16[2,224,128]{2,1,0:T(8,128)(2,1)S(1)} %get-tuple-element.59), channel_id=1, source_target_pairs={{0,1},{1,0},{2,18},{3,19},{4,5},{5,4},{6,22},{7,23},{8,9},{9,8},{1... | collective-permute-start | bytes 344072 | tf_op jit(solution)/shard_map/ppermute | solution.py:124
  106.3 5.1 %collective-permute-start.20 = (bf16[2,224,128]{2,1,0:T(8,128)(2,1)S(1)}, bf16[2,224,128]{2,1,0:T(8,128)(2,1)S(1)}, u32[]{:S(2)}, u32[]{:S(2)}) collective-permute-start(bf16[2,224,128]{2,1,0:T(8,128)(2,1)S(1)} %get-tuple-element.56), channel_id=1, source_target_pairs={{0,8},{1,9},{2,10},{3,11},{4,12},{5,13},{6,14},{7,15},{8,0},{9,1},... | collective-permute-start | bytes 344072 | tf_op jit(solution)/shard_map/ppermute | solution.py:124
  107.5 7.7 %collective-permute-start.19 = (bf16[1,224,128]{2,1,0:T(8,128)(2,1)S(1)}, bf16[1,224,128]{2,1,0:T(8,128)(2,1)S(1)}, u32[]{:S(2)}, u32[]{:S(2)}) collective-permute-start(bf16[1,224,128]{2,1,0:T(8,128)(2,1)S(1)} %add_convert_fusion.7), channel_id=1, source_target_pairs={{0,16},{1,17},{2,6},{3,7},{4,20},{5,21},{6,2},{7,3},{8,24},{9,25},... | collective-permute-start | bytes 172040 | tf_op jit(solution)/shard_map/ppermute | solution.py:124
  111.4 6.0 %collective-permute-start.21 = (bf16[1,224,128]{2,1,0:T(8,128)(2,1)S(1)}, bf16[1,224,128]{2,1,0:T(8,128)(2,1)S(1)}, u32[]{:S(2)}, u32[]{:S(2)}) collective-permute-start(bf16[1,224,128]{2,1,0:T(8,128)(2,1)S(1)} %add_convert_fusion.6), channel_id=1, source_target_pairs={{0,16},{1,17},{2,3},{3,2},{4,20},{5,21},{6,7},{7,6},{8,24},{9,25},... | collective-permute-start | bytes 172040 | tf_op jit(solution)/shard_map/ppermute | solution.py:124

commit v4 on v3

--- a/solution.py
+++ b/solution.py
@@ -29,7 +29,7 @@
 VMEM_LIMIT = 44 * 1024 * 1024
 BLOCK = 512
 GROUP = 8
-COLUMNS = 512
+COLUMNS = 768
 FLOWS = 2
 
 

time: 119 us -> 118 us (level)
  no operation moved by 1% of the time
where the time goes in v4:
time: 118 us
  Pallas kernels  48.1 us (41%)
  starting transfers between devices  32.2 us (27%)
  waiting for transfers between devices  30.7 us (26%)
  other arithmetic  3 us (3%)
  between operations  2.18 us (2%)
  local copies, waits for them, and re-layouts  1.37 us (1%)
    pallas_call x1, Pallas kernels, layer(): pl.pallas_call(functools.partial(layer_kernel, flows, shard), name='layer...  48.1 us
    ppermute x8, starting transfers between devices, scatter_chunks(): parts[turn].append(lax.ppermute(last, AXES, flow.swaps[index]))  16.5 us
    ppermute x8, waiting for transfers between devices, gather_chunks(): taken[turn] = lax.ppermute(last, AXES, flows[turn].swaps[index])  15.5 us
    ppermute x8, starting transfers between devices, gather_chunks(): taken[turn] = lax.ppermute(last, AXES, flows[turn].swaps[index])  14.7 us
    ppermute x8, waiting for transfers between devices, scatter_chunks(): parts[turn].append(lax.ppermute(last, AXES, flow.swaps[index]))  11.4 us
  transfers between devices with their start and end apart: 22, of which 15 were waited for; matrix products, arithmetic and copies ran while one was open for 1% of the time, Pallas kernels for 0%

profile of v4, /device:TPU:0, one launch (start us, length us, event | category | flops | bytes accessed | tf_op | source)
XLA Modules:
  0.0 117.5 jit_solution(108048471210729812)
XLA Ops:
  0.6 1.0 convert_element_type.142
  1.6 0.0 copy-start
  1.6 1.1 dynamic_update_slice.3
  2.8 4.1 %collective-permute-start = (bf16[1,224,128]{2,1,0:T(8,128)(2,1)S(1)}, bf16[1,224,128]{2,1,0:T(8,128)(2,1)S(1)}, u32[]{:S(2)}, u32[]{:S(2)}) collective-permute-start(bf16[1,224,128]{2,1,0:T(8,128)(2,1)S(1)} %get-tuple-element.60), channel_id=1, source_target_pairs={{0,16},{1,17},{2,3},{3,2},{4,20},{5,21},{6,7},{7,6},{8,24},{9,25},... | collective-permute-start | bytes 172040 | tf_op jit(solution)/shard_map/ppermute | solution.py:103
  6.9 0.1 collective-permute-start.1
  7.0 2.1 %collective-permute-done = bf16[1,224,128]{2,1,0:T(8,128)(2,1)S(1)} collective-permute-done((bf16[1,224,128]{2,1,0:T(8,128)(2,1)S(1)}, bf16[1,224,128]{2,1,0:T(8,128)(2,1)S(1)}, u32[]{:S(2)}, u32[]{:S(2)}) %collective-permute-start) | collective-permute-done | bytes 57376 | tf_op jit(solution)/shard_map/ppermute | solution.py:103
  9.1 2.3 %collective-permute-start.2 = (bf16[2,224,128]{2,1,0:T(8,128)(2,1)S(1)}, bf16[2,224,128]{2,1,0:T(8,128)(2,1)S(1)}, u32[]{:S(2)}, u32[]{:S(2)}) collective-permute-start(bf16[2,224,128]{2,1,0:T(8,128)(2,1)S(1)} %constant_dynamic-update-slice_fusion), channel_id=1, source_target_pairs={{0,8},{1,9},{2,10},{3,11},{4,12},{5,13},{6,14},{7,15},{8,0},{9,1},... | collective-permute-start | bytes 344072 | tf_op jit(solution)/shard_map/ppermute | solution.py:103
  11.4 0.6 collective-permute-done.1
  12.0 1.6 %collective-permute-start.3 = (bf16[2,224,128]{2,1,0:T(8,128)(2,1)S(1)}, bf16[2,224,128]{2,1,0:T(8,128)(2,1)S(1)}, u32[]{:S(2)}, u32[]{:S(2)}) collective-permute-start(bf16[2,224,128]{2,1,0:T(8,128)(2,1)S(1)} %constant_dynamic-update-slice_fusion.2), channel_id=1, source_target_pairs={{0,1},{1,0},{2,18},{3,19},{4,5},{5,4},{6,22},{7,23},{8,9},{9,8},{1... | collective-permute-start | bytes 344072 | tf_op jit(solution)/shard_map/ppermute | solution.py:103
  13.6 1.1 collective-permute-done.2
  14.7 1.6 %collective-permute-start.4 = (bf16[4,224,128]{2,1,0:T(8,128)(2,1)S(1)}, bf16[4,224,128]{2,1,0:T(8,128)(2,1)S(1)}, u32[]{:S(2)}, u32[]{:S(2)}) collective-permute-start(bf16[4,224,128]{2,1,0:T(8,128)(2,1)S(1)} %constant_dynamic-update-slice_fusion.4), channel_id=1, source_target_pairs={{0,4},{1,5},{2,18},{3,19},{4,0},{5,1},{6,22},{7,23},{8,12},{9,13},... | collective-permute-start | bytes 688136 | tf_op jit(solution)/shard_map/ppermute | solution.py:103
  16.3 0.6 collective-permute-done.3
  16.9 1.6 %collective-permute-start.5 = (bf16[4,224,128]{2,1,0:T(8,128)(2,1)S(1)}, bf16[4,224,128]{2,1,0:T(8,128)(2,1)S(1)}, u32[]{:S(2)}, u32[]{:S(2)}) collective-permute-start(bf16[4,224,128]{2,1,0:T(8,128)(2,1)S(1)} %constant_dynamic-update-slice_fusion.6), channel_id=1, source_target_pairs={{0,4},{1,5},{2,10},{3,11},{4,0},{5,1},{6,14},{7,15},{8,12},{9,13},... | collective-permute-start | bytes 688136 | tf_op jit(solution)/shard_map/ppermute | solution.py:103
  18.5 2.3 %collective-permute-done.4 = bf16[4,224,128]{2,1,0:T(8,128)(2,1)S(1)} collective-permute-done((bf16[4,224,128]{2,1,0:T(8,128)(2,1)S(1)}, bf16[4,224,128]{2,1,0:T(8,128)(2,1)S(1)}, u32[]{:S(2)}, u32[]{:S(2)}) %collective-permute-start.4) | collective-permute-done | bytes 229408 | tf_op jit(solution)/shard_map/ppermute | solution.py:103
  20.8 2.4 %collective-permute-done.5 = bf16[4,224,128]{2,1,0:T(8,128)(2,1)S(1)} collective-permute-done((bf16[4,224,128]{2,1,0:T(8,128)(2,1)S(1)}, bf16[4,224,128]{2,1,0:T(8,128)(2,1)S(1)}, u32[]{:S(2)}, u32[]{:S(2)}) %collective-permute-start.5) | collective-permute-done | bytes 229408 | tf_op jit(solution)/shard_map/ppermute | solution.py:103
  23.3 1.9 %collective-permute-start.6 = (bf16[8,224,128]{2,1,0:T(8,128)(2,1)S(1)}, bf16[8,224,128]{2,1,0:T(8,128)(2,1)S(1)}, u32[]{:S(2)}, u32[]{:S(2)}) collective-permute-start(bf16[8,224,128]{2,1,0:T(8,128)(2,1)S(1)} %constant_dynamic-update-slice_fusion.10.refs_2_), channel_id=1, source_target_pairs={{0,8},{1,9},{2,3},{3,2},{4,12},{5,13},{6,7},{7,6},{8,0},{9,1},{10,... | collective-permute-start | bytes 1376264 | tf_op jit(solution)/shard_map/ppermute | solution.py:103
  25.2 1.5 %collective-permute-start.9 = (bf16[8,224,128]{2,1,0:T(8,128)(2,1)S(1)}, bf16[8,224,128]{2,1,0:T(8,128)(2,1)S(1)}, u32[]{:S(2)}, u32[]{:S(2)}) collective-permute-start(bf16[8,224,128]{2,1,0:T(8,128)(2,1)S(1)} %constant_dynamic-update-slice_fusion.8.refs_6_), channel_id=1, source_target_pairs={{0,1},{1,0},{2,6},{3,7},{4,5},{5,4},{6,2},{7,3},{8,9},{9,8},{10,14... | collective-permute-start | bytes 1376264 | tf_op jit(solution)/shard_map/ppermute | solution.py:103
  26.7 0.0 collective-permute-start.7
  26.7 0.5 collective-permute-start.10
  27.2 4.6 %collective-permute-done.6.refs_3_ = bf16[8,224,128]{2,1,0:T(8,128)(2,1)S(1)} collective-permute-done((bf16[8,224,128]{2,1,0:T(8,128)(2,1)S(1)}, bf16[8,224,128]{2,1,0:T(8,128)(2,1)S(1)}, u32[]{:S(2)}, u32[]{:S(2)}) %collective-permute-start.6) | collective-permute-done | bytes 458784 | tf_op jit(solution)/shard_map/ppermute | solution.py:103
  31.8 0.0 collective-permute-start.8
  31.8 1.9 %collective-permute-done.9.refs_7_ = bf16[8,224,128]{2,1,0:T(8,128)(2,1)S(1)} collective-permute-done((bf16[8,224,128]{2,1,0:T(8,128)(2,1)S(1)}, bf16[8,224,128]{2,1,0:T(8,128)(2,1)S(1)}, u32[]{:S(2)}, u32[]{:S(2)}) %collective-permute-start.9) | collective-permute-done | bytes 458784 | tf_op jit(solution)/shard_map/ppermute | solution.py:103
  33.7 0.0 collective-permute-start.11
  33.7 0.0 collective-permute-done.7.refs_4_
  33.7 0.0 collective-permute-done.10.refs_8_
  33.7 0.0 collective-permute-done.8.refs_5_
  33.7 1.8 %collective-permute-done.11.refs_9_ = bf16[8,224,128]{2,1,0:T(8,128)(2,1)S(1)} collective-permute-done((bf16[8,224,128]{2,1,0:T(8,128)(2,1)S(1)}, bf16[8,224,128]{2,1,0:T(8,128)(2,1)S(1)}, u32[]{:S(2)}, u32[]{:S(2)}) %collective-permute-start.11) | collective-permute-done | bytes 458784 | tf_op jit(solution)/shard_map/ppermute | solution.py:107
  35.5 0.0 copy-done
  35.5 48.1 %layer.1 = (bf16[2048,384]{1,0:T(8,128)(2,1)}, bf16[2048,384]{1,0:T(8,128)(2,1)}, f32[16,224,128]{2,1,0:T(8,128)S(1)}, bf16[16,224,128]{2,1,0:T(8,128)(2,1)S(1)}...) custom-call(s32[1]{0:T(128)} %bitcast.refs_0_, s32[32]{0:T(128)S(1)} %copy-done, ...), custom_call_target="tpu_custom_call" | custom-call | tf_op jit(solution)/shard_map/layer/pallas_call | solution.py:437
  83.6 0.1 collective-permute-start.12
  83.8 0.4 collective-permute-start.13
  84.1 2.0 %collective-permute-done.12 = bf16[16,224,128]{2,1,0:T(8,128)(2,1)S(1)} collective-permute-done((bf16[16,224,128]{2,1,0:T(8,128)(2,1)S(1)}, bf16[16,224,128]{2,1,0:T(8,128)(2,1)S(1)}, u32[]{:S(2)}, u32[]{:S(2)}) %collective-permute-start.12) | collective-permute-done | bytes 917536 | tf_op jit(solution)/shard_map/ppermute | solution.py:113
  86.1 0.2 fusion.7
  86.3 1.2 %collective-permute-start.14 = (bf16[8,224,128]{2,1,0:T(8,128)(2,1)S(1)}, bf16[8,224,128]{2,1,0:T(8,128)(2,1)S(1)}, u32[]{:S(2)}, u32[]{:S(2)}) collective-permute-start(bf16[8,224,128]{2,1,0:T(8,128)(2,1)S(1)} %get-tuple-element.51), channel_id=1, source_target_pairs={{0,8},{1,9},{2,3},{3,2},{4,12},{5,13},{6,7},{7,6},{8,0},{9,1},{10,... | collective-permute-start | bytes 1376264 | tf_op jit(solution)/shard_map/ppermute | solution.py:124
  87.5 0.0 collective-permute-done.13
  87.5 0.2 add_convert_fusion
  87.7 1.8 %collective-permute-start.15 = (bf16[8,224,128]{2,1,0:T(8,128)(2,1)S(1)}, bf16[8,224,128]{2,1,0:T(8,128)(2,1)S(1)}, u32[]{:S(2)}, u32[]{:S(2)}) collective-permute-start(bf16[8,224,128]{2,1,0:T(8,128)(2,1)S(1)} %get-tuple-element.48), channel_id=1, source_target_pairs={{0,1},{1,0},{2,6},{3,7},{4,5},{5,4},{6,2},{7,3},{8,9},{9,8},{10,14... | collective-permute-start | bytes 1376264 | tf_op jit(solution)/shard_map/ppermute | solution.py:124
  90.8 4.0 %collective-permute-done.14 = bf16[8,224,128]{2,1,0:T(8,128)(2,1)S(1)} collective-permute-done((bf16[8,224,128]{2,1,0:T(8,128)(2,1)S(1)}, bf16[8,224,128]{2,1,0:T(8,128)(2,1)S(1)}, u32[]{:S(2)}, u32[]{:S(2)}) %collective-permute-start.14) | collective-permute-done | bytes 458784 | tf_op jit(solution)/shard_map/ppermute | solution.py:124
  94.8 0.1 fusion.8
  94.9 1.5 %collective-permute-start.16 = (bf16[4,224,128]{2,1,0:T(8,128)(2,1)S(1)}, bf16[4,224,128]{2,1,0:T(8,128)(2,1)S(1)}, u32[]{:S(2)}, u32[]{:S(2)}) collective-permute-start(bf16[4,224,128]{2,1,0:T(8,128)(2,1)S(1)} %get-tuple-element.55), channel_id=1, source_target_pairs={{0,4},{1,5},{2,10},{3,11},{4,0},{5,1},{6,14},{7,15},{8,12},{9,13},... | collective-permute-start | bytes 688136 | tf_op jit(solution)/shard_map/ppermute | solution.py:124
  96.4 2.5 %collective-permute-done.15 = bf16[8,224,128]{2,1,0:T(8,128)(2,1)S(1)} collective-permute-done((bf16[8,224,128]{2,1,0:T(8,128)(2,1)S(1)}, bf16[8,224,128]{2,1,0:T(8,128)(2,1)S(1)}, u32[]{:S(2)}, u32[]{:S(2)}) %collective-permute-start.15) | collective-permute-done | bytes 458784 | tf_op jit(solution)/shard_map/ppermute | solution.py:124
  98.9 0.1 add_convert_fusion.2
  99.0 1.5 %collective-permute-start.17 = (bf16[4,224,128]{2,1,0:T(8,128)(2,1)S(1)}, bf16[4,224,128]{2,1,0:T(8,128)(2,1)S(1)}, u32[]{:S(2)}, u32[]{:S(2)}) collective-permute-start(bf16[4,224,128]{2,1,0:T(8,128)(2,1)S(1)} %get-tuple-element.52), channel_id=1, source_target_pairs={{0,4},{1,5},{2,18},{3,19},{4,0},{5,1},{6,22},{7,23},{8,12},{9,13},... | collective-permute-start | bytes 688136 | tf_op jit(solution)/shard_map/ppermute | solution.py:124
  100.5 0.5 collective-permute-done.16
  101.0 0.1 fusion.9
  101.1 0.0 copy-start.1
  101.1 0.0 copy-start.2
  101.1 0.0 copy-start.3
  101.1 1.6 %collective-permute-start.18 = (bf16[2,224,128]{2,1,0:T(8,128)(2,1)S(1)}, bf16[2,224,128]{2,1,0:T(8,128)(2,1)S(1)}, u32[]{:S(2)}, u32[]{:S(2)}) collective-permute-start(bf16[2,224,128]{2,1,0:T(8,128)(2,1)S(1)} %get-tuple-element.59), channel_id=1, source_target_pairs={{0,1},{1,0},{2,18},{3,19},{4,5},{5,4},{6,22},{7,23},{8,9},{9,8},{1... | collective-permute-start | bytes 344072 | tf_op jit(solution)/shard_map/ppermute | solution.py:124
  102.8 2.3 %collective-permute-done.17 = bf16[4,224,128]{2,1,0:T(8,128)(2,1)S(1)} collective-permute-done((bf16[4,224,128]{2,1,0:T(8,128)(2,1)S(1)}, bf16[4,224,128]{2,1,0:T(8,128)(2,1)S(1)}, u32[]{:S(2)}, u32[]{:S(2)}) %collective-permute-start.17) | collective-permute-done | bytes 229408 | tf_op jit(solution)/shard_map/ppermute | solution.py:124
  105.1 0.1 add_convert_fusion.4
  105.2 1.2 %collective-permute-start.20 = (bf16[2,224,128]{2,1,0:T(8,128)(2,1)S(1)}, bf16[2,224,128]{2,1,0:T(8,128)(2,1)S(1)}, u32[]{:S(2)}, u32[]{:S(2)}) collective-permute-start(bf16[2,224,128]{2,1,0:T(8,128)(2,1)S(1)} %get-tuple-element.56), channel_id=1, source_target_pairs={{0,8},{1,9},{2,10},{3,11},{4,12},{5,13},{6,14},{7,15},{8,0},{9,1},... | collective-permute-start | bytes 344072 | tf_op jit(solution)/shard_map/ppermute | solution.py:124
  106.4 0.0 collective-permute-done.18
  106.4 3.8 %collective-permute-start.19 = (bf16[1,224,128]{2,1,0:T(8,128)(2,1)S(1)}, bf16[1,224,128]{2,1,0:T(8,128)(2,1)S(1)}, u32[]{:S(2)}, u32[]{:S(2)}) collective-permute-start(bf16[1,224,128]{2,1,0:T(8,128)(2,1)S(1)} %add_convert_fusion.7), channel_id=1, source_target_pairs={{0,16},{1,17},{2,6},{3,7},{4,20},{5,21},{6,2},{7,3},{8,24},{9,25},... | collective-permute-start | bytes 172040 | tf_op jit(solution)/shard_map/ppermute | solution.py:124
  110.2 0.0 collective-permute-done.20
  110.3 3.8 %collective-permute-start.21 = (bf16[1,224,128]{2,1,0:T(8,128)(2,1)S(1)}, bf16[1,224,128]{2,1,0:T(8,128)(2,1)S(1)}, u32[]{:S(2)}, u32[]{:S(2)}) collective-permute-start(bf16[1,224,128]{2,1,0:T(8,128)(2,1)S(1)} %add_convert_fusion.6), channel_id=1, source_target_pairs={{0,16},{1,17},{2,3},{3,2},{4,20},{5,21},{6,7},{7,6},{8,24},{9,25},... | collective-permute-start | bytes 172040 | tf_op jit(solution)/shard_map/ppermute | solution.py:124
  114.1 0.0 collective-permute-done.19
  114.2 2.1 %collective-permute-done.21 = bf16[1,224,128]{2,1,0:T(8,128)(2,1)S(1)} collective-permute-done((bf16[1,224,128]{2,1,0:T(8,128)(2,1)S(1)}, bf16[1,224,128]{2,1,0:T(8,128)(2,1)S(1)}, u32[]{:S(2)}, u32[]{:S(2)}) %collective-permute-start.21) | collective-permute-done | bytes 57376 | tf_op jit(solution)/shard_map/ppermute | solution.py:124
  116.3 0.0 copy-done.1
  116.3 0.0 copy-done.2
  116.4 0.0 copy-done.3
  116.4 1.2 fusion.5
  (19 shorter events, 0.4 us)
Async XLA Ops:
  1.6 33.9 %copy-start = (s32[32]{0:T(128)S(1)}, s32[32]{0:T(128)}, u32[]{:S(2)}) copy-start(s32[32]{0:T(128)} %refs_1_.1) | copy-start | bytes 388
  2.8 6.3 %collective-permute-start = (bf16[1,224,128]{2,1,0:T(8,128)(2,1)S(1)}, bf16[1,224,128]{2,1,0:T(8,128)(2,1)S(1)}, u32[]{:S(2)}, u32[]{:S(2)}) collective-permute-start(bf16[1,224,128]{2,1,0:T(8,128)(2,1)S(1)} %get-tuple-element.60), channel_id=1, source_target_pairs={{0,16},{1,17},{2,3},{3,2},{4,20},{5,21},{6,7},{7,6},{8,24},{9,25},... | collective-permute-start | bytes 172040 | tf_op jit(solution)/shard_map/ppermute | solution.py:103
  6.9 5.1 %collective-permute-start.1 = (bf16[1,224,128]{2,1,0:T(8,128)(2,1)S(1)}, bf16[1,224,128]{2,1,0:T(8,128)(2,1)S(1)}, u32[]{:S(2)}, u32[]{:S(2)}) collective-permute-start(bf16[1,224,128]{2,1,0:T(8,128)(2,1)S(1)} %get-tuple-element.26), channel_id=1, source_target_pairs={{0,16},{1,17},{2,6},{3,7},{4,20},{5,21},{6,2},{7,3},{8,24},{9,25},... | collective-permute-start | bytes 172040 | tf_op jit(solution)/shard_map/ppermute | solution.py:103
  9.1 5.6 %collective-permute-start.2 = (bf16[2,224,128]{2,1,0:T(8,128)(2,1)S(1)}, bf16[2,224,128]{2,1,0:T(8,128)(2,1)S(1)}, u32[]{:S(2)}, u32[]{:S(2)}) collective-permute-start(bf16[2,224,128]{2,1,0:T(8,128)(2,1)S(1)} %constant_dynamic-update-slice_fusion), channel_id=1, source_target_pairs={{0,8},{1,9},{2,10},{3,11},{4,12},{5,13},{6,14},{7,15},{8,0},{9,1},... | collective-permute-start | bytes 344072 | tf_op jit(solution)/shard_map/ppermute | solution.py:103
  12.0 4.9 %collective-permute-start.3 = (bf16[2,224,128]{2,1,0:T(8,128)(2,1)S(1)}, bf16[2,224,128]{2,1,0:T(8,128)(2,1)S(1)}, u32[]{:S(2)}, u32[]{:S(2)}) collective-permute-start(bf16[2,224,128]{2,1,0:T(8,128)(2,1)S(1)} %constant_dynamic-update-slice_fusion.2), channel_id=1, source_target_pairs={{0,1},{1,0},{2,18},{3,19},{4,5},{5,4},{6,22},{7,23},{8,9},{9,8},{1... | collective-permute-start | bytes 344072 | tf_op jit(solution)/shard_map/ppermute | solution.py:103
  14.7 6.1 %collective-permute-start.4 = (bf16[4,224,128]{2,1,0:T(8,128)(2,1)S(1)}, bf16[4,224,128]{2,1,0:T(8,128)(2,1)S(1)}, u32[]{:S(2)}, u32[]{:S(2)}) collective-permute-start(bf16[4,224,128]{2,1,0:T(8,128)(2,1)S(1)} %constant_dynamic-update-slice_fusion.4), channel_id=1, source_target_pairs={{0,4},{1,5},{2,18},{3,19},{4,0},{5,1},{6,22},{7,23},{8,12},{9,13},... | collective-permute-start | bytes 688136 | tf_op jit(solution)/shard_map/ppermute | solution.py:103
  16.9 6.3 %collective-permute-start.5 = (bf16[4,224,128]{2,1,0:T(8,128)(2,1)S(1)}, bf16[4,224,128]{2,1,0:T(8,128)(2,1)S(1)}, u32[]{:S(2)}, u32[]{:S(2)}) collective-permute-start(bf16[4,224,128]{2,1,0:T(8,128)(2,1)S(1)} %constant_dynamic-update-slice_fusion.6), channel_id=1, source_target_pairs={{0,4},{1,5},{2,10},{3,11},{4,0},{5,1},{6,14},{7,15},{8,12},{9,13},... | collective-permute-start | bytes 688136 | tf_op jit(solution)/shard_map/ppermute | solution.py:103
  23.3 8.5 %collective-permute-start.6 = (bf16[8,224,128]{2,1,0:T(8,128)(2,1)S(1)}, bf16[8,224,128]{2,1,0:T(8,128)(2,1)S(1)}, u32[]{:S(2)}, u32[]{:S(2)}) collective-permute-start(bf16[8,224,128]{2,1,0:T(8,128)(2,1)S(1)} %constant_dynamic-update-slice_fusion.10.refs_2_), channel_id=1, source_target_pairs={{0,8},{1,9},{2,3},{3,2},{4,12},{5,13},{6,7},{7,6},{8,0},{9,1},{10,... | collective-permute-start | bytes 1376264 | tf_op jit(solution)/shard_map/ppermute | solution.py:103
  25.2 8.5 %collective-permute-start.9 = (bf16[8,224,128]{2,1,0:T(8,128)(2,1)S(1)}, bf16[8,224,128]{2,1,0:T(8,128)(2,1)S(1)}, u32[]{:S(2)}, u32[]{:S(2)}) collective-permute-start(bf16[8,224,128]{2,1,0:T(8,128)(2,1)S(1)} %constant_dynamic-update-slice_fusion.8.refs_6_), channel_id=1, source_target_pairs={{0,1},{1,0},{2,6},{3,7},{4,5},{5,4},{6,2},{7,3},{8,9},{9,8},{10,14... | collective-permute-start | bytes 1376264 | tf_op jit(solution)/shard_map/ppermute | solution.py:103
  26.7 7.0 %collective-permute-start.7 = (bf16[8,224,128]{2,1,0:T(8,128)(2,1)S(1)}, bf16[8,224,128]{2,1,0:T(8,128)(2,1)S(1)}, u32[]{:S(2)}, u32[]{:S(2)}) collective-permute-start(bf16[8,224,128]{2,1,0:T(8,128)(2,1)S(1)} %constant_dynamic-update-slice_fusion.10.refs_2_), channel_id=1, source_target_pairs={{0,2},{1,3},{2,0},{3,1},{4,6},{5,7},{6,4},{7,5},{8,10},{9,11},{10,... | collective-permute-start | bytes 1376264 | tf_op jit(solution)/shard_map/ppermute | solution.py:107
  26.7 7.0 %collective-permute-start.10 = (bf16[8,224,128]{2,1,0:T(8,128)(2,1)S(1)}, bf16[8,224,128]{2,1,0:T(8,128)(2,1)S(1)}, u32[]{:S(2)}, u32[]{:S(2)}) collective-permute-start(bf16[8,224,128]{2,1,0:T(8,128)(2,1)S(1)} %constant_dynamic-update-slice_fusion.8.refs_6_), channel_id=1, source_target_pairs={{0,2},{1,3},{2,0},{3,1},{4,6},{5,7},{6,4},{7,5},{8,10},{9,11},{10,... | collective-permute-start | bytes 1376264 | tf_op jit(solution)/shard_map/ppermute | solution.py:107
  31.8 1.9 %collective-permute-start.8 = (bf16[8,224,128]{2,1,0:T(8,128)(2,1)S(1)}, bf16[8,224,128]{2,1,0:T(8,128)(2,1)S(1)}, u32[]{:S(2)}, u32[]{:S(2)}) collective-permute-start(bf16[8,224,128]{2,1,0:T(8,128)(2,1)S(1)} %collective-permute-done.6.refs_3_), channel_id=1, source_target_pairs={{0,2},{1,3},{2,0},{3,1},{4,6},{5,7},{6,4},{7,5},{8,10},{9,11},{10,... | collective-permute-start | bytes 1376264 | tf_op jit(solution)/shard_map/ppermute | solution.py:107
  33.7 1.8 %collective-permute-start.11 = (bf16[8,224,128]{2,1,0:T(8,128)(2,1)S(1)}, bf16[8,224,128]{2,1,0:T(8,128)(2,1)S(1)}, u32[]{:S(2)}, u32[]{:S(2)}) collective-permute-start(bf16[8,224,128]{2,1,0:T(8,128)(2,1)S(1)} %collective-permute-done.9.refs_7_), channel_id=1, source_target_pairs={{0,2},{1,3},{2,0},{3,1},{4,6},{5,7},{6,4},{7,5},{8,10},{9,11},{10,... | collective-permute-start | bytes 1376264 | tf_op jit(solution)/shard_map/ppermute | solution.py:107
  83.6 2.5 %collective-permute-start.12 = (bf16[16,224,128]{2,1,0:T(8,128)(2,1)S(1)}, bf16[16,224,128]{2,1,0:T(8,128)(2,1)S(1)}, u32[]{:S(2)}, u32[]{:S(2)}) collective-permute-start(bf16[16,224,128]{2,1,0:T(8,128)(2,1)S(1)} %get-tuple-element.35), channel_id=1, source_target_pairs={{0,2},{1,3},{2,0},{3,1},{4,6},{5,7},{6,4},{7,5},{8,10},{9,11},{10,... | collective-permute-start | bytes 2752520 | tf_op jit(solution)/shard_map/ppermute | solution.py:113
  83.8 3.7 %collective-permute-start.13 = (bf16[16,224,128]{2,1,0:T(8,128)(2,1)S(1)}, bf16[16,224,128]{2,1,0:T(8,128)(2,1)S(1)}, u32[]{:S(2)}, u32[]{:S(2)}) collective-permute-start(bf16[16,224,128]{2,1,0:T(8,128)(2,1)S(1)} %get-tuple-element.37), channel_id=1, source_target_pairs={{0,2},{1,3},{2,0},{3,1},{4,6},{5,7},{6,4},{7,5},{8,10},{9,11},{10,... | collective-permute-start | bytes 2752520 | tf_op jit(solution)/shard_map/ppermute | solution.py:113
  86.3 8.5 %collective-permute-start.14 = (bf16[8,224,128]{2,1,0:T(8,128)(2,1)S(1)}, bf16[8,224,128]{2,1,0:T(8,128)(2,1)S(1)}, u32[]{:S(2)}, u32[]{:S(2)}) collective-permute-start(bf16[8,224,128]{2,1,0:T(8,128)(2,1)S(1)} %get-tuple-element.51), channel_id=1, source_target_pairs={{0,8},{1,9},{2,3},{3,2},{4,12},{5,13},{6,7},{7,6},{8,0},{9,1},{10,... | collective-permute-start | bytes 1376264 | tf_op jit(solution)/shard_map/ppermute | solution.py:124
  87.7 11.2 %collective-permute-start.15 = (bf16[8,224,128]{2,1,0:T(8,128)(2,1)S(1)}, bf16[8,224,128]{2,1,0:T(8,128)(2,1)S(1)}, u32[]{:S(2)}, u32[]{:S(2)}) collective-permute-start(bf16[8,224,128]{2,1,0:T(8,128)(2,1)S(1)} %get-tuple-element.48), channel_id=1, source_target_pairs={{0,1},{1,0},{2,6},{3,7},{4,5},{5,4},{6,2},{7,3},{8,9},{9,8},{10,14... | collective-permute-start | bytes 1376264 | tf_op jit(solution)/shard_map/ppermute | solution.py:124
  94.9 6.1 %collective-permute-start.16 = (bf16[4,224,128]{2,1,0:T(8,128)(2,1)S(1)}, bf16[4,224,128]{2,1,0:T(8,128)(2,1)S(1)}, u32[]{:S(2)}, u32[]{:S(2)}) collective-permute-start(bf16[4,224,128]{2,1,0:T(8,128)(2,1)S(1)} %get-tuple-element.55), channel_id=1, source_target_pairs={{0,4},{1,5},{2,10},{3,11},{4,0},{5,1},{6,14},{7,15},{8,12},{9,13},... | collective-permute-start | bytes 688136 | tf_op jit(solution)/shard_map/ppermute | solution.py:124
  99.0 6.1 %collective-permute-start.17 = (bf16[4,224,128]{2,1,0:T(8,128)(2,1)S(1)}, bf16[4,224,128]{2,1,0:T(8,128)(2,1)S(1)}, u32[]{:S(2)}, u32[]{:S(2)}) collective-permute-start(bf16[4,224,128]{2,1,0:T(8,128)(2,1)S(1)} %get-tuple-element.52), channel_id=1, source_target_pairs={{0,4},{1,5},{2,18},{3,19},{4,0},{5,1},{6,22},{7,23},{8,12},{9,13},... | collective-permute-start | bytes 688136 | tf_op jit(solution)/shard_map/ppermute | solution.py:124
  101.1 15.2 %copy-start.1 = (f32[55416]{0:T(1024)S(1)}, f32[55416]{0:T(1024)}, u32[]{:S(2)}) copy-start(f32[55416]{0:T(1024)} %param.11) | copy-start | bytes 664996
  101.1 15.2 %copy-start.2 = (f32[55416]{0:T(1024)S(1)}, f32[55416]{0:T(1024)}, u32[]{:S(2)}) copy-start(f32[55416]{0:T(1024)} %param.13) | copy-start | bytes 664996
  101.1 15.2 %copy-start.3 = (f32[55416]{0:T(1024)S(1)}, f32[55416]{0:T(1024)}, u32[]{:S(2)}) copy-start(f32[55416]{0:T(1024)} %param.12) | copy-start | bytes 664996
  101.1 5.3 %collective-permute-start.18 = (bf16[2,224,128]{2,1,0:T(8,128)(2,1)S(1)}, bf16[2,224,128]{2,1,0:T(8,128)(2,1)S(1)}, u32[]{:S(2)}, u32[]{:S(2)}) collective-permute-start(bf16[2,224,128]{2,1,0:T(8,128)(2,1)S(1)} %get-tuple-element.59), channel_id=1, source_target_pairs={{0,1},{1,0},{2,18},{3,19},{4,5},{5,4},{6,22},{7,23},{8,9},{9,8},{1... | collective-permute-start | bytes 344072 | tf_op jit(solution)/shard_map/ppermute | solution.py:124
  105.2 5.1 %collective-permute-start.20 = (bf16[2,224,128]{2,1,0:T(8,128)(2,1)S(1)}, bf16[2,224,128]{2,1,0:T(8,128)(2,1)S(1)}, u32[]{:S(2)}, u32[]{:S(2)}) collective-permute-start(bf16[2,224,128]{2,1,0:T(8,128)(2,1)S(1)} %get-tuple-element.56), channel_id=1, source_target_pairs={{0,8},{1,9},{2,10},{3,11},{4,12},{5,13},{6,14},{7,15},{8,0},{9,1},... | collective-permute-start | bytes 344072 | tf_op jit(solution)/shard_map/ppermute | solution.py:124
  106.4 7.7 %collective-permute-start.19 = (bf16[1,224,128]{2,1,0:T(8,128)(2,1)S(1)}, bf16[1,224,128]{2,1,0:T(8,128)(2,1)S(1)}, u32[]{:S(2)}, u32[]{:S(2)}) collective-permute-start(bf16[1,224,128]{2,1,0:T(8,128)(2,1)S(1)} %add_convert_fusion.7), channel_id=1, source_target_pairs={{0,16},{1,17},{2,6},{3,7},{4,20},{5,21},{6,2},{7,3},{8,24},{9,25},... | collective-permute-start | bytes 172040 | tf_op jit(solution)/shard_map/ppermute | solution.py:124
  110.3 6.0 %collective-permute-start.21 = (bf16[1,224,128]{2,1,0:T(8,128)(2,1)S(1)}, bf16[1,224,128]{2,1,0:T(8,128)(2,1)S(1)}, u32[]{:S(2)}, u32[]{:S(2)}) collective-permute-start(bf16[1,224,128]{2,1,0:T(8,128)(2,1)S(1)} %add_convert_fusion.6), channel_id=1, source_target_pairs={{0,16},{1,17},{2,3},{3,2},{4,20},{5,21},{6,7},{7,6},{8,24},{9,25},... | collective-permute-start | bytes 172040 | tf_op jit(solution)/shard_map/ppermute | solution.py:124

commit v5 on v4

--- a/solution.py
+++ b/solution.py
@@ -189,10 +189,14 @@
         (grad_qkv, 0),
         (grad_out, BASE_OUT),
         (grad_up, BASE_UP),
-        (grad_down, BASE_DOWN),
     ):
         for columns, rows_of in matrix_blocks(matrix, base):
             flat[rows_of, :] = matrix[:, columns]
+    blocks = D // LANES
+    for block in range(blocks):
+        flat[pl.ds(BASE_DOWN + block, FF, stride=blocks), :] = grad_down[
+            block * LANES : (block + 1) * LANES, :
+        ].T
     for index, columns, row in vector_rows():
         flat[row : row + 1, :] = vectors[index : index + 1, columns]
     flat[FLAT_ROWS:, :] = jnp.zeros((flat.shape[0] - FLAT_ROWS, LANES), jnp.float32)
@@ -393,7 +397,7 @@
         grad_upward = dot(grad_out_low, w_down[columns, :], 1, 1) * slope
         grad_upward = grad_upward.astype(jnp.bfloat16)
         add_vector("bias_up", grad_upward.astype(jnp.float32), at)
-        acc_down[columns, :] += dot(active, grad_out_low, 0, 0)
+        acc_down[:, columns] += dot(grad_out_low, active, 0, 0)
         acc_up[:, columns] += dot(normed_two, grad_upward, 0, 0)
         grad_normed_two = grad_normed_two + dot(grad_upward, w_up[:, columns], 1, 1)
     result[...] = total.astype(jnp.bfloat16)
@@ -454,7 +458,7 @@
                 pltpu.VMEM((D, 3 * D), full),
                 pltpu.VMEM((D, D), full),
                 pltpu.VMEM((D, FF), full),
-                pltpu.VMEM((FF, D), full),
+                pltpu.VMEM((D, FF), full),
                 pltpu.VMEM((8, FF), full),
                 pltpu.VMEM((block, 3 * D), low),
                 pltpu.VMEM((block, D), full),

time: 118 us -> 118 us (level)
  no operation moved by 1% of the time
where the time goes in v5:
time: 118 us; the launch traced here: 117 us
  Pallas kernels  47.9 us (41%)
  starting transfers between devices  32.2 us (27%)
  waiting for transfers between devices  30.7 us (26%)
  other arithmetic  3 us (3%)
  between operations  2.18 us (2%)
  local copies, waits for them, and re-layouts  1.37 us (1%)
    pallas_call x1, Pallas kernels, layer(): pl.pallas_call(functools.partial(layer_kernel, flows, shard), name='layer...  47.9 us
    ppermute x8, starting transfers between devices, scatter_chunks(): parts[turn].append(lax.ppermute(last, AXES, flow.swaps[index]))  16.5 us
    ppermute x8, waiting for transfers between devices, gather_chunks(): taken[turn] = lax.ppermute(last, AXES, flows[turn].swaps[index])  15.5 us
    ppermute x8, starting transfers between devices, gather_chunks(): taken[turn] = lax.ppermute(last, AXES, flows[turn].swaps[index])  14.7 us
    ppermute x8, waiting for transfers between devices, scatter_chunks(): parts[turn].append(lax.ppermute(last, AXES, flow.swaps[index]))  11.4 us
  transfers between devices with their start and end apart: 22, of which 15 were waited for; matrix products, arithmetic and copies ran while one was open for 1% of the time, Pallas kernels for 0%

profile of v5, /device:TPU:0, one launch (start us, length us, event | category | flops | bytes accessed | tf_op | source)
XLA Modules:
  0.0 117.3 jit_solution(1852488170966101454)
XLA Ops:
  0.6 1.0 convert_element_type.142
  1.6 0.0 copy-start
  1.6 1.1 dynamic_update_slice.3
  2.8 4.1 %collective-permute-start = (bf16[1,224,128]{2,1,0:T(8,128)(2,1)S(1)}, bf16[1,224,128]{2,1,0:T(8,128)(2,1)S(1)}, u32[]{:S(2)}, u32[]{:S(2)}) collective-permute-start(bf16[1,224,128]{2,1,0:T(8,128)(2,1)S(1)} %get-tuple-element.60), channel_id=1, source_target_pairs={{0,16},{1,17},{2,3},{3,2},{4,20},{5,21},{6,7},{7,6},{8,24},{9,25},... | collective-permute-start | bytes 172040 | tf_op jit(solution)/shard_map/ppermute | solution.py:103
  6.9 0.1 collective-permute-start.1
  7.0 2.1 %collective-permute-done = bf16[1,224,128]{2,1,0:T(8,128)(2,1)S(1)} collective-permute-done((bf16[1,224,128]{2,1,0:T(8,128)(2,1)S(1)}, bf16[1,224,128]{2,1,0:T(8,128)(2,1)S(1)}, u32[]{:S(2)}, u32[]{:S(2)}) %collective-permute-start) | collective-permute-done | bytes 57376 | tf_op jit(solution)/shard_map/ppermute | solution.py:103
  9.1 2.3 %collective-permute-start.2 = (bf16[2,224,128]{2,1,0:T(8,128)(2,1)S(1)}, bf16[2,224,128]{2,1,0:T(8,128)(2,1)S(1)}, u32[]{:S(2)}, u32[]{:S(2)}) collective-permute-start(bf16[2,224,128]{2,1,0:T(8,128)(2,1)S(1)} %constant_dynamic-update-slice_fusion), channel_id=1, source_target_pairs={{0,8},{1,9},{2,10},{3,11},{4,12},{5,13},{6,14},{7,15},{8,0},{9,1},... | collective-permute-start | bytes 344072 | tf_op jit(solution)/shard_map/ppermute | solution.py:103
  11.4 0.6 collective-permute-done.1
  12.0 1.6 %collective-permute-start.3 = (bf16[2,224,128]{2,1,0:T(8,128)(2,1)S(1)}, bf16[2,224,128]{2,1,0:T(8,128)(2,1)S(1)}, u32[]{:S(2)}, u32[]{:S(2)}) collective-permute-start(bf16[2,224,128]{2,1,0:T(8,128)(2,1)S(1)} %constant_dynamic-update-slice_fusion.2), channel_id=1, source_target_pairs={{0,1},{1,0},{2,18},{3,19},{4,5},{5,4},{6,22},{7,23},{8,9},{9,8},{1... | collective-permute-start | bytes 344072 | tf_op jit(solution)/shard_map/ppermute | solution.py:103
  13.6 1.1 collective-permute-done.2
  14.7 1.6 %collective-permute-start.4 = (bf16[4,224,128]{2,1,0:T(8,128)(2,1)S(1)}, bf16[4,224,128]{2,1,0:T(8,128)(2,1)S(1)}, u32[]{:S(2)}, u32[]{:S(2)}) collective-permute-start(bf16[4,224,128]{2,1,0:T(8,128)(2,1)S(1)} %constant_dynamic-update-slice_fusion.4), channel_id=1, source_target_pairs={{0,4},{1,5},{2,18},{3,19},{4,0},{5,1},{6,22},{7,23},{8,12},{9,13},... | collective-permute-start | bytes 688136 | tf_op jit(solution)/shard_map/ppermute | solution.py:103
  16.3 0.6 collective-permute-done.3
  16.9 1.6 %collective-permute-start.5 = (bf16[4,224,128]{2,1,0:T(8,128)(2,1)S(1)}, bf16[4,224,128]{2,1,0:T(8,128)(2,1)S(1)}, u32[]{:S(2)}, u32[]{:S(2)}) collective-permute-start(bf16[4,224,128]{2,1,0:T(8,128)(2,1)S(1)} %constant_dynamic-update-slice_fusion.6), channel_id=1, source_target_pairs={{0,4},{1,5},{2,10},{3,11},{4,0},{5,1},{6,14},{7,15},{8,12},{9,13},... | collective-permute-start | bytes 688136 | tf_op jit(solution)/shard_map/ppermute | solution.py:103
  18.5 2.3 %collective-permute-done.4 = bf16[4,224,128]{2,1,0:T(8,128)(2,1)S(1)} collective-permute-done((bf16[4,224,128]{2,1,0:T(8,128)(2,1)S(1)}, bf16[4,224,128]{2,1,0:T(8,128)(2,1)S(1)}, u32[]{:S(2)}, u32[]{:S(2)}) %collective-permute-start.4) | collective-permute-done | bytes 229408 | tf_op jit(solution)/shard_map/ppermute | solution.py:103
  20.8 2.4 %collective-permute-done.5 = bf16[4,224,128]{2,1,0:T(8,128)(2,1)S(1)} collective-permute-done((bf16[4,224,128]{2,1,0:T(8,128)(2,1)S(1)}, bf16[4,224,128]{2,1,0:T(8,128)(2,1)S(1)}, u32[]{:S(2)}, u32[]{:S(2)}) %collective-permute-start.5) | collective-permute-done | bytes 229408 | tf_op jit(solution)/shard_map/ppermute | solution.py:103
  23.3 1.9 %collective-permute-start.6 = (bf16[8,224,128]{2,1,0:T(8,128)(2,1)S(1)}, bf16[8,224,128]{2,1,0:T(8,128)(2,1)S(1)}, u32[]{:S(2)}, u32[]{:S(2)}) collective-permute-start(bf16[8,224,128]{2,1,0:T(8,128)(2,1)S(1)} %constant_dynamic-update-slice_fusion.10.refs_2_), channel_id=1, source_target_pairs={{0,8},{1,9},{2,3},{3,2},{4,12},{5,13},{6,7},{7,6},{8,0},{9,1},{10,... | collective-permute-start | bytes 1376264 | tf_op jit(solution)/shard_map/ppermute | solution.py:103
  25.2 1.5 %collective-permute-start.9 = (bf16[8,224,128]{2,1,0:T(8,128)(2,1)S(1)}, bf16[8,224,128]{2,1,0:T(8,128)(2,1)S(1)}, u32[]{:S(2)}, u32[]{:S(2)}) collective-permute-start(bf16[8,224,128]{2,1,0:T(8,128)(2,1)S(1)} %constant_dynamic-update-slice_fusion.8.refs_6_), channel_id=1, source_target_pairs={{0,1},{1,0},{2,6},{3,7},{4,5},{5,4},{6,2},{7,3},{8,9},{9,8},{10,14... | collective-permute-start | bytes 1376264 | tf_op jit(solution)/shard_map/ppermute | solution.py:103
  26.7 0.0 collective-permute-start.7
  26.7 0.5 collective-permute-start.10
  27.2 4.6 %collective-permute-done.6.refs_3_ = bf16[8,224,128]{2,1,0:T(8,128)(2,1)S(1)} collective-permute-done((bf16[8,224,128]{2,1,0:T(8,128)(2,1)S(1)}, bf16[8,224,128]{2,1,0:T(8,128)(2,1)S(1)}, u32[]{:S(2)}, u32[]{:S(2)}) %collective-permute-start.6) | collective-permute-done | bytes 458784 | tf_op jit(solution)/shard_map/ppermute | solution.py:103
  31.8 0.0 collective-permute-start.8
  31.8 1.9 %collective-permute-done.9.refs_7_ = bf16[8,224,128]{2,1,0:T(8,128)(2,1)S(1)} collective-permute-done((bf16[8,224,128]{2,1,0:T(8,128)(2,1)S(1)}, bf16[8,224,128]{2,1,0:T(8,128)(2,1)S(1)}, u32[]{:S(2)}, u32[]{:S(2)}) %collective-permute-start.9) | collective-permute-done | bytes 458784 | tf_op jit(solution)/shard_map/ppermute | solution.py:103
  33.7 0.0 collective-permute-start.11
  33.7 0.0 collective-permute-done.7.refs_4_
  33.7 0.0 collective-permute-done.10.refs_8_
  33.7 0.0 collective-permute-done.8.refs_5_
  33.7 1.8 %collective-permute-done.11.refs_9_ = bf16[8,224,128]{2,1,0:T(8,128)(2,1)S(1)} collective-permute-done((bf16[8,224,128]{2,1,0:T(8,128)(2,1)S(1)}, bf16[8,224,128]{2,1,0:T(8,128)(2,1)S(1)}, u32[]{:S(2)}, u32[]{:S(2)}) %collective-permute-start.11) | collective-permute-done | bytes 458784 | tf_op jit(solution)/shard_map/ppermute | solution.py:107
  35.5 0.0 copy-done
  35.5 47.9 %layer.1 = (bf16[2048,384]{1,0:T(8,128)(2,1)}, bf16[2048,384]{1,0:T(8,128)(2,1)}, f32[16,224,128]{2,1,0:T(8,128)S(1)}, bf16[16,224,128]{2,1,0:T(8,128)(2,1)S(1)}...) custom-call(s32[1]{0:T(128)} %bitcast.refs_0_, s32[32]{0:T(128)S(1)} %copy-done, ...), custom_call_target="tpu_custom_call" | custom-call | tf_op jit(solution)/shard_map/layer/pallas_call | solution.py:441
  83.4 0.1 collective-permute-start.12
  83.5 0.4 collective-permute-start.13
  83.9 2.0 %collective-permute-done.12 = bf16[16,224,128]{2,1,0:T(8,128)(2,1)S(1)} collective-permute-done((bf16[16,224,128]{2,1,0:T(8,128)(2,1)S(1)}, bf16[16,224,128]{2,1,0:T(8,128)(2,1)S(1)}, u32[]{:S(2)}, u32[]{:S(2)}) %collective-permute-start.12) | collective-permute-done | bytes 917536 | tf_op jit(solution)/shard_map/ppermute | solution.py:113
  85.9 0.2 fusion.7
  86.1 1.2 %collective-permute-start.14 = (bf16[8,224,128]{2,1,0:T(8,128)(2,1)S(1)}, bf16[8,224,128]{2,1,0:T(8,128)(2,1)S(1)}, u32[]{:S(2)}, u32[]{:S(2)}) collective-permute-start(bf16[8,224,128]{2,1,0:T(8,128)(2,1)S(1)} %get-tuple-element.51), channel_id=1, source_target_pairs={{0,8},{1,9},{2,3},{3,2},{4,12},{5,13},{6,7},{7,6},{8,0},{9,1},{10,... | collective-permute-start | bytes 1376264 | tf_op jit(solution)/shard_map/ppermute | solution.py:124
  87.3 0.0 collective-permute-done.13
  87.3 0.2 add_convert_fusion
  87.5 1.8 %collective-permute-start.15 = (bf16[8,224,128]{2,1,0:T(8,128)(2,1)S(1)}, bf16[8,224,128]{2,1,0:T(8,128)(2,1)S(1)}, u32[]{:S(2)}, u32[]{:S(2)}) collective-permute-start(bf16[8,224,128]{2,1,0:T(8,128)(2,1)S(1)} %get-tuple-element.48), channel_id=1, source_target_pairs={{0,1},{1,0},{2,6},{3,7},{4,5},{5,4},{6,2},{7,3},{8,9},{9,8},{10,14... | collective-permute-start | bytes 1376264 | tf_op jit(solution)/shard_map/ppermute | solution.py:124
  90.6 4.0 %collective-permute-done.14 = bf16[8,224,128]{2,1,0:T(8,128)(2,1)S(1)} collective-permute-done((bf16[8,224,128]{2,1,0:T(8,128)(2,1)S(1)}, bf16[8,224,128]{2,1,0:T(8,128)(2,1)S(1)}, u32[]{:S(2)}, u32[]{:S(2)}) %collective-permute-start.14) | collective-permute-done | bytes 458784 | tf_op jit(solution)/shard_map/ppermute | solution.py:124
  94.6 0.1 fusion.8
  94.7 1.5 %collective-permute-start.16 = (bf16[4,224,128]{2,1,0:T(8,128)(2,1)S(1)}, bf16[4,224,128]{2,1,0:T(8,128)(2,1)S(1)}, u32[]{:S(2)}, u32[]{:S(2)}) collective-permute-start(bf16[4,224,128]{2,1,0:T(8,128)(2,1)S(1)} %get-tuple-element.55), channel_id=1, source_target_pairs={{0,4},{1,5},{2,10},{3,11},{4,0},{5,1},{6,14},{7,15},{8,12},{9,13},... | collective-permute-start | bytes 688136 | tf_op jit(solution)/shard_map/ppermute | solution.py:124
  96.2 2.5 %collective-permute-done.15 = bf16[8,224,128]{2,1,0:T(8,128)(2,1)S(1)} collective-permute-done((bf16[8,224,128]{2,1,0:T(8,128)(2,1)S(1)}, bf16[8,224,128]{2,1,0:T(8,128)(2,1)S(1)}, u32[]{:S(2)}, u32[]{:S(2)}) %collective-permute-start.15) | collective-permute-done | bytes 458784 | tf_op jit(solution)/shard_map/ppermute | solution.py:124
  98.7 0.1 add_convert_fusion.2
  98.8 1.5 %collective-permute-start.17 = (bf16[4,224,128]{2,1,0:T(8,128)(2,1)S(1)}, bf16[4,224,128]{2,1,0:T(8,128)(2,1)S(1)}, u32[]{:S(2)}, u32[]{:S(2)}) collective-permute-start(bf16[4,224,128]{2,1,0:T(8,128)(2,1)S(1)} %get-tuple-element.52), channel_id=1, source_target_pairs={{0,4},{1,5},{2,18},{3,19},{4,0},{5,1},{6,22},{7,23},{8,12},{9,13},... | collective-permute-start | bytes 688136 | tf_op jit(solution)/shard_map/ppermute | solution.py:124
  100.3 0.5 collective-permute-done.16
  100.8 0.1 fusion.9
  100.9 0.0 copy-start.1
  100.9 0.0 copy-start.2
  100.9 0.0 copy-start.3
  100.9 1.6 %collective-permute-start.18 = (bf16[2,224,128]{2,1,0:T(8,128)(2,1)S(1)}, bf16[2,224,128]{2,1,0:T(8,128)(2,1)S(1)}, u32[]{:S(2)}, u32[]{:S(2)}) collective-permute-start(bf16[2,224,128]{2,1,0:T(8,128)(2,1)S(1)} %get-tuple-element.59), channel_id=1, source_target_pairs={{0,1},{1,0},{2,18},{3,19},{4,5},{5,4},{6,22},{7,23},{8,9},{9,8},{1... | collective-permute-start | bytes 344072 | tf_op jit(solution)/shard_map/ppermute | solution.py:124
  102.5 2.3 %collective-permute-done.17 = bf16[4,224,128]{2,1,0:T(8,128)(2,1)S(1)} collective-permute-done((bf16[4,224,128]{2,1,0:T(8,128)(2,1)S(1)}, bf16[4,224,128]{2,1,0:T(8,128)(2,1)S(1)}, u32[]{:S(2)}, u32[]{:S(2)}) %collective-permute-start.17) | collective-permute-done | bytes 229408 | tf_op jit(solution)/shard_map/ppermute | solution.py:124
  104.9 0.1 add_convert_fusion.4
  104.9 1.2 %collective-permute-start.20 = (bf16[2,224,128]{2,1,0:T(8,128)(2,1)S(1)}, bf16[2,224,128]{2,1,0:T(8,128)(2,1)S(1)}, u32[]{:S(2)}, u32[]{:S(2)}) collective-permute-start(bf16[2,224,128]{2,1,0:T(8,128)(2,1)S(1)} %get-tuple-element.56), channel_id=1, source_target_pairs={{0,8},{1,9},{2,10},{3,11},{4,12},{5,13},{6,14},{7,15},{8,0},{9,1},... | collective-permute-start | bytes 344072 | tf_op jit(solution)/shard_map/ppermute | solution.py:124
  106.2 0.0 collective-permute-done.18
  106.2 3.8 %collective-permute-start.19 = (bf16[1,224,128]{2,1,0:T(8,128)(2,1)S(1)}, bf16[1,224,128]{2,1,0:T(8,128)(2,1)S(1)}, u32[]{:S(2)}, u32[]{:S(2)}) collective-permute-start(bf16[1,224,128]{2,1,0:T(8,128)(2,1)S(1)} %add_convert_fusion.7), channel_id=1, source_target_pairs={{0,16},{1,17},{2,6},{3,7},{4,20},{5,21},{6,2},{7,3},{8,24},{9,25},... | collective-permute-start | bytes 172040 | tf_op jit(solution)/shard_map/ppermute | solution.py:124
  110.0 0.0 collective-permute-done.20
  110.1 3.8 %collective-permute-start.21 = (bf16[1,224,128]{2,1,0:T(8,128)(2,1)S(1)}, bf16[1,224,128]{2,1,0:T(8,128)(2,1)S(1)}, u32[]{:S(2)}, u32[]{:S(2)}) collective-permute-start(bf16[1,224,128]{2,1,0:T(8,128)(2,1)S(1)} %add_convert_fusion.6), channel_id=1, source_target_pairs={{0,16},{1,17},{2,3},{3,2},{4,20},{5,21},{6,7},{7,6},{8,24},{9,25},... | collective-permute-start | bytes 172040 | tf_op jit(solution)/shard_map/ppermute | solution.py:124
  113.9 0.0 collective-permute-done.19
  113.9 2.1 %collective-permute-done.21 = bf16[1,224,128]{2,1,0:T(8,128)(2,1)S(1)} collective-permute-done((bf16[1,224,128]{2,1,0:T(8,128)(2,1)S(1)}, bf16[1,224,128]{2,1,0:T(8,128)(2,1)S(1)}, u32[]{:S(2)}, u32[]{:S(2)}) %collective-permute-start.21) | collective-permute-done | bytes 57376 | tf_op jit(solution)/shard_map/ppermute | solution.py:124
  116.1 0.0 copy-done.1
  116.1 0.0 copy-done.2
  116.1 0.0 copy-done.3
  116.2 1.2 fusion.5
  (19 shorter events, 0.4 us)
Async XLA Ops:
  1.6 33.9 %copy-start = (s32[32]{0:T(128)S(1)}, s32[32]{0:T(128)}, u32[]{:S(2)}) copy-start(s32[32]{0:T(128)} %refs_1_.1) | copy-start | bytes 388
  2.8 6.3 %collective-permute-start = (bf16[1,224,128]{2,1,0:T(8,128)(2,1)S(1)}, bf16[1,224,128]{2,1,0:T(8,128)(2,1)S(1)}, u32[]{:S(2)}, u32[]{:S(2)}) collective-permute-start(bf16[1,224,128]{2,1,0:T(8,128)(2,1)S(1)} %get-tuple-element.60), channel_id=1, source_target_pairs={{0,16},{1,17},{2,3},{3,2},{4,20},{5,21},{6,7},{7,6},{8,24},{9,25},... | collective-permute-start | bytes 172040 | tf_op jit(solution)/shard_map/ppermute | solution.py:103
  6.9 5.1 %collective-permute-start.1 = (bf16[1,224,128]{2,1,0:T(8,128)(2,1)S(1)}, bf16[1,224,128]{2,1,0:T(8,128)(2,1)S(1)}, u32[]{:S(2)}, u32[]{:S(2)}) collective-permute-start(bf16[1,224,128]{2,1,0:T(8,128)(2,1)S(1)} %get-tuple-element.26), channel_id=1, source_target_pairs={{0,16},{1,17},{2,6},{3,7},{4,20},{5,21},{6,2},{7,3},{8,24},{9,25},... | collective-permute-start | bytes 172040 | tf_op jit(solution)/shard_map/ppermute | solution.py:103
  9.1 5.6 %collective-permute-start.2 = (bf16[2,224,128]{2,1,0:T(8,128)(2,1)S(1)}, bf16[2,224,128]{2,1,0:T(8,128)(2,1)S(1)}, u32[]{:S(2)}, u32[]{:S(2)}) collective-permute-start(bf16[2,224,128]{2,1,0:T(8,128)(2,1)S(1)} %constant_dynamic-update-slice_fusion), channel_id=1, source_target_pairs={{0,8},{1,9},{2,10},{3,11},{4,12},{5,13},{6,14},{7,15},{8,0},{9,1},... | collective-permute-start | bytes 344072 | tf_op jit(solution)/shard_map/ppermute | solution.py:103
  12.0 4.9 %collective-permute-start.3 = (bf16[2,224,128]{2,1,0:T(8,128)(2,1)S(1)}, bf16[2,224,128]{2,1,0:T(8,128)(2,1)S(1)}, u32[]{:S(2)}, u32[]{:S(2)}) collective-permute-start(bf16[2,224,128]{2,1,0:T(8,128)(2,1)S(1)} %constant_dynamic-update-slice_fusion.2), channel_id=1, source_target_pairs={{0,1},{1,0},{2,18},{3,19},{4,5},{5,4},{6,22},{7,23},{8,9},{9,8},{1... | collective-permute-start | bytes 344072 | tf_op jit(solution)/shard_map/ppermute | solution.py:103
  14.7 6.1 %collective-permute-start.4 = (bf16[4,224,128]{2,1,0:T(8,128)(2,1)S(1)}, bf16[4,224,128]{2,1,0:T(8,128)(2,1)S(1)}, u32[]{:S(2)}, u32[]{:S(2)}) collective-permute-start(bf16[4,224,128]{2,1,0:T(8,128)(2,1)S(1)} %constant_dynamic-update-slice_fusion.4), channel_id=1, source_target_pairs={{0,4},{1,5},{2,18},{3,19},{4,0},{5,1},{6,22},{7,23},{8,12},{9,13},... | collective-permute-start | bytes 688136 | tf_op jit(solution)/shard_map/ppermute | solution.py:103
  16.9 6.3 %collective-permute-start.5 = (bf16[4,224,128]{2,1,0:T(8,128)(2,1)S(1)}, bf16[4,224,128]{2,1,0:T(8,128)(2,1)S(1)}, u32[]{:S(2)}, u32[]{:S(2)}) collective-permute-start(bf16[4,224,128]{2,1,0:T(8,128)(2,1)S(1)} %constant_dynamic-update-slice_fusion.6), channel_id=1, source_target_pairs={{0,4},{1,5},{2,10},{3,11},{4,0},{5,1},{6,14},{7,15},{8,12},{9,13},... | collective-permute-start | bytes 688136 | tf_op jit(solution)/shard_map/ppermute | solution.py:103
  23.3 8.5 %collective-permute-start.6 = (bf16[8,224,128]{2,1,0:T(8,128)(2,1)S(1)}, bf16[8,224,128]{2,1,0:T(8,128)(2,1)S(1)}, u32[]{:S(2)}, u32[]{:S(2)}) collective-permute-start(bf16[8,224,128]{2,1,0:T(8,128)(2,1)S(1)} %constant_dynamic-update-slice_fusion.10.refs_2_), channel_id=1, source_target_pairs={{0,8},{1,9},{2,3},{3,2},{4,12},{5,13},{6,7},{7,6},{8,0},{9,1},{10,... | collective-permute-start | bytes 1376264 | tf_op jit(solution)/shard_map/ppermute | solution.py:103
  25.2 8.5 %collective-permute-start.9 = (bf16[8,224,128]{2,1,0:T(8,128)(2,1)S(1)}, bf16[8,224,128]{2,1,0:T(8,128)(2,1)S(1)}, u32[]{:S(2)}, u32[]{:S(2)}) collective-permute-start(bf16[8,224,128]{2,1,0:T(8,128)(2,1)S(1)} %constant_dynamic-update-slice_fusion.8.refs_6_), channel_id=1, source_target_pairs={{0,1},{1,0},{2,6},{3,7},{4,5},{5,4},{6,2},{7,3},{8,9},{9,8},{10,14... | collective-permute-start | bytes 1376264 | tf_op jit(solution)/shard_map/ppermute | solution.py:103
  26.7 7.0 %collective-permute-start.7 = (bf16[8,224,128]{2,1,0:T(8,128)(2,1)S(1)}, bf16[8,224,128]{2,1,0:T(8,128)(2,1)S(1)}, u32[]{:S(2)}, u32[]{:S(2)}) collective-permute-start(bf16[8,224,128]{2,1,0:T(8,128)(2,1)S(1)} %constant_dynamic-update-slice_fusion.10.refs_2_), channel_id=1, source_target_pairs={{0,2},{1,3},{2,0},{3,1},{4,6},{5,7},{6,4},{7,5},{8,10},{9,11},{10,... | collective-permute-start | bytes 1376264 | tf_op jit(solution)/shard_map/ppermute | solution.py:107
  26.7 7.0 %collective-permute-start.10 = (bf16[8,224,128]{2,1,0:T(8,128)(2,1)S(1)}, bf16[8,224,128]{2,1,0:T(8,128)(2,1)S(1)}, u32[]{:S(2)}, u32[]{:S(2)}) collective-permute-start(bf16[8,224,128]{2,1,0:T(8,128)(2,1)S(1)} %constant_dynamic-update-slice_fusion.8.refs_6_), channel_id=1, source_target_pairs={{0,2},{1,3},{2,0},{3,1},{4,6},{5,7},{6,4},{7,5},{8,10},{9,11},{10,... | collective-permute-start | bytes 1376264 | tf_op jit(solution)/shard_map/ppermute | solution.py:107
  31.8 1.9 %collective-permute-start.8 = (bf16[8,224,128]{2,1,0:T(8,128)(2,1)S(1)}, bf16[8,224,128]{2,1,0:T(8,128)(2,1)S(1)}, u32[]{:S(2)}, u32[]{:S(2)}) collective-permute-start(bf16[8,224,128]{2,1,0:T(8,128)(2,1)S(1)} %collective-permute-done.6.refs_3_), channel_id=1, source_target_pairs={{0,2},{1,3},{2,0},{3,1},{4,6},{5,7},{6,4},{7,5},{8,10},{9,11},{10,... | collective-permute-start | bytes 1376264 | tf_op jit(solution)/shard_map/ppermute | solution.py:107
  33.7 1.8 %collective-permute-start.11 = (bf16[8,224,128]{2,1,0:T(8,128)(2,1)S(1)}, bf16[8,224,128]{2,1,0:T(8,128)(2,1)S(1)}, u32[]{:S(2)}, u32[]{:S(2)}) collective-permute-start(bf16[8,224,128]{2,1,0:T(8,128)(2,1)S(1)} %collective-permute-done.9.refs_7_), channel_id=1, source_target_pairs={{0,2},{1,3},{2,0},{3,1},{4,6},{5,7},{6,4},{7,5},{8,10},{9,11},{10,... | collective-permute-start | bytes 1376264 | tf_op jit(solution)/shard_map/ppermute | solution.py:107
  83.4 2.5 %collective-permute-start.12 = (bf16[16,224,128]{2,1,0:T(8,128)(2,1)S(1)}, bf16[16,224,128]{2,1,0:T(8,128)(2,1)S(1)}, u32[]{:S(2)}, u32[]{:S(2)}) collective-permute-start(bf16[16,224,128]{2,1,0:T(8,128)(2,1)S(1)} %get-tuple-element.35), channel_id=1, source_target_pairs={{0,2},{1,3},{2,0},{3,1},{4,6},{5,7},{6,4},{7,5},{8,10},{9,11},{10,... | collective-permute-start | bytes 2752520 | tf_op jit(solution)/shard_map/ppermute | solution.py:113
  83.5 3.7 %collective-permute-start.13 = (bf16[16,224,128]{2,1,0:T(8,128)(2,1)S(1)}, bf16[16,224,128]{2,1,0:T(8,128)(2,1)S(1)}, u32[]{:S(2)}, u32[]{:S(2)}) collective-permute-start(bf16[16,224,128]{2,1,0:T(8,128)(2,1)S(1)} %get-tuple-element.37), channel_id=1, source_target_pairs={{0,2},{1,3},{2,0},{3,1},{4,6},{5,7},{6,4},{7,5},{8,10},{9,11},{10,... | collective-permute-start | bytes 2752520 | tf_op jit(solution)/shard_map/ppermute | solution.py:113
  86.1 8.5 %collective-permute-start.14 = (bf16[8,224,128]{2,1,0:T(8,128)(2,1)S(1)}, bf16[8,224,128]{2,1,0:T(8,128)(2,1)S(1)}, u32[]{:S(2)}, u32[]{:S(2)}) collective-permute-start(bf16[8,224,128]{2,1,0:T(8,128)(2,1)S(1)} %get-tuple-element.51), channel_id=1, source_target_pairs={{0,8},{1,9},{2,3},{3,2},{4,12},{5,13},{6,7},{7,6},{8,0},{9,1},{10,... | collective-permute-start | bytes 1376264 | tf_op jit(solution)/shard_map/ppermute | solution.py:124
  87.5 11.2 %collective-permute-start.15 = (bf16[8,224,128]{2,1,0:T(8,128)(2,1)S(1)}, bf16[8,224,128]{2,1,0:T(8,128)(2,1)S(1)}, u32[]{:S(2)}, u32[]{:S(2)}) collective-permute-start(bf16[8,224,128]{2,1,0:T(8,128)(2,1)S(1)} %get-tuple-element.48), channel_id=1, source_target_pairs={{0,1},{1,0},{2,6},{3,7},{4,5},{5,4},{6,2},{7,3},{8,9},{9,8},{10,14... | collective-permute-start | bytes 1376264 | tf_op jit(solution)/shard_map/ppermute | solution.py:124
  94.7 6.1 %collective-permute-start.16 = (bf16[4,224,128]{2,1,0:T(8,128)(2,1)S(1)}, bf16[4,224,128]{2,1,0:T(8,128)(2,1)S(1)}, u32[]{:S(2)}, u32[]{:S(2)}) collective-permute-start(bf16[4,224,128]{2,1,0:T(8,128)(2,1)S(1)} %get-tuple-element.55), channel_id=1, source_target_pairs={{0,4},{1,5},{2,10},{3,11},{4,0},{5,1},{6,14},{7,15},{8,12},{9,13},... | collective-permute-start | bytes 688136 | tf_op jit(solution)/shard_map/ppermute | solution.py:124
  98.8 6.1 %collective-permute-start.17 = (bf16[4,224,128]{2,1,0:T(8,128)(2,1)S(1)}, bf16[4,224,128]{2,1,0:T(8,128)(2,1)S(1)}, u32[]{:S(2)}, u32[]{:S(2)}) collective-permute-start(bf16[4,224,128]{2,1,0:T(8,128)(2,1)S(1)} %get-tuple-element.52), channel_id=1, source_target_pairs={{0,4},{1,5},{2,18},{3,19},{4,0},{5,1},{6,22},{7,23},{8,12},{9,13},... | collective-permute-start | bytes 688136 | tf_op jit(solution)/shard_map/ppermute | solution.py:124
  100.9 15.3 %copy-start.1 = (f32[55416]{0:T(1024)S(1)}, f32[55416]{0:T(1024)}, u32[]{:S(2)}) copy-start(f32[55416]{0:T(1024)} %param.11) | copy-start | bytes 664996
  100.9 15.2 %copy-start.2 = (f32[55416]{0:T(1024)S(1)}, f32[55416]{0:T(1024)}, u32[]{:S(2)}) copy-start(f32[55416]{0:T(1024)} %param.13) | copy-start | bytes 664996
  100.9 15.2 %copy-start.3 = (f32[55416]{0:T(1024)S(1)}, f32[55416]{0:T(1024)}, u32[]{:S(2)}) copy-start(f32[55416]{0:T(1024)} %param.12) | copy-start | bytes 664996
  100.9 5.3 %collective-permute-start.18 = (bf16[2,224,128]{2,1,0:T(8,128)(2,1)S(1)}, bf16[2,224,128]{2,1,0:T(8,128)(2,1)S(1)}, u32[]{:S(2)}, u32[]{:S(2)}) collective-permute-start(bf16[2,224,128]{2,1,0:T(8,128)(2,1)S(1)} %get-tuple-element.59), channel_id=1, source_target_pairs={{0,1},{1,0},{2,18},{3,19},{4,5},{5,4},{6,22},{7,23},{8,9},{9,8},{1... | collective-permute-start | bytes 344072 | tf_op jit(solution)/shard_map/ppermute | solution.py:124
  104.9 5.1 %collective-permute-start.20 = (bf16[2,224,128]{2,1,0:T(8,128)(2,1)S(1)}, bf16[2,224,128]{2,1,0:T(8,128)(2,1)S(1)}, u32[]{:S(2)}, u32[]{:S(2)}) collective-permute-start(bf16[2,224,128]{2,1,0:T(8,128)(2,1)S(1)} %get-tuple-element.56), channel_id=1, source_target_pairs={{0,8},{1,9},{2,10},{3,11},{4,12},{5,13},{6,14},{7,15},{8,0},{9,1},... | collective-permute-start | bytes 344072 | tf_op jit(solution)/shard_map/ppermute | solution.py:124
  106.2 7.7 %collective-permute-start.19 = (bf16[1,224,128]{2,1,0:T(8,128)(2,1)S(1)}, bf16[1,224,128]{2,1,0:T(8,128)(2,1)S(1)}, u32[]{:S(2)}, u32[]{:S(2)}) collective-permute-start(bf16[1,224,128]{2,1,0:T(8,128)(2,1)S(1)} %add_convert_fusion.7), channel_id=1, source_target_pairs={{0,16},{1,17},{2,6},{3,7},{4,20},{5,21},{6,2},{7,3},{8,24},{9,25},... | collective-permute-start | bytes 172040 | tf_op jit(solution)/shard_map/ppermute | solution.py:124
  110.1 6.0 %collective-permute-start.21 = (bf16[1,224,128]{2,1,0:T(8,128)(2,1)S(1)}, bf16[1,224,128]{2,1,0:T(8,128)(2,1)S(1)}, u32[]{:S(2)}, u32[]{:S(2)}) collective-permute-start(bf16[1,224,128]{2,1,0:T(8,128)(2,1)S(1)} %add_convert_fusion.6), channel_id=1, source_target_pairs={{0,16},{1,17},{2,3},{3,2},{4,20},{5,21},{6,7},{7,6},{8,24},{9,25},... | collective-permute-start | bytes 172040 | tf_op jit(solution)/shard_map/ppermute | solution.py:124
